TPU v7x, 512 devices: a whole 4x8x8 slice. The times are simulated.
512 devices in a mesh: segment: 4 (over z_lo), row: 16 (over y, z_hi), col: 8 (over x, core).
Axes of the slice: x: 4, y: 8, z: 8 (z_hi: 2, z_lo: 4; z = z_hi * 4 + z_lo), core: 2. Of those that a mesh axis runs over, the one named last changes fastest.
Arguments:
- frames: bfloat16 [2, 256, 128, 128], P(None, 'row', 'col'), may hold values from -6 to 6
- caches: bfloat16 [4, 2, 2, 256, 128, 128], P('segment', None, None, 'row', 'col'), may hold values from -5 to 5
- weights: bfloat16 [4, 2, 3, 3, 3, 128, 128], P('segment'), may hold values from -0.109375 to 0.109375
- biases: float32 [4, 2, 128], P('segment'), may hold values from -0.5 to 0.5
- gains: float32 [4, 2, 128], P('segment'), may hold values from 0.1 to 1.9
Outputs:
- sections: bfloat16 [4, 2, 256, 128, 128], P('segment', None, 'row', 'col')
All inputs are finite; a program needn't handle non-finite values.
Results may differ from a plain program's by a relative error of at most 0.0055.
Values may be sent and summed in bfloat16 or wider, within the bound.
No kernel may reach another device: no remote copies, remote signals or barrier semaphores. Data moves between devices by JAX's collectives and lax.ppermute only.
A program may use at most 64 MiB of HBM per device.

v0:
```python
import jax
import jax.numpy as jnp
from jax import lax
from jax.sharding import PartitionSpec as P

BLOCK_FRAMES = 2


def with_halo(block, sides, width):
    for axis, dim in sides:
        count = lax.axis_size(axis)
        forward = [(i, i + 1) for i in range(count - 1)]
        backward = [(target, source) for source, target in forward]
        low = lax.ppermute(
            lax.slice_in_dim(block, block.shape[dim] - width, None, axis=dim), axis, forward
        )
        high = lax.ppermute(lax.slice_in_dim(block, 0, width, axis=dim), axis, backward)
        block = jnp.concatenate([low, block, high], axis=dim)
    return block


def shifted(value, axis, steps):
    count = lax.axis_size(axis)
    initial, last = (max(0, -steps), min(count, count - steps))
    return lax.ppermute(value, axis, [(source, source + steps) for source in range(initial, last)])


def norm_act(values, gain_row):
    values = values.astype(jnp.float32)
    scaled = (
        values * lax.rsqrt(jnp.mean(values * values, axis=-1, keepdims=True) + 1e-06) * gain_row
    )
    return jax.nn.silu(scaled).astype(jnp.bfloat16)


def convolve(padded, kernel, bias_row, piece_frames):
    tile_rows = padded.shape[1] - 2
    tile_cols = padded.shape[2] - 2
    channels = kernel.shape[-2]
    slabs = []
    for tap_t in range(3):
        for tap_h in range(3):
            for tap_w in range(3):
                slabs.append(
                    padded[
                        tap_t : tap_t + piece_frames,
                        tap_h : tap_h + tile_rows,
                        tap_w : tap_w + tile_cols,
                    ]
                )
    patches = jnp.concatenate(slabs, axis=-1)
    flat_patches = patches.reshape((piece_frames * tile_rows * tile_cols, 27 * channels))
    flat_kernel = kernel.reshape((27 * channels, kernel.shape[-1]))
    accum = jnp.dot(flat_patches, flat_kernel, preferred_element_type=jnp.float32)
    accum = accum.reshape((piece_frames, tile_rows, tile_cols, kernel.shape[-1]))
    return accum + bias_row


def window(held, fresh):
    joined = jnp.concatenate([held, fresh], axis=0)
    padded = with_halo(joined, (("row", 1), ("col", 2)), 1)
    return (padded, joined[-2:])


def on_device(frames, caches, weights, biases, gains):
    segment_index = lax.axis_index("segment")
    segment_count = lax.axis_size("segment")
    kernels = weights[0]
    offsets = biases[0]
    gain_rows = gains[0]
    piece_frames = BLOCK_FRAMES
    total_frames = frames.shape[0]
    pieces = total_frames // piece_frames
    cached = caches[0]
    held_one = cached[0]
    held_two = cached[1]
    tile_rows = frames.shape[1]
    tile_cols = frames.shape[2]
    channels = frames.shape[3]
    received = jnp.zeros((piece_frames, tile_rows, tile_cols, channels), jnp.bfloat16)
    results = jnp.zeros((total_frames, tile_rows, tile_cols, channels), jnp.bfloat16)
    empty = jnp.zeros((piece_frames, tile_rows, tile_cols, channels), jnp.float32)
    last_step = pieces + segment_count - 2
    for step_index in range(pieces + segment_count - 1):
        piece_index = step_index - segment_index
        active = (piece_index >= 0) & (piece_index < pieces)
        inputs = jnp.where(segment_index == 0, frames, received)
        normed_one = norm_act(inputs, gain_rows[0])
        window_one, next_one = window(held_one, normed_one)
        hidden = lax.cond(
            active,
            lambda window_arg: convolve(window_arg, kernels[0], offsets[0], piece_frames),
            lambda window_arg: empty,
            window_one,
        )
        normed_two = norm_act(hidden, gain_rows[1])
        window_two, next_two = window(held_two, normed_two)
        branch = lax.cond(
            active,
            lambda window_arg: convolve(window_arg, kernels[1], offsets[1], piece_frames),
            lambda window_arg: empty,
            window_two,
        )
        section_out = (inputs.astype(jnp.float32) + branch).astype(jnp.bfloat16)
        held_one = jnp.where(active, next_one, held_one)
        held_two = jnp.where(active, next_two, held_two)
        results = jnp.where(active, section_out, results)
        if step_index < last_step:
            received = shifted(section_out, "segment", 1)
    return results[None]


def solution(mesh):
    in_specs = (
        P(None, "row", "col", None),
        P("segment", None, None, "row", "col", None),
        P("segment", None, None, None, None, None, None),
        P("segment", None, None),
        P("segment", None, None),
    )
    out_specs = P("segment", None, "row", "col", None)
    return jax.shard_map(
        on_device, mesh=mesh, in_specs=in_specs, out_specs=out_specs, check_vma=False
    )
```

profile of v0, /device:TPU:210, one launch (start us, length us, event | category | flops | bytes accessed | tf_op | source)
XLA Modules:
  0.0 235.2 jit_solution(1783209120905657757)
XLA Ops:
  3.1 8.2 %collective-permute-start = (bf16[4,1,16,128]{3,2,1,0:T(8,128)(2,1)S(1)}, bf16[4,1,16,128]{3,2,1,0:T(8,128)(2,1)S(1)}, u32[]{:S(2)}, u32[]{:S(2)}) collective-permute-start(bf16[4,1,16,128]{3,2,1,0:T(8,128)(2,1)S(1)} %get-tuple-element.263), channel_id=1, source_target_pairs={{0,8},{8,16},{16,24},{24,32},{32,40},{40,48},{48,56},{56,64},{64,7... | collective-permute-start | bytes 49160 | tf_op jit(solution)/shard_map/ppermute | solution.py:14
  11.3 2.4 %collective-permute-start.1 = (bf16[4,1,16,128]{3,2,1,0:T(8,128)(2,1)S(1)}, bf16[4,1,16,128]{3,2,1,0:T(8,128)(2,1)S(1)}, u32[]{:S(2)}, u32[]{:S(2)}) collective-permute-start(bf16[4,1,16,128]{3,2,1,0:T(8,128)(2,1)S(1)} %get-tuple-element.264), channel_id=1, source_target_pairs={{8,0},{16,8},{24,16},{32,24},{40,32},{48,40},{56,48},{64,56},{72,6... | collective-permute-start | bytes 49160 | tf_op jit(solution)/shard_map/ppermute | solution.py:17
  13.8 7.1 %collective-permute-done.1 = bf16[4,1,16,128]{3,2,1,0:T(8,128)(2,1)S(1)} collective-permute-done((bf16[4,1,16,128]{3,2,1,0:T(8,128)(2,1)S(1)}, bf16[4,1,16,128]{3,2,1,0:T(8,128)(2,1)S(1)}, u32[]{:S(2)}, u32[]{:S(2)}) %collective-permute-start.1) | collective-permute-done | bytes 16416 | tf_op jit(solution)/shard_map/ppermute | solution.py:17
  21.0 1.9 collective-permute-start.2
  22.9 3.6 %collective-permute-start.3 = (bf16[4,18,1,128]{3,2,1,0:T(2,128)(2,1)S(1)}, bf16[4,18,1,128]{3,2,1,0:T(2,128)(2,1)S(1)}, u32[]{:S(2)}, u32[]{:S(2)}) collective-permute-start(bf16[4,18,1,128]{3,2,1,0:T(2,128)(2,1)S(1)} %get-tuple-element.248), channel_id=1, source_target_pairs={{1,0},{2,1},{3,2},{4,3},{5,4},{6,5},{7,6},{9,8},{10,9},{11,10},{12... | collective-permute-start | bytes 55304 | tf_op jit(solution)/shard_map/ppermute | solution.py:17
  29.6 3.4 %collective-permute-start.4 = (bf16[4,1,16,128]{3,2,1,0:T(8,128)(2,1)S(1)}, bf16[4,1,16,128]{3,2,1,0:T(8,128)(2,1)S(1)}, u32[]{:S(2)}, u32[]{:S(2)}) collective-permute-start(bf16[4,1,16,128]{3,2,1,0:T(8,128)(2,1)S(1)} %get-tuple-element.261), channel_id=1, source_target_pairs={{0,8},{8,16},{16,24},{24,32},{32,40},{40,48},{48,56},{56,64},{64,7... | collective-permute-start | bytes 49160 | tf_op jit(solution)/shard_map/ppermute | solution.py:14
  33.0 7.2 %collective-permute-start.5 = (bf16[4,1,16,128]{3,2,1,0:T(8,128)(2,1)S(1)}, bf16[4,1,16,128]{3,2,1,0:T(8,128)(2,1)S(1)}, u32[]{:S(2)}, u32[]{:S(2)}) collective-permute-start(bf16[4,1,16,128]{3,2,1,0:T(8,128)(2,1)S(1)} %get-tuple-element.262), channel_id=1, source_target_pairs={{8,0},{16,8},{24,16},{32,24},{40,32},{48,40},{56,48},{64,56},{72,6... | collective-permute-start | bytes 49160 | tf_op jit(solution)/shard_map/ppermute | solution.py:17
  40.3 2.3 collective-permute-done.5
  42.7 2.1 collective-permute-start.6
  44.8 3.5 %collective-permute-start.7 = (bf16[4,18,1,128]{3,2,1,0:T(2,128)(2,1)S(1)}, bf16[4,18,1,128]{3,2,1,0:T(2,128)(2,1)S(1)}, u32[]{:S(2)}, u32[]{:S(2)}) collective-permute-start(bf16[4,18,1,128]{3,2,1,0:T(2,128)(2,1)S(1)} %get-tuple-element.246), channel_id=1, source_target_pairs={{1,0},{2,1},{3,2},{4,3},{5,4},{6,5},{7,6},{9,8},{10,9},{11,10},{12... | collective-permute-start | bytes 55304 | tf_op jit(solution)/shard_map/ppermute | solution.py:17
  48.3 1.6 collective-permute-done.7
  52.4 6.3 %collective-permute-done.8 = bf16[2,16,16,128]{3,2,1,0:T(8,128)(2,1)S(1)} collective-permute-done((bf16[2,16,16,128]{3,2,1,0:T(8,128)(2,1)S(1)}, bf16[2,16,16,128]{3,2,1,0:T(8,128)(2,1)S(1)}, u32[]{:S(2)}, u32[]{:S(2)}) %collective-permute-start.8) | collective-permute-done | bytes 131104 | tf_op jit(solution)/shard_map/ppermute | solution.py:25
  59.0 8.1 %collective-permute-start.10 = (bf16[4,1,16,128]{3,2,1,0:T(8,128)(2,1)S(1)}, bf16[4,1,16,128]{3,2,1,0:T(8,128)(2,1)S(1)}, u32[]{:S(2)}, u32[]{:S(2)}) collective-permute-start(bf16[4,1,16,128]{3,2,1,0:T(8,128)(2,1)S(1)} %get-tuple-element.260), channel_id=1, source_target_pairs={{8,0},{16,8},{24,16},{32,24},{40,32},{48,40},{56,48},{64,56},{72,6... | collective-permute-start | bytes 49160 | tf_op jit(solution)/shard_map/ppermute | solution.py:17
  67.1 2.1 collective-permute-start.9
  69.2 8.4 %collective-permute-done.9 = bf16[4,1,16,128]{3,2,1,0:T(8,128)(2,1)S(1)} collective-permute-done((bf16[4,1,16,128]{3,2,1,0:T(8,128)(2,1)S(1)}, bf16[4,1,16,128]{3,2,1,0:T(8,128)(2,1)S(1)}, u32[]{:S(2)}, u32[]{:S(2)}) %collective-permute-start.9) | collective-permute-done | bytes 16416 | tf_op jit(solution)/shard_map/ppermute | solution.py:14
  77.7 1.9 collective-permute-start.11
  79.7 3.6 %collective-permute-start.12 = (bf16[4,18,1,128]{3,2,1,0:T(2,128)(2,1)S(1)}, bf16[4,18,1,128]{3,2,1,0:T(2,128)(2,1)S(1)}, u32[]{:S(2)}, u32[]{:S(2)}) collective-permute-start(bf16[4,18,1,128]{3,2,1,0:T(2,128)(2,1)S(1)} %get-tuple-element.244), channel_id=1, source_target_pairs={{1,0},{2,1},{3,2},{4,3},{5,4},{6,5},{7,6},{9,8},{10,9},{11,10},{12... | collective-permute-start | bytes 55304 | tf_op jit(solution)/shard_map/ppermute | solution.py:17
  85.4 1.9 collective-permute-start.13
  87.4 8.7 %collective-permute-start.14 = (bf16[4,1,16,128]{3,2,1,0:T(8,128)(2,1)S(1)}, bf16[4,1,16,128]{3,2,1,0:T(8,128)(2,1)S(1)}, u32[]{:S(2)}, u32[]{:S(2)}) collective-permute-start(bf16[4,1,16,128]{3,2,1,0:T(8,128)(2,1)S(1)} %get-tuple-element.258), channel_id=1, source_target_pairs={{8,0},{16,8},{24,16},{32,24},{40,32},{48,40},{56,48},{64,56},{72,6... | collective-permute-start | bytes 49160 | tf_op jit(solution)/shard_map/ppermute | solution.py:17
  96.1 1.8 collective-permute-done.14
  98.0 2.9 %collective-permute-start.15 = (bf16[4,18,1,128]{3,2,1,0:T(2,128)(2,1)S(1)}, bf16[4,18,1,128]{3,2,1,0:T(2,128)(2,1)S(1)}, u32[]{:S(2)}, u32[]{:S(2)}) collective-permute-start(bf16[4,18,1,128]{3,2,1,0:T(2,128)(2,1)S(1)} %get-tuple-element.241), channel_id=1, source_target_pairs={{0,1},{1,2},{2,3},{3,4},{4,5},{5,6},{6,7},{8,9},{9,10},{10,11},{11... | collective-permute-start | bytes 55304 | tf_op jit(solution)/shard_map/ppermute | solution.py:14
  101.0 2.6 %collective-permute-start.16 = (bf16[4,18,1,128]{3,2,1,0:T(2,128)(2,1)S(1)}, bf16[4,18,1,128]{3,2,1,0:T(2,128)(2,1)S(1)}, u32[]{:S(2)}, u32[]{:S(2)}) collective-permute-start(bf16[4,18,1,128]{3,2,1,0:T(2,128)(2,1)S(1)} %get-tuple-element.242), channel_id=1, source_target_pairs={{1,0},{2,1},{3,2},{4,3},{5,4},{6,5},{7,6},{9,8},{10,9},{11,10},{12... | collective-permute-start | bytes 55304 | tf_op jit(solution)/shard_map/ppermute | solution.py:17
  107.1 5.6 %collective-permute-done.17 = bf16[2,16,16,128]{3,2,1,0:T(8,128)(2,1)S(1)} collective-permute-done((bf16[2,16,16,128]{3,2,1,0:T(8,128)(2,1)S(1)}, bf16[2,16,16,128]{3,2,1,0:T(8,128)(2,1)S(1)}, u32[]{:S(2)}, u32[]{:S(2)}) %collective-permute-start.17) | collective-permute-done | bytes 131104 | tf_op jit(solution)/shard_map/ppermute | solution.py:25
  113.2 8.9 %collective-permute-start.18 = (bf16[4,1,16,128]{3,2,1,0:T(8,128)(2,1)S(1)}, bf16[4,1,16,128]{3,2,1,0:T(8,128)(2,1)S(1)}, u32[]{:S(2)}, u32[]{:S(2)}) collective-permute-start(bf16[4,1,16,128]{3,2,1,0:T(8,128)(2,1)S(1)} %get-tuple-element.255), channel_id=1, source_target_pairs={{0,8},{8,16},{16,24},{24,32},{32,40},{40,48},{48,56},{56,64},{64,7... | collective-permute-start | bytes 49160 | tf_op jit(solution)/shard_map/ppermute | solution.py:14
  122.0 1.9 collective-permute-start.19
  124.0 7.6 %collective-permute-done.19 = bf16[4,1,16,128]{3,2,1,0:T(8,128)(2,1)S(1)} collective-permute-done((bf16[4,1,16,128]{3,2,1,0:T(8,128)(2,1)S(1)}, bf16[4,1,16,128]{3,2,1,0:T(8,128)(2,1)S(1)}, u32[]{:S(2)}, u32[]{:S(2)}) %collective-permute-start.19) | collective-permute-done | bytes 16416 | tf_op jit(solution)/shard_map/ppermute | solution.py:17
  131.7 1.9 collective-permute-start.20
  133.6 3.6 %collective-permute-start.21 = (bf16[4,18,1,128]{3,2,1,0:T(2,128)(2,1)S(1)}, bf16[4,18,1,128]{3,2,1,0:T(2,128)(2,1)S(1)}, u32[]{:S(2)}, u32[]{:S(2)}) collective-permute-start(bf16[4,18,1,128]{3,2,1,0:T(2,128)(2,1)S(1)} %get-tuple-element.240), channel_id=1, source_target_pairs={{1,0},{2,1},{3,2},{4,3},{5,4},{6,5},{7,6},{9,8},{10,9},{11,10},{12... | collective-permute-start | bytes 55304 | tf_op jit(solution)/shard_map/ppermute | solution.py:17
  137.3 1.6 collective-permute-done.21
  139.5 9.4 %collective-permute-start.22 = (bf16[4,1,16,128]{3,2,1,0:T(8,128)(2,1)S(1)}, bf16[4,1,16,128]{3,2,1,0:T(8,128)(2,1)S(1)}, u32[]{:S(2)}, u32[]{:S(2)}) collective-permute-start(bf16[4,1,16,128]{3,2,1,0:T(8,128)(2,1)S(1)} %get-tuple-element.253), channel_id=1, source_target_pairs={{0,8},{8,16},{16,24},{24,32},{32,40},{40,48},{48,56},{56,64},{64,7... | collective-permute-start | bytes 49160 | tf_op jit(solution)/shard_map/ppermute | solution.py:14
  148.9 1.9 collective-permute-start.23
  150.8 7.6 %collective-permute-done.23 = bf16[4,1,16,128]{3,2,1,0:T(8,128)(2,1)S(1)} collective-permute-done((bf16[4,1,16,128]{3,2,1,0:T(8,128)(2,1)S(1)}, bf16[4,1,16,128]{3,2,1,0:T(8,128)(2,1)S(1)}, u32[]{:S(2)}, u32[]{:S(2)}) %collective-permute-start.23) | collective-permute-done | bytes 16416 | tf_op jit(solution)/shard_map/ppermute | solution.py:17
  158.5 2.8 %collective-permute-start.24 = (bf16[4,18,1,128]{3,2,1,0:T(2,128)(2,1)S(1)}, bf16[4,18,1,128]{3,2,1,0:T(2,128)(2,1)S(1)}, u32[]{:S(2)}, u32[]{:S(2)}) collective-permute-start(bf16[4,18,1,128]{3,2,1,0:T(2,128)(2,1)S(1)} %get-tuple-element.237), channel_id=1, source_target_pairs={{0,1},{1,2},{2,3},{3,4},{4,5},{5,6},{6,7},{8,9},{9,10},{10,11},{11... | collective-permute-start | bytes 55304 | tf_op jit(solution)/shard_map/ppermute | solution.py:14
  161.3 2.8 %collective-permute-start.25 = (bf16[4,18,1,128]{3,2,1,0:T(2,128)(2,1)S(1)}, bf16[4,18,1,128]{3,2,1,0:T(2,128)(2,1)S(1)}, u32[]{:S(2)}, u32[]{:S(2)}) collective-permute-start(bf16[4,18,1,128]{3,2,1,0:T(2,128)(2,1)S(1)} %get-tuple-element.238), channel_id=1, source_target_pairs={{1,0},{2,1},{3,2},{4,3},{5,4},{6,5},{7,6},{9,8},{10,9},{11,10},{12... | collective-permute-start | bytes 55304 | tf_op jit(solution)/shard_map/ppermute | solution.py:17
  168.2 13.7 %collective-permute-done.26 = bf16[2,16,16,128]{3,2,1,0:T(8,128)(2,1)S(1)} collective-permute-done((bf16[2,16,16,128]{3,2,1,0:T(8,128)(2,1)S(1)}, bf16[2,16,16,128]{3,2,1,0:T(8,128)(2,1)S(1)}, u32[]{:S(2)}, u32[]{:S(2)}) %collective-permute-start.26) | collective-permute-done | bytes 131104 | tf_op jit(solution)/shard_map/ppermute | solution.py:25
  182.2 8.7 %collective-permute-start.27 = (bf16[4,1,16,128]{3,2,1,0:T(8,128)(2,1)S(1)}, bf16[4,1,16,128]{3,2,1,0:T(8,128)(2,1)S(1)}, u32[]{:S(2)}, u32[]{:S(2)}) collective-permute-start(bf16[4,1,16,128]{3,2,1,0:T(8,128)(2,1)S(1)} %get-tuple-element.251), channel_id=1, source_target_pairs={{0,8},{8,16},{16,24},{24,32},{32,40},{40,48},{48,56},{56,64},{64,7... | collective-permute-start | bytes 49160 | tf_op jit(solution)/shard_map/ppermute | solution.py:14
  190.9 1.9 collective-permute-start.28
  192.9 7.6 %collective-permute-done.28 = bf16[4,1,16,128]{3,2,1,0:T(8,128)(2,1)S(1)} collective-permute-done((bf16[4,1,16,128]{3,2,1,0:T(8,128)(2,1)S(1)}, bf16[4,1,16,128]{3,2,1,0:T(8,128)(2,1)S(1)}, u32[]{:S(2)}, u32[]{:S(2)}) %collective-permute-start.28) | collective-permute-done | bytes 16416 | tf_op jit(solution)/shard_map/ppermute | solution.py:17
  200.6 2.5 %collective-permute-start.29 = (bf16[4,18,1,128]{3,2,1,0:T(2,128)(2,1)S(1)}, bf16[4,18,1,128]{3,2,1,0:T(2,128)(2,1)S(1)}, u32[]{:S(2)}, u32[]{:S(2)}) collective-permute-start(bf16[4,18,1,128]{3,2,1,0:T(2,128)(2,1)S(1)} %get-tuple-element.235), channel_id=1, source_target_pairs={{0,1},{1,2},{2,3},{3,4},{4,5},{5,6},{6,7},{8,9},{9,10},{10,11},{11... | collective-permute-start | bytes 55304 | tf_op jit(solution)/shard_map/ppermute | solution.py:14
  203.1 3.1 %collective-permute-start.30 = (bf16[4,18,1,128]{3,2,1,0:T(2,128)(2,1)S(1)}, bf16[4,18,1,128]{3,2,1,0:T(2,128)(2,1)S(1)}, u32[]{:S(2)}, u32[]{:S(2)}) collective-permute-start(bf16[4,18,1,128]{3,2,1,0:T(2,128)(2,1)S(1)} %get-tuple-element.236), channel_id=1, source_target_pairs={{1,0},{2,1},{3,2},{4,3},{5,4},{6,5},{7,6},{9,8},{10,9},{11,10},{12... | collective-permute-start | bytes 55304 | tf_op jit(solution)/shard_map/ppermute | solution.py:17
  206.2 1.9 collective-permute-done.30
  208.4 2.6 %conditional.14 = (f32[2,16,16,128]{3,2,1,0:T(8,128)S(1)}, f32[2,16,16,1]{2,1,0,3:T(8,128)S(1)}) conditional(s32[]{:T(128)} %convert_element_type.84, () %tuple.82, (bf16[4,18,18,128]{3,2,1,0:T(8,128)(2,1)S(1)}, bf16[4,18,16,128]{3,2,1,0:T(8,128)(2,1)S(1)}, bf16[4,16,16,128]{3,2,1,0:T(8,128)(2,1)S(1)}, bf16[2,16,16,128]{3,2,1,0:T(8,128)(2,1)S(1)}, ...), branch_computations={%region_19.20_spmd, %region_20.22_spmd} | conditional | flops 453180928 | bytes 13536784 | solution.py:90
  211.2 3.7 %collective-permute-start.31 = (bf16[4,1,16,128]{3,2,1,0:T(8,128)(2,1)S(1)}, bf16[4,1,16,128]{3,2,1,0:T(8,128)(2,1)S(1)}, u32[]{:S(2)}, u32[]{:S(2)}) collective-permute-start(bf16[4,1,16,128]{3,2,1,0:T(8,128)(2,1)S(1)} %get-tuple-element.249), channel_id=1, source_target_pairs={{0,8},{8,16},{16,24},{24,32},{32,40},{40,48},{48,56},{56,64},{64,7... | collective-permute-start | bytes 49160 | tf_op jit(solution)/shard_map/ppermute | solution.py:14
  214.9 7.0 %collective-permute-start.32 = (bf16[4,1,16,128]{3,2,1,0:T(8,128)(2,1)S(1)}, bf16[4,1,16,128]{3,2,1,0:T(8,128)(2,1)S(1)}, u32[]{:S(2)}, u32[]{:S(2)}) collective-permute-start(bf16[4,1,16,128]{3,2,1,0:T(8,128)(2,1)S(1)} %get-tuple-element.250), channel_id=1, source_target_pairs={{8,0},{16,8},{24,16},{32,24},{40,32},{48,40},{56,48},{64,56},{72,6... | collective-permute-start | bytes 49160 | tf_op jit(solution)/shard_map/ppermute | solution.py:17
  221.9 2.6 %collective-permute-done.32 = bf16[4,1,16,128]{3,2,1,0:T(8,128)(2,1)S(1)} collective-permute-done((bf16[4,1,16,128]{3,2,1,0:T(8,128)(2,1)S(1)}, bf16[4,1,16,128]{3,2,1,0:T(8,128)(2,1)S(1)}, u32[]{:S(2)}, u32[]{:S(2)}) %collective-permute-start.32) | collective-permute-done | bytes 16416 | tf_op jit(solution)/shard_map/ppermute | solution.py:17
  224.5 3.1 %collective-permute-start.33 = (bf16[4,18,1,128]{3,2,1,0:T(2,128)(2,1)S(1)}, bf16[4,18,1,128]{3,2,1,0:T(2,128)(2,1)S(1)}, u32[]{:S(2)}, u32[]{:S(2)}) collective-permute-start(bf16[4,18,1,128]{3,2,1,0:T(2,128)(2,1)S(1)} %get-tuple-element.233), channel_id=1, source_target_pairs={{0,1},{1,2},{2,3},{3,4},{4,5},{5,6},{6,7},{8,9},{9,10},{10,11},{11... | collective-permute-start | bytes 55304 | tf_op jit(solution)/shard_map/ppermute | solution.py:14
  227.7 2.4 %collective-permute-start.34 = (bf16[4,18,1,128]{3,2,1,0:T(2,128)(2,1)S(1)}, bf16[4,18,1,128]{3,2,1,0:T(2,128)(2,1)S(1)}, u32[]{:S(2)}, u32[]{:S(2)}) collective-permute-start(bf16[4,18,1,128]{3,2,1,0:T(2,128)(2,1)S(1)} %get-tuple-element.234), channel_id=1, source_target_pairs={{1,0},{2,1},{3,2},{4,3},{5,4},{6,5},{7,6},{9,8},{10,9},{11,10},{12... | collective-permute-start | bytes 55304 | tf_op jit(solution)/shard_map/ppermute | solution.py:17
  232.0 2.5 %conditional.15 = (f32[2,16,16,128]{3,2,1,0:T(8,128)S(1)}) conditional(s32[]{:T(128)} %convert_element_type.84, () %tuple.81, (bf16[4,18,18,128]{3,2,1,0:T(8,128)(2,1)S(1)}, bf16[4,18,16,128]{3,2,1,0:T(8,128)(2,1)S(1)}, bf16[4,16,16,128]{3,2,1,0:T(8,128)(2,1)S(1)}, bf16[2,16,16,128]{3,2,1,0:T(8,128)(2,1)S(1)}, ...), branch_computations={%region_22.23_spmd, %region_23.24_spmd} | conditional | flops 453050368 | bytes 13534728 | solution.py:98
  (177 shorter events, 28.4 us)
Async XLA Ops:
  0.0 28.4 %copy-start = (bf16[1,2,3,3,3,128,128]{6,5,4,3,2,1,0:T(8,128)(2,1)S(1)}, bf16[1,2,3,3,3,128,128]{6,5,4,3,2,1,0:T(8,128)(2,1)}, u32[]{:S(2)}) copy-start(bf16[1,2,3,3,3,128,128]{6,5,4,3,2,1,0:T(8,128)(2,1)} %param.23) | copy-start | bytes 5308420
  0.0 28.4 %copy-start.5 = (f32[1,2,128]{2,1,0:T(2,128)S(1)}, f32[1,2,128]{2,1,0:T(2,128)}, u32[]{:S(2)}) copy-start(f32[1,2,128]{2,1,0:T(2,128)} %param.24) | copy-start | bytes 3076
  3.1 10.7 %collective-permute-start = (bf16[4,1,16,128]{3,2,1,0:T(8,128)(2,1)S(1)}, bf16[4,1,16,128]{3,2,1,0:T(8,128)(2,1)S(1)}, u32[]{:S(2)}, u32[]{:S(2)}) collective-permute-start(bf16[4,1,16,128]{3,2,1,0:T(8,128)(2,1)S(1)} %get-tuple-element.263), channel_id=1, source_target_pairs={{0,8},{8,16},{16,24},{24,32},{32,40},{40,48},{48,56},{56,64},{64,7... | collective-permute-start | bytes 49160 | tf_op jit(solution)/shard_map/ppermute | solution.py:14
  11.3 9.5 %collective-permute-start.1 = (bf16[4,1,16,128]{3,2,1,0:T(8,128)(2,1)S(1)}, bf16[4,1,16,128]{3,2,1,0:T(8,128)(2,1)S(1)}, u32[]{:S(2)}, u32[]{:S(2)}) collective-permute-start(bf16[4,1,16,128]{3,2,1,0:T(8,128)(2,1)S(1)} %get-tuple-element.264), channel_id=1, source_target_pairs={{8,0},{16,8},{24,16},{32,24},{40,32},{48,40},{56,48},{64,56},{72,6... | collective-permute-start | bytes 49160 | tf_op jit(solution)/shard_map/ppermute | solution.py:17
  21.0 5.6 %collective-permute-start.2 = (bf16[4,18,1,128]{3,2,1,0:T(2,128)(2,1)S(1)}, bf16[4,18,1,128]{3,2,1,0:T(2,128)(2,1)S(1)}, u32[]{:S(2)}, u32[]{:S(2)}) collective-permute-start(bf16[4,18,1,128]{3,2,1,0:T(2,128)(2,1)S(1)} %get-tuple-element.247), channel_id=1, source_target_pairs={{0,1},{1,2},{2,3},{3,4},{4,5},{5,6},{6,7},{8,9},{9,10},{10,11},{11... | collective-permute-start | bytes 55304 | tf_op jit(solution)/shard_map/ppermute | solution.py:14
  22.9 5.3 %collective-permute-start.3 = (bf16[4,18,1,128]{3,2,1,0:T(2,128)(2,1)S(1)}, bf16[4,18,1,128]{3,2,1,0:T(2,128)(2,1)S(1)}, u32[]{:S(2)}, u32[]{:S(2)}) collective-permute-start(bf16[4,18,1,128]{3,2,1,0:T(2,128)(2,1)S(1)} %get-tuple-element.248), channel_id=1, source_target_pairs={{1,0},{2,1},{3,2},{4,3},{5,4},{6,5},{7,6},{9,8},{10,9},{11,10},{12... | collective-permute-start | bytes 55304 | tf_op jit(solution)/shard_map/ppermute | solution.py:17
  28.4 1.0 copy-start.4
  29.6 10.7 %collective-permute-start.4 = (bf16[4,1,16,128]{3,2,1,0:T(8,128)(2,1)S(1)}, bf16[4,1,16,128]{3,2,1,0:T(8,128)(2,1)S(1)}, u32[]{:S(2)}, u32[]{:S(2)}) collective-permute-start(bf16[4,1,16,128]{3,2,1,0:T(8,128)(2,1)S(1)} %get-tuple-element.261), channel_id=1, source_target_pairs={{0,8},{8,16},{16,24},{24,32},{32,40},{40,48},{48,56},{56,64},{64,7... | collective-permute-start | bytes 49160 | tf_op jit(solution)/shard_map/ppermute | solution.py:14
  33.0 9.5 %collective-permute-start.5 = (bf16[4,1,16,128]{3,2,1,0:T(8,128)(2,1)S(1)}, bf16[4,1,16,128]{3,2,1,0:T(8,128)(2,1)S(1)}, u32[]{:S(2)}, u32[]{:S(2)}) collective-permute-start(bf16[4,1,16,128]{3,2,1,0:T(8,128)(2,1)S(1)} %get-tuple-element.262), channel_id=1, source_target_pairs={{8,0},{16,8},{24,16},{32,24},{40,32},{48,40},{56,48},{64,56},{72,6... | collective-permute-start | bytes 49160 | tf_op jit(solution)/shard_map/ppermute | solution.py:17
  42.7 5.6 %collective-permute-start.6 = (bf16[4,18,1,128]{3,2,1,0:T(2,128)(2,1)S(1)}, bf16[4,18,1,128]{3,2,1,0:T(2,128)(2,1)S(1)}, u32[]{:S(2)}, u32[]{:S(2)}) collective-permute-start(bf16[4,18,1,128]{3,2,1,0:T(2,128)(2,1)S(1)} %get-tuple-element.245), channel_id=1, source_target_pairs={{0,1},{1,2},{2,3},{3,4},{4,5},{5,6},{6,7},{8,9},{9,10},{10,11},{11... | collective-permute-start | bytes 55304 | tf_op jit(solution)/shard_map/ppermute | solution.py:14
  44.8 5.1 %collective-permute-start.7 = (bf16[4,18,1,128]{3,2,1,0:T(2,128)(2,1)S(1)}, bf16[4,18,1,128]{3,2,1,0:T(2,128)(2,1)S(1)}, u32[]{:S(2)}, u32[]{:S(2)}) collective-permute-start(bf16[4,18,1,128]{3,2,1,0:T(2,128)(2,1)S(1)} %get-tuple-element.246), channel_id=1, source_target_pairs={{1,0},{2,1},{3,2},{4,3},{5,4},{6,5},{7,6},{9,8},{10,9},{11,10},{12... | collective-permute-start | bytes 55304 | tf_op jit(solution)/shard_map/ppermute | solution.py:17
  50.2 0.9 copy-start.1
  51.1 7.6 %collective-permute-start.8 = (bf16[2,16,16,128]{3,2,1,0:T(8,128)(2,1)S(1)}, bf16[2,16,16,128]{3,2,1,0:T(8,128)(2,1)S(1)}, u32[]{:S(2)}, u32[]{:S(2)}) collective-permute-start(bf16[2,16,16,128]{3,2,1,0:T(8,128)(2,1)S(1)} %fusion.8), channel_id=1, source_target_pairs={{0,128},{128,256},{256,384},{1,129},{129,257},{257,385},{2,130},{1... | collective-permute-start | bytes 393224 | tf_op jit(solution)/shard_map/ppermute | solution.py:25
  59.0 10.2 %collective-permute-start.10 = (bf16[4,1,16,128]{3,2,1,0:T(8,128)(2,1)S(1)}, bf16[4,1,16,128]{3,2,1,0:T(8,128)(2,1)S(1)}, u32[]{:S(2)}, u32[]{:S(2)}) collective-permute-start(bf16[4,1,16,128]{3,2,1,0:T(8,128)(2,1)S(1)} %get-tuple-element.260), channel_id=1, source_target_pairs={{8,0},{16,8},{24,16},{32,24},{40,32},{48,40},{56,48},{64,56},{72,6... | collective-permute-start | bytes 49160 | tf_op jit(solution)/shard_map/ppermute | solution.py:17
  67.1 10.5 %collective-permute-start.9 = (bf16[4,1,16,128]{3,2,1,0:T(8,128)(2,1)S(1)}, bf16[4,1,16,128]{3,2,1,0:T(8,128)(2,1)S(1)}, u32[]{:S(2)}, u32[]{:S(2)}) collective-permute-start(bf16[4,1,16,128]{3,2,1,0:T(8,128)(2,1)S(1)} %get-tuple-element.259), channel_id=1, source_target_pairs={{0,8},{8,16},{16,24},{24,32},{32,40},{40,48},{48,56},{56,64},{64,7... | collective-permute-start | bytes 49160 | tf_op jit(solution)/shard_map/ppermute | solution.py:14
  77.7 5.6 %collective-permute-start.11 = (bf16[4,18,1,128]{3,2,1,0:T(2,128)(2,1)S(1)}, bf16[4,18,1,128]{3,2,1,0:T(2,128)(2,1)S(1)}, u32[]{:S(2)}, u32[]{:S(2)}) collective-permute-start(bf16[4,18,1,128]{3,2,1,0:T(2,128)(2,1)S(1)} %get-tuple-element.243), channel_id=1, source_target_pairs={{0,1},{1,2},{2,3},{3,4},{4,5},{5,6},{6,7},{8,9},{9,10},{10,11},{11... | collective-permute-start | bytes 55304 | tf_op jit(solution)/shard_map/ppermute | solution.py:14
  79.7 5.3 %collective-permute-start.12 = (bf16[4,18,1,128]{3,2,1,0:T(2,128)(2,1)S(1)}, bf16[4,18,1,128]{3,2,1,0:T(2,128)(2,1)S(1)}, u32[]{:S(2)}, u32[]{:S(2)}) collective-permute-start(bf16[4,18,1,128]{3,2,1,0:T(2,128)(2,1)S(1)} %get-tuple-element.244), channel_id=1, source_target_pairs={{1,0},{2,1},{3,2},{4,3},{5,4},{6,5},{7,6},{9,8},{10,9},{11,10},{12... | collective-permute-start | bytes 55304 | tf_op jit(solution)/shard_map/ppermute | solution.py:17
  85.4 10.7 %collective-permute-start.13 = (bf16[4,1,16,128]{3,2,1,0:T(8,128)(2,1)S(1)}, bf16[4,1,16,128]{3,2,1,0:T(8,128)(2,1)S(1)}, u32[]{:S(2)}, u32[]{:S(2)}) collective-permute-start(bf16[4,1,16,128]{3,2,1,0:T(8,128)(2,1)S(1)} %get-tuple-element.257), channel_id=1, source_target_pairs={{0,8},{8,16},{16,24},{24,32},{32,40},{40,48},{48,56},{56,64},{64,7... | collective-permute-start | bytes 49160 | tf_op jit(solution)/shard_map/ppermute | solution.py:14
  87.4 10.6 %collective-permute-start.14 = (bf16[4,1,16,128]{3,2,1,0:T(8,128)(2,1)S(1)}, bf16[4,1,16,128]{3,2,1,0:T(8,128)(2,1)S(1)}, u32[]{:S(2)}, u32[]{:S(2)}) collective-permute-start(bf16[4,1,16,128]{3,2,1,0:T(8,128)(2,1)S(1)} %get-tuple-element.258), channel_id=1, source_target_pairs={{8,0},{16,8},{24,16},{32,24},{40,32},{48,40},{56,48},{64,56},{72,6... | collective-permute-start | bytes 49160 | tf_op jit(solution)/shard_map/ppermute | solution.py:17
  98.0 5.6 %collective-permute-start.15 = (bf16[4,18,1,128]{3,2,1,0:T(2,128)(2,1)S(1)}, bf16[4,18,1,128]{3,2,1,0:T(2,128)(2,1)S(1)}, u32[]{:S(2)}, u32[]{:S(2)}) collective-permute-start(bf16[4,18,1,128]{3,2,1,0:T(2,128)(2,1)S(1)} %get-tuple-element.241), channel_id=1, source_target_pairs={{0,1},{1,2},{2,3},{3,4},{4,5},{5,6},{6,7},{8,9},{9,10},{10,11},{11... | collective-permute-start | bytes 55304 | tf_op jit(solution)/shard_map/ppermute | solution.py:14
  101.0 4.3 %collective-permute-start.16 = (bf16[4,18,1,128]{3,2,1,0:T(2,128)(2,1)S(1)}, bf16[4,18,1,128]{3,2,1,0:T(2,128)(2,1)S(1)}, u32[]{:S(2)}, u32[]{:S(2)}) collective-permute-start(bf16[4,18,1,128]{3,2,1,0:T(2,128)(2,1)S(1)} %get-tuple-element.242), channel_id=1, source_target_pairs={{1,0},{2,1},{3,2},{4,3},{5,4},{6,5},{7,6},{9,8},{10,9},{11,10},{12... | collective-permute-start | bytes 55304 | tf_op jit(solution)/shard_map/ppermute | solution.py:17
  105.8 6.9 %collective-permute-start.17 = (bf16[2,16,16,128]{3,2,1,0:T(8,128)(2,1)S(1)}, bf16[2,16,16,128]{3,2,1,0:T(8,128)(2,1)S(1)}, u32[]{:S(2)}, u32[]{:S(2)}) collective-permute-start(bf16[2,16,16,128]{3,2,1,0:T(8,128)(2,1)S(1)} %fusion.17), channel_id=1, source_target_pairs={{0,128},{128,256},{256,384},{1,129},{129,257},{257,385},{2,130},{1... | collective-permute-start | bytes 393224 | tf_op jit(solution)/shard_map/ppermute | solution.py:25
  112.8 11.1 %copy-start.2 = (bf16[2,16,16,128]{3,2,1,0:T(8,128)(2,1)}, bf16[2,16,16,128]{3,2,1,0:T(8,128)(2,1)S(1)}, u32[]{:S(2)}) copy-start(bf16[2,16,16,128]{3,2,1,0:T(8,128)(2,1)S(1)} %get-tuple-element.218) | copy-start | bytes 393220
  113.2 10.8 %collective-permute-start.18 = (bf16[4,1,16,128]{3,2,1,0:T(8,128)(2,1)S(1)}, bf16[4,1,16,128]{3,2,1,0:T(8,128)(2,1)S(1)}, u32[]{:S(2)}, u32[]{:S(2)}) collective-permute-start(bf16[4,1,16,128]{3,2,1,0:T(8,128)(2,1)S(1)} %get-tuple-element.255), channel_id=1, source_target_pairs={{0,8},{8,16},{16,24},{24,32},{32,40},{40,48},{48,56},{56,64},{64,7... | collective-permute-start | bytes 49160 | tf_op jit(solution)/shard_map/ppermute | solution.py:14
  122.0 9.5 %collective-permute-start.19 = (bf16[4,1,16,128]{3,2,1,0:T(8,128)(2,1)S(1)}, bf16[4,1,16,128]{3,2,1,0:T(8,128)(2,1)S(1)}, u32[]{:S(2)}, u32[]{:S(2)}) collective-permute-start(bf16[4,1,16,128]{3,2,1,0:T(8,128)(2,1)S(1)} %get-tuple-element.256), channel_id=1, source_target_pairs={{8,0},{16,8},{24,16},{32,24},{40,32},{48,40},{56,48},{64,56},{72,6... | collective-permute-start | bytes 49160 | tf_op jit(solution)/shard_map/ppermute | solution.py:17
  131.7 5.6 %collective-permute-start.20 = (bf16[4,18,1,128]{3,2,1,0:T(2,128)(2,1)S(1)}, bf16[4,18,1,128]{3,2,1,0:T(2,128)(2,1)S(1)}, u32[]{:S(2)}, u32[]{:S(2)}) collective-permute-start(bf16[4,18,1,128]{3,2,1,0:T(2,128)(2,1)S(1)} %get-tuple-element.239), channel_id=1, source_target_pairs={{0,1},{1,2},{2,3},{3,4},{4,5},{5,6},{6,7},{8,9},{9,10},{10,11},{11... | collective-permute-start | bytes 55304 | tf_op jit(solution)/shard_map/ppermute | solution.py:14
  133.6 5.3 %collective-permute-start.21 = (bf16[4,18,1,128]{3,2,1,0:T(2,128)(2,1)S(1)}, bf16[4,18,1,128]{3,2,1,0:T(2,128)(2,1)S(1)}, u32[]{:S(2)}, u32[]{:S(2)}) collective-permute-start(bf16[4,18,1,128]{3,2,1,0:T(2,128)(2,1)S(1)} %get-tuple-element.240), channel_id=1, source_target_pairs={{1,0},{2,1},{3,2},{4,3},{5,4},{6,5},{7,6},{9,8},{10,9},{11,10},{12... | collective-permute-start | bytes 55304 | tf_op jit(solution)/shard_map/ppermute | solution.py:17
  139.5 11.3 %collective-permute-start.22 = (bf16[4,1,16,128]{3,2,1,0:T(8,128)(2,1)S(1)}, bf16[4,1,16,128]{3,2,1,0:T(8,128)(2,1)S(1)}, u32[]{:S(2)}, u32[]{:S(2)}) collective-permute-start(bf16[4,1,16,128]{3,2,1,0:T(8,128)(2,1)S(1)} %get-tuple-element.253), channel_id=1, source_target_pairs={{0,8},{8,16},{16,24},{24,32},{32,40},{40,48},{48,56},{56,64},{64,7... | collective-permute-start | bytes 49160 | tf_op jit(solution)/shard_map/ppermute | solution.py:14
  148.9 9.5 %collective-permute-start.23 = (bf16[4,1,16,128]{3,2,1,0:T(8,128)(2,1)S(1)}, bf16[4,1,16,128]{3,2,1,0:T(8,128)(2,1)S(1)}, u32[]{:S(2)}, u32[]{:S(2)}) collective-permute-start(bf16[4,1,16,128]{3,2,1,0:T(8,128)(2,1)S(1)} %get-tuple-element.254), channel_id=1, source_target_pairs={{8,0},{16,8},{24,16},{32,24},{40,32},{48,40},{56,48},{64,56},{72,6... | collective-permute-start | bytes 49160 | tf_op jit(solution)/shard_map/ppermute | solution.py:17
  158.5 5.6 %collective-permute-start.24 = (bf16[4,18,1,128]{3,2,1,0:T(2,128)(2,1)S(1)}, bf16[4,18,1,128]{3,2,1,0:T(2,128)(2,1)S(1)}, u32[]{:S(2)}, u32[]{:S(2)}) collective-permute-start(bf16[4,18,1,128]{3,2,1,0:T(2,128)(2,1)S(1)} %get-tuple-element.237), channel_id=1, source_target_pairs={{0,1},{1,2},{2,3},{3,4},{4,5},{5,6},{6,7},{8,9},{9,10},{10,11},{11... | collective-permute-start | bytes 55304 | tf_op jit(solution)/shard_map/ppermute | solution.py:14
  161.3 4.4 %collective-permute-start.25 = (bf16[4,18,1,128]{3,2,1,0:T(2,128)(2,1)S(1)}, bf16[4,18,1,128]{3,2,1,0:T(2,128)(2,1)S(1)}, u32[]{:S(2)}, u32[]{:S(2)}) collective-permute-start(bf16[4,18,1,128]{3,2,1,0:T(2,128)(2,1)S(1)} %get-tuple-element.238), channel_id=1, source_target_pairs={{1,0},{2,1},{3,2},{4,3},{5,4},{6,5},{7,6},{9,8},{10,9},{11,10},{12... | collective-permute-start | bytes 55304 | tf_op jit(solution)/shard_map/ppermute | solution.py:17
  166.0 0.9 copy-start.3
  166.9 15.0 %collective-permute-start.26 = (bf16[2,16,16,128]{3,2,1,0:T(8,128)(2,1)S(1)}, bf16[2,16,16,128]{3,2,1,0:T(8,128)(2,1)S(1)}, u32[]{:S(2)}, u32[]{:S(2)}) collective-permute-start(bf16[2,16,16,128]{3,2,1,0:T(8,128)(2,1)S(1)} %fusion.26), channel_id=1, source_target_pairs={{0,128},{128,256},{256,384},{1,129},{129,257},{257,385},{2,130},{1... | collective-permute-start | bytes 393224 | tf_op jit(solution)/shard_map/ppermute | solution.py:25
  182.2 10.7 %collective-permute-start.27 = (bf16[4,1,16,128]{3,2,1,0:T(8,128)(2,1)S(1)}, bf16[4,1,16,128]{3,2,1,0:T(8,128)(2,1)S(1)}, u32[]{:S(2)}, u32[]{:S(2)}) collective-permute-start(bf16[4,1,16,128]{3,2,1,0:T(8,128)(2,1)S(1)} %get-tuple-element.251), channel_id=1, source_target_pairs={{0,8},{8,16},{16,24},{24,32},{32,40},{40,48},{48,56},{56,64},{64,7... | collective-permute-start | bytes 49160 | tf_op jit(solution)/shard_map/ppermute | solution.py:14
  190.9 9.5 %collective-permute-start.28 = (bf16[4,1,16,128]{3,2,1,0:T(8,128)(2,1)S(1)}, bf16[4,1,16,128]{3,2,1,0:T(8,128)(2,1)S(1)}, u32[]{:S(2)}, u32[]{:S(2)}) collective-permute-start(bf16[4,1,16,128]{3,2,1,0:T(8,128)(2,1)S(1)} %get-tuple-element.252), channel_id=1, source_target_pairs={{8,0},{16,8},{24,16},{32,24},{40,32},{48,40},{56,48},{64,56},{72,6... | collective-permute-start | bytes 49160 | tf_op jit(solution)/shard_map/ppermute | solution.py:17
  200.6 5.6 %collective-permute-start.29 = (bf16[4,18,1,128]{3,2,1,0:T(2,128)(2,1)S(1)}, bf16[4,18,1,128]{3,2,1,0:T(2,128)(2,1)S(1)}, u32[]{:S(2)}, u32[]{:S(2)}) collective-permute-start(bf16[4,18,1,128]{3,2,1,0:T(2,128)(2,1)S(1)} %get-tuple-element.235), channel_id=1, source_target_pairs={{0,1},{1,2},{2,3},{3,4},{4,5},{5,6},{6,7},{8,9},{9,10},{10,11},{11... | collective-permute-start | bytes 55304 | tf_op jit(solution)/shard_map/ppermute | solution.py:14
  203.1 5.1 %collective-permute-start.30 = (bf16[4,18,1,128]{3,2,1,0:T(2,128)(2,1)S(1)}, bf16[4,18,1,128]{3,2,1,0:T(2,128)(2,1)S(1)}, u32[]{:S(2)}, u32[]{:S(2)}) collective-permute-start(bf16[4,18,1,128]{3,2,1,0:T(2,128)(2,1)S(1)} %get-tuple-element.236), channel_id=1, source_target_pairs={{1,0},{2,1},{3,2},{4,3},{5,4},{6,5},{7,6},{9,8},{10,9},{11,10},{12... | collective-permute-start | bytes 55304 | tf_op jit(solution)/shard_map/ppermute | solution.py:17
  211.2 10.7 %collective-permute-start.31 = (bf16[4,1,16,128]{3,2,1,0:T(8,128)(2,1)S(1)}, bf16[4,1,16,128]{3,2,1,0:T(8,128)(2,1)S(1)}, u32[]{:S(2)}, u32[]{:S(2)}) collective-permute-start(bf16[4,1,16,128]{3,2,1,0:T(8,128)(2,1)S(1)} %get-tuple-element.249), channel_id=1, source_target_pairs={{0,8},{8,16},{16,24},{24,32},{32,40},{40,48},{48,56},{56,64},{64,7... | collective-permute-start | bytes 49160 | tf_op jit(solution)/shard_map/ppermute | solution.py:14
  214.9 9.5 %collective-permute-start.32 = (bf16[4,1,16,128]{3,2,1,0:T(8,128)(2,1)S(1)}, bf16[4,1,16,128]{3,2,1,0:T(8,128)(2,1)S(1)}, u32[]{:S(2)}, u32[]{:S(2)}) collective-permute-start(bf16[4,1,16,128]{3,2,1,0:T(8,128)(2,1)S(1)} %get-tuple-element.250), channel_id=1, source_target_pairs={{8,0},{16,8},{24,16},{32,24},{40,32},{48,40},{56,48},{64,56},{72,6... | collective-permute-start | bytes 49160 | tf_op jit(solution)/shard_map/ppermute | solution.py:17
  224.5 5.6 %collective-permute-start.33 = (bf16[4,18,1,128]{3,2,1,0:T(2,128)(2,1)S(1)}, bf16[4,18,1,128]{3,2,1,0:T(2,128)(2,1)S(1)}, u32[]{:S(2)}, u32[]{:S(2)}) collective-permute-start(bf16[4,18,1,128]{3,2,1,0:T(2,128)(2,1)S(1)} %get-tuple-element.233), channel_id=1, source_target_pairs={{0,1},{1,2},{2,3},{3,4},{4,5},{5,6},{6,7},{8,9},{9,10},{10,11},{11... | collective-permute-start | bytes 55304 | tf_op jit(solution)/shard_map/ppermute | solution.py:14
  227.7 4.0 %collective-permute-start.34 = (bf16[4,18,1,128]{3,2,1,0:T(2,128)(2,1)S(1)}, bf16[4,18,1,128]{3,2,1,0:T(2,128)(2,1)S(1)}, u32[]{:S(2)}, u32[]{:S(2)}) collective-permute-start(bf16[4,18,1,128]{3,2,1,0:T(2,128)(2,1)S(1)} %get-tuple-element.234), channel_id=1, source_target_pairs={{1,0},{2,1},{3,2},{4,3},{5,4},{6,5},{7,6},{9,8},{10,9},{11,10},{12... | collective-permute-start | bytes 55304 | tf_op jit(solution)/shard_map/ppermute | solution.py:17
where the time goes:
time: 239 us; the launch traced here: 235 us
  starting transfers between devices  134 us (56%)
  waiting for transfers between devices  83.4 us (35%)
  local copies, waits for them, and re-layouts  7.4 us (3%)
  other arithmetic  6.55 us (3%)
    ppermute x16, starting transfers between devices, with_halo(): lax.ppermute(lax.slice_in_dim(block, block.shape[dim] - width, None, axis...  65.4 us
    ppermute x16, starting transfers between devices, with_halo(): lax.ppermute(lax.slice_in_dim(block, 0, width, axis=dim), axis, backward)  64.5 us
    ppermute x16, waiting for transfers between devices, with_halo(): lax.ppermute(lax.slice_in_dim(block, 0, width, axis=dim), axis, backward)  49.5 us
    ppermute x3, waiting for transfers between devices, shifted(): lax.ppermute(value, axis, [(source, source + steps) for source in range(i...  25.5 us
    ppermute x16, waiting for transfers between devices, with_halo(): lax.ppermute(lax.slice_in_dim(block, block.shape[dim] - width, None, axis...  8.45 us
  transfers between devices with their start and end apart: 35, of which 19 were waited for; matrix products, arithmetic and copies ran while one was open for 0% of the time, Pallas kernels for 0%

commit v1 on v0

v1 whole, which is shorter than its diff:
```python
import functools

import jax
import jax.numpy as jnp
from jax import lax
from jax.experimental import pallas as pl
from jax.experimental.pallas import tpu as pltpu
from jax.sharding import PartitionSpec as P

PITCH = 32
CHUNK = 8
AXES = ("segment", "row", "col")


def norm_act(values, gain_row, mask):
    scale = lax.rsqrt(jnp.mean(values * values, axis=-1, keepdims=True) + 1e-06)
    scaled = values * scale * gain_row
    return scaled / (1.0 + jnp.exp(-scaled)) * mask


def chunks(rows):
    return [(first, min(CHUNK, rows - first)) for first in range(0, rows, CHUNK)]


def column_mask(side, width, channels):
    col = lax.broadcasted_iota(jnp.int32, (PITCH, channels), 0) + side
    return jnp.where((col >= 0) & (col < width), 1.0, 0.0)


def cell_mask(columns, top, height, first, count):
    parts = []
    for row in range(first, first + count):
        here = top + row
        parts.append(columns * jnp.where((here >= 0) & (here < height), 1.0, 0.0))
    return jnp.concatenate(parts, axis=0)


def spread(source, start, patches, block, rows):
    channels = source.shape[-1]
    for tap in range(3):
        lane = (block * 3 + tap) * channels
        begin = start + tap
        patches[: rows * PITCH, lane : lane + channels] = source[
            begin : begin + rows * PITCH, :
        ].astype(jnp.bfloat16)


def weight_rows(kernel, tap, left, right):
    empty = jnp.zeros(kernel.shape[2:], jnp.bfloat16)

    def column(taps):
        return jnp.concatenate(
            [empty if t is None else kernel[t, tap] for t in taps], axis=0
        )

    return jnp.concatenate([column(left), column(right)], axis=1)


BOTH = ((0, 1, 2, None), (None, 0, 1, 2))
HELD = ((0, 1), (None, 0))
FRESH = ((2, None), (1, 2))


def convolve(patches, kernel, taps, total, first, rows):
    count = rows * PITCH
    for tap in range(3):
        begin = (first + tap) * PITCH
        total = total + jnp.dot(
            patches[begin : begin + count, :],
            weight_rows(kernel, tap, *taps),
            preferred_element_type=jnp.float32,
        )
    return total


def bias_of(bias, count):
    return jnp.broadcast_to(
        jnp.concatenate([bias, bias], axis=1), (count, 2 * bias.shape[-1])
    )


def assemble(grid, frame, source, mid, low, high, left, right):
    reach = low.shape[1]
    tile = mid.shape[1]
    for row in range(tile + 2 * reach):
        begin = row * PITCH
        if row < reach:
            body = low[source, row]
        elif row < reach + tile:
            body = mid[source, row - reach]
        else:
            body = high[source, row - reach - tile]
        grid[frame, begin : begin + reach, :] = left[source, row].astype(jnp.float32)
        grid[frame, begin + reach : begin + reach + tile, :] = body.astype(jnp.float32)
        grid[frame, begin + reach + tile : begin + 2 * reach + tile, :] = right[
            source, row
        ].astype(jnp.float32)


def finish(step, place, halo, span, first, count, branch, held, o_ref, r_ref):
    channels = held.shape[-1]
    tile = r_ref.shape[2]
    edge = halo - 2
    for frame in range(2):
        offset = (first + 2) * PITCH + 2
        out = (
            held[frame, offset : offset + count * PITCH, :]
            + branch[:, frame * channels : (frame + 1) * channels]
        )
        for row in range(count):
            line = out[row * PITCH : (row + 1) * PITCH]
            if o_ref is not None:
                o_ref[frame, first + row] = line[: span - 4].astype(jnp.bfloat16)
            own = first + row - edge
            if 0 <= own < tile:
                cells = line[edge : edge + tile].astype(jnp.bfloat16)
                if step == 0:
                    r_ref[frame, own] = cells
                else:

                    @pl.when(place[2] == step)
                    def _(frame=frame, own=own, cells=cells):
                        r_ref[frame, own] = cells


def middle(place, halo, height, width, hidden_of, g_ref, flat, span):
    channels = g_ref.shape[-1]
    tile = span - 2 * halo
    top = place[0] * tile - (halo - 1)
    columns = column_mask(place[1] * tile - (halo - 1), width, channels)
    for first, count in chunks(span - 2):
        hidden = hidden_of(first, count)
        keep = cell_mask(columns, top, height, first, count)
        for frame in range(2):
            flat[frame, first * PITCH : (first + count) * PITCH, :] = norm_act(
                hidden[:, frame * channels : (frame + 1) * channels], g_ref[1:2, :], keep
            )


def entry(place, halo, height, width, held, g_ref, flat, span):
    channels = g_ref.shape[-1]
    tile = span - 2 * halo
    top = place[0] * tile - halo
    columns = column_mask(place[1] * tile - halo, width, channels)
    for first, count in chunks(span):
        area = pl.ds(first * PITCH, count * PITCH)
        keep = cell_mask(columns, top, height, first, count)
        for frame in range(2):
            flat[frame, area, :] = norm_act(held[frame, area, :], g_ref[0:1, :], keep)


def first_kernel(
    halo, height, width, place, frames, cached, low, high, left, right, w_ref, b_ref, g_ref,
    o_ref, r_ref, grid, flat, patches,
):
    tile = frames.shape[1]
    span = tile + 2 * halo
    for frame in range(2):
        assemble(grid, frame, frame, frames, low, high, left, right)
    for frame in range(4):
        assemble(
            grid, frame + 2, frame, cached, low.at[2:6], high.at[2:6],
            left.at[2:6], right.at[2:6],
        )
    entry(place, halo, height, width, grid, g_ref, flat, span)
    for frame in range(2):
        spread(grid.at[frame + 2], 0, patches, frame, span)
        spread(flat.at[frame], 0, patches, frame + 2, span)
    middle(
        place, halo, height, width,
        lambda first, count: convolve(
            patches, w_ref.at[0], BOTH, bias_of(b_ref[0:1, :], count * PITCH), first, count
        ),
        g_ref, flat, span,
    )
    for frame in range(2):
        spread(grid.at[frame + 4], PITCH + 1, patches, frame, span - 2)
        spread(flat.at[frame], 0, patches, frame + 2, span - 2)
    for first, count in chunks(span - 4):
        branch = convolve(
            patches, w_ref.at[1], BOTH, bias_of(b_ref[1:2, :], count * PITCH), first, count
        )
        finish(0, place, halo, span, first, count, branch, grid, o_ref, r_ref)


def held_kernel(
    cached, low, high, left, right, w_ref, b_ref, one_ref, two_ref, grid, patches
):
    span = cached.shape[1] + 2 * low.shape[1]
    for frame in range(4):
        assemble(grid, frame, frame, cached, low, high, left, right)
    for conv, out in ((0, one_ref), (1, two_ref)):
        start = conv * (PITCH + 1)
        rows = span - 2 * conv
        for frame in range(2):
            spread(grid.at[2 * conv + frame], start, patches, frame, rows)
        for first, count in chunks(rows - 2):
            out[first * PITCH : (first + count) * PITCH, :] = convolve(
                patches, w_ref.at[conv], HELD,
                bias_of(b_ref[conv : conv + 1, :], count * PITCH), first, count,
            )


def later_kernel(
    step, halo, drop, height, width, place, x_ref, one_ref, two_ref, w_ref, g_ref, p_ref,
    *rest,
):
    o_ref = rest[0] if len(rest) == 5 else None
    r_ref, held, flat, patches = rest[-4:]
    span = x_ref.shape[1]
    r_ref[...] = p_ref[...]
    for frame in range(2):
        for row in range(span):
            held[frame, row * PITCH : row * PITCH + span, :] = x_ref[frame, row].astype(
                jnp.float32
            )
    entry(place, halo, height, width, held, g_ref, flat, span)
    for frame in range(2):
        spread(flat.at[frame], 0, patches, frame, span)

    def known(ref, first, count):
        begin = drop * (PITCH + 1) + first * PITCH
        return ref[begin : begin + count * PITCH, :]

    middle(
        place, halo, height, width,
        lambda first, count: convolve(
            patches, w_ref.at[0], FRESH, known(one_ref, first, count), first, count
        ),
        g_ref, flat, span,
    )
    for frame in range(2):
        spread(flat.at[frame], 0, patches, frame, span - 2)
    for first, count in chunks(span - 4):
        branch = convolve(
            patches, w_ref.at[1], FRESH, known(two_ref, first, count), first, count
        )
        finish(step, place, halo, span, first, count, branch, held, o_ref, r_ref)


SCALARS = pl.BlockSpec(memory_space=pltpu.SMEM)
WHOLE = pl.BlockSpec(memory_space=pltpu.VMEM)


def cost(span, frames, channels):
    return pl.CostEstimate(
        flops=4 * 9 * frames * span * PITCH * channels * 2 * channels,
        bytes_accessed=4 << 20,
        transcendentals=0,
    )


def first_section(place, frames, cached, pieces, weights, biases, gains, halo, height, width):
    tile, channels = frames.shape[1], frames.shape[-1]
    span = tile + 2 * halo
    room = span * PITCH + 3 * PITCH
    return pl.pallas_call(
        functools.partial(first_kernel, halo, height, width),
        out_shape=(
            jax.ShapeDtypeStruct((2, span - 4, span - 4, channels), jnp.bfloat16),
            jax.ShapeDtypeStruct(frames.shape, jnp.bfloat16),
        ),
        in_specs=[SCALARS] + [WHOLE] * 9,
        out_specs=(WHOLE, WHOLE),
        scratch_shapes=[
            pltpu.VMEM((6, room, channels), jnp.float32),
            pltpu.VMEM((2, room, channels), jnp.float32),
            pltpu.VMEM((room, 12 * channels), jnp.bfloat16),
        ],
        cost_estimate=cost(span, 4, channels),
        compiler_params=pltpu.CompilerParams(vmem_limit_bytes=40 << 20),
    )(place, frames, cached, *pieces, weights, biases, gains)


def held_part(cached, pieces, weights, biases):
    channels = cached.shape[-1]
    span = cached.shape[1] + 2 * pieces[0].shape[1]
    room = span * PITCH + 3 * PITCH
    return pl.pallas_call(
        held_kernel,
        out_shape=(
            jax.ShapeDtypeStruct(((span - 2) * PITCH, 2 * channels), jnp.float32),
            jax.ShapeDtypeStruct(((span - 4) * PITCH, 2 * channels), jnp.float32),
        ),
        in_specs=[WHOLE] * 7,
        out_specs=(WHOLE, WHOLE),
        scratch_shapes=[
            pltpu.VMEM((4, room, channels), jnp.float32),
            pltpu.VMEM((room, 6 * channels), jnp.bfloat16),
        ],
        cost_estimate=cost(span, 2, channels),
        compiler_params=pltpu.CompilerParams(vmem_limit_bytes=40 << 20),
    )(cached, *pieces, weights, biases)


def later_section(
    step, place, values, known, weights, gains, results, halo, drop, last, height, width
):
    span, channels = values.shape[1], values.shape[-1]
    room = span * PITCH + 3 * PITCH
    out_shape = [jax.ShapeDtypeStruct(results.shape, jnp.bfloat16)]
    if not last:
        onward = (2, span - 4, span - 4, channels)
        out_shape = [jax.ShapeDtypeStruct(onward, jnp.bfloat16)] + out_shape
    return pl.pallas_call(
        functools.partial(later_kernel, step, halo, drop, height, width),
        out_shape=out_shape,
        in_specs=[SCALARS] + [WHOLE] * 6,
        out_specs=[WHOLE] * len(out_shape),
        scratch_shapes=[
            pltpu.VMEM((2, room, channels), jnp.float32),
            pltpu.VMEM((2, room, channels), jnp.float32),
            pltpu.VMEM((room, 6 * channels), jnp.bfloat16),
        ],
        cost_estimate=cost(span, 2, channels),
        compiler_params=pltpu.CompilerParams(vmem_limit_bytes=40 << 20),
    )(place, values, *known, weights, gains, results)


def moved(value, segments, shift):
    sizes = [lax.axis_size(axis) for axis in AXES]
    pairs = []
    for segment in segments:
        for row in range(sizes[1]):
            for col in range(sizes[2]):
                target = (segment + shift[0], row + shift[1], col + shift[2])
                if all(0 <= t < n for t, n in zip(target, sizes)):
                    source = (segment * sizes[1] + row) * sizes[2] + col
                    place = (target[0] * sizes[1] + target[1]) * sizes[2] + target[2]
                    pairs.append((source, place))
    return lax.ppermute(value, AXES, pairs)


def ends(parts, cut):
    taken = [cut(part) for part in parts]
    return taken[0] if len(taken) == 1 else jnp.concatenate(taken, axis=0)


def rows_of(parts, segments, halo):
    low = moved(
        ends(parts, lambda part: part[:, part.shape[1] - halo :]), segments, (0, 1, 0)
    )
    high = moved(ends(parts, lambda part: part[:, :halo]), segments, (0, -1, 0))
    return low, high


def sides_of(parts, low, high, halo):
    def side(cut):
        return jnp.concatenate([cut(low), ends(parts, cut), cut(high)], axis=1)

    return side(lambda part: part[:, :, part.shape[2] - halo :]), side(
        lambda part: part[:, :, :halo]
    )


def columns_of(left, right, segments):
    return moved(left, segments, (0, 0, 1)), moved(right, segments, (0, 0, -1))


def on_device(height, width, frames, caches, weights, biases, gains):
    sections = lax.axis_size("segment")
    place = jnp.stack(
        [lax.axis_index("row"), lax.axis_index("col"), lax.axis_index("segment")]
    ).astype(jnp.int32)
    channels = frames.shape[-1]
    kernels = weights[0].reshape((2, 3, 3, 3 * channels, channels))
    cached = caches[0].reshape((4,) + frames.shape[1:])
    halo = 2 * sections
    reach = halo - 2
    others = list(range(1, sections))
    low, high = rows_of([frames, cached], [0], halo)
    left, right = sides_of([frames, cached], low, high, halo)
    left, right = columns_of(left, right, [0])
    left, later = lax.optimization_barrier((left, cached))
    pieces = (low, high, left, right)
    low, high = rows_of([later], others, reach)
    left, right = sides_of([later], low, high, reach)
    ahead = (low, high) + columns_of(left, right, others)
    values, results = first_section(
        place, frames, cached, pieces, kernels, biases[0], gains[0], halo, height, width
    )
    values, cached = lax.optimization_barrier((values, cached))
    received = moved(values, [0], (1, 0, 0))
    known = held_part(cached, ahead, kernels, biases[0])
    halo = reach
    for step in others:
        last = step == sections - 1
        outs = later_section(
            step, place, received, known, kernels, gains[0], results,
            halo, reach - halo, last, height, width,
        )
        results = outs[-1]
        halo = halo - 2
        if not last:
            received = moved(outs[0], [step], (1, 0, 0))
    return results[None]


def solution(mesh):
    height = 16 * mesh.shape["row"]
    width = 16 * mesh.shape["col"]
    in_specs = (
        P(None, "row", "col", None),
        P("segment", None, None, "row", "col", None),
        P("segment", None, None, None, None, None, None),
        P("segment", None, None),
        P("segment", None, None),
    )
    out_specs = P("segment", None, "row", "col", None)
    return jax.shard_map(
        functools.partial(on_device, height, width),
        mesh=mesh, in_specs=in_specs, out_specs=out_specs, check_vma=False,
    )
```

time: 239 us -> 83.2 us (0.35)
  the two profiles are of different devices: /device:TPU:210 before, /device:TPU:204 now
where the time goes in v1:
time: 83.2 us; the launch traced here: 82.9 us
  waiting for transfers between devices  35.5 us (43%)
  starting transfers between devices  21.4 us (26%)
  Pallas kernels  20 us (24%)
  local copies, waits for them, and re-layouts  4.44 us (5%)
  other arithmetic  1.27 us (2%)
    ppermute x11, waiting for transfers between devices, moved(): return lax.ppermute(value, AXES, pairs)  35.5 us
    ppermute x11, starting transfers between devices, moved(): return lax.ppermute(value, AXES, pairs)  21.4 us
    pallas_call x3, Pallas kernels, later_section(): pl.pallas_call(functools.partial(later_kernel, step, halo, drop, height,...  11.7 us
    pallas_call x1, Pallas kernels, first_section(): pl.pallas_call(functools.partial(first_kernel, halo, height, width), out_...  5.8 us
    slice x7, local copies, waits for them, and re-layouts, sides_of(): part[:, :, :halo]  2.48 us
    pallas_call x1, Pallas kernels, held_part(): pl.pallas_call(held_kernel, out_shape=(jax.ShapeDtypeStruct(((span - 2) *...  2.42 us
    slice x3, local copies, waits for them, and re-layouts, rows_of(): high = moved(ends(parts, lambda part: part[:, :halo]), segments, (0, -1, 0))  1.93 us
  transfers between devices with their start and end apart: 11, of which 4 were waited for; matrix products, arithmetic and copies ran while one was open for 4% of the time, Pallas kernels for 10%

profile of v1, /device:TPU:204, one launch (start us, length us, event | category | flops | bytes accessed | tf_op | source)
XLA Modules:
  0.0 82.9 jit_solution(11943804516561671178)
XLA Ops:
  0.0 0.0 copy-start.1
  0.0 0.9 %fusion.7 = (bf16[2,8,16,128]{3,2,1,0:T(8,128)(2,1)S(1)}, bf16[2,8,16,128]{3,2,1,0:T(8,128)(2,1)S(1)}) fusion(bf16[2,16,16,128]{3,2,1,0:T(8,128)(2,1)} %frames.1), kind=kLoop, calls=%fused_computation.14 | loop fusion | bytes 262144 | tf_op jit(solution)/shard_map/slice | solution.py:343
  0.9 1.0 %fusion.3 = (bf16[4,8,16,128]{3,2,1,0:T(8,128)(2,1)S(1)}, bf16[4,8,16,128]{3,2,1,0:T(8,128)(2,1)S(1)}) fusion(bf16[4,16,16,128]{3,2,1,0:T(8,128)(2,1)} %bitcast.8), kind=kLoop, calls=%fused_computation.10 | loop fusion | bytes 524288 | tf_op jit(solution)/shard_map/slice | solution.py:343
  2.0 0.7 collective-permute-start
  2.6 0.0 copy-start
  2.7 0.8 collective-permute-start.1
  3.5 1.0 %fusion.2 = (bf16[4,16,8,128]{3,2,1,0:T(8,128)(2,1)S(1)}, bf16[4,16,8,128]{3,2,1,0:T(8,128)(2,1)S(1)}) fusion(bf16[4,16,16,128]{3,2,1,0:T(8,128)(2,1)} %bitcast.9), kind=kLoop, calls=%fused_computation.9 | loop fusion | bytes 524288 | tf_op jit(solution)/shard_map/slice | solution.py:352
  4.5 0.0 copy-done.1
  4.5 0.0 copy-start.2
  4.5 0.0 copy-start.3
  4.5 0.0 copy-start.4
  4.6 0.0 collective-permute-done.low
  4.6 0.7 fusion.4
  5.2 0.0 collective-permute-done.1.high
  5.3 0.7 fusion.5
  5.9 0.1 pad_maximum_fusion
  6.0 0.7 collective-permute-start.2
  6.7 0.1 pad_add_fusion.place
  6.8 1.0 %pad_maximum_fusion.1 = bf16[6,32,8,128]{3,2,1,0:T(8,128)(2,1)S(1)} fusion(bf16[6,8,8,128]{3,2,1,0:T(8,128)(2,1)} %get-tuple-element.39, bf16[4,16,8,128]{3,2,1,0:T(8,128)(2,1)S(1)} %get-tuple-element.33, bf16[2,16,8,128]{3,2,1,0:T(8,128)(2,1)S(1)} %get-tuple-element.41, bf16[6,8,8,128]{3,2,1,0:T(8,128)(2,1)} %get-tuple-element.37), kind=kLoop, calls=%fused_computation.1 | loop fusion | flops 589824 | bytes 786432 | tf_op jit(solution)/shard_map/concatenate | solution.py:349
  7.8 0.7 collective-permute-start.3
  8.5 0.0 collective-permute-done.2.left
  8.5 0.0 copy-done
  8.5 8.1 %collective-permute-start.6 = (bf16[4,6,16,128]{3,2,1,0:T(8,128)(2,1)S(1)}, bf16[4,6,16,128]{3,2,1,0:T(8,128)(2,1)S(1)}, u32[]{:S(2)}, u32[]{:S(2)}) collective-permute-start(bf16[4,6,16,128]{3,2,1,0:T(8,128)(2,1)S(1)} %get-tuple-element.31), channel_id=1, source_target_pairs={{136,128},{137,129},{138,130},{139,131},{140,132},{141,133},{142,1... | collective-permute-start | bytes 294920 | tf_op jit(solution)/shard_map/ppermute | solution.py:331
  16.6 2.0 %collective-permute-start.5 = (bf16[4,6,16,128]{3,2,1,0:T(8,128)(2,1)S(1)}, bf16[4,6,16,128]{3,2,1,0:T(8,128)(2,1)S(1)}, u32[]{:S(2)}, u32[]{:S(2)}) collective-permute-start(bf16[4,6,16,128]{3,2,1,0:T(8,128)(2,1)S(1)} %get-tuple-element.32), channel_id=1, source_target_pairs={{128,136},{129,137},{130,138},{131,139},{132,140},{133,141},{134,1... | collective-permute-start | bytes 294920 | tf_op jit(solution)/shard_map/ppermute | solution.py:331
  18.7 0.1 fusion
  18.7 0.0 collective-permute-done.3.right
  18.7 0.0 copy-done.2
  18.7 0.0 copy-done.3
  18.8 0.0 copy-done.4
  18.8 5.8 %shard_map.55 = (bf16[2,28,28,128]{3,2,1,0:T(8,128)(2,1)S(1)}, bf16[2,16,16,128]{3,2,1,0:T(8,128)(2,1)S(1)}) custom-call(s32[3]{0:T(128)S(1)} %pad_add_fusion.place, bf16[2,16,16,128]{3,2,1,0:T(8,128)(2,1)S(1)} %copy-done.1, bf16[4,16,16,128]{3,2,1,0:T(8,128)(2,1)S(1)} %bitcast.12, bf16[6,8,16,128]{3,2,1,0:T(8,128)(2,1)S(1)} %collective-permute-done.low, ...), custom_call_target="tpu_custom_call" | custom-call | flops 4831838208 | bytes 4194304 | tf_op jit(solution)/shard_map/pallas_call | solution.py:257
  24.6 0.7 collective-permute-start.4
  25.3 0.0 collective-permute-done.6.high
  25.3 2.9 %collective-permute-done.5.low = bf16[4,6,16,128]{3,2,1,0:T(8,128)(2,1)S(1)} collective-permute-done((bf16[4,6,16,128]{3,2,1,0:T(8,128)(2,1)S(1)}, bf16[4,6,16,128]{3,2,1,0:T(8,128)(2,1)S(1)}, u32[]{:S(2)}, u32[]{:S(2)}) %collective-permute-start.5) | collective-permute-done | bytes 98336 | tf_op jit(solution)/shard_map/ppermute | solution.py:331
  28.2 0.1 pad_maximum_fusion.2
  28.3 1.9 %collective-permute-start.7 = (bf16[4,28,6,128]{3,2,1,0:T(8,128)(2,1)S(1)}, bf16[4,28,6,128]{3,2,1,0:T(8,128)(2,1)S(1)}, u32[]{:S(2)}, u32[]{:S(2)}) collective-permute-start(bf16[4,28,6,128]{3,2,1,0:T(8,128)(2,1)S(1)} %pad_maximum_fusion.2), channel_id=1, source_target_pairs={{128,129},{129,130},{130,131},{131,132},{132,133},{133,134},{134,1... | collective-permute-start | bytes 516104 | tf_op jit(solution)/shard_map/ppermute | solution.py:331
  30.2 0.1 pad_maximum_fusion.3
  30.3 3.6 %collective-permute-start.8 = (bf16[4,28,6,128]{3,2,1,0:T(8,128)(2,1)S(1)}, bf16[4,28,6,128]{3,2,1,0:T(8,128)(2,1)S(1)}, u32[]{:S(2)}, u32[]{:S(2)}) collective-permute-start(bf16[4,28,6,128]{3,2,1,0:T(8,128)(2,1)S(1)} %pad_maximum_fusion.3), channel_id=1, source_target_pairs={{129,128},{130,129},{131,130},{132,131},{133,132},{134,133},{135,1... | collective-permute-start | bytes 516104 | tf_op jit(solution)/shard_map/ppermute | solution.py:331
  34.0 1.7 %collective-permute-done.7.left = bf16[4,28,6,128]{3,2,1,0:T(8,128)(2,1)S(1)} collective-permute-done((bf16[4,28,6,128]{3,2,1,0:T(8,128)(2,1)S(1)}, bf16[4,28,6,128]{3,2,1,0:T(8,128)(2,1)S(1)}, u32[]{:S(2)}, u32[]{:S(2)}) %collective-permute-start.7) | collective-permute-done | bytes 172064 | tf_op jit(solution)/shard_map/ppermute | solution.py:331
  35.7 1.8 %collective-permute-done.8.right = bf16[4,28,6,128]{3,2,1,0:T(8,128)(2,1)S(1)} collective-permute-done((bf16[4,28,6,128]{3,2,1,0:T(8,128)(2,1)S(1)}, bf16[4,28,6,128]{3,2,1,0:T(8,128)(2,1)S(1)}, u32[]{:S(2)}, u32[]{:S(2)}) %collective-permute-start.8) | collective-permute-done | bytes 172064 | tf_op jit(solution)/shard_map/ppermute | solution.py:331
  37.5 2.4 %shard_map.56 = (f32[832,256]{1,0:T(8,128)S(1)}, f32[768,256]{1,0:T(8,128)S(1)}) custom-call(bf16[4,16,16,128]{3,2,1,0:T(8,128)(2,1)S(1)} %bitcast.13, bf16[4,6,16,128]{3,2,1,0:T(8,128)(2,1)S(1)} %collective-permute-done.5.low, bf16[4,6,16,128]{3,2,1,0:T(8,128)(2,1)S(1)} %collective-permute-done.6.high, ...), custom_call_target="tpu_custom_call" | custom-call | flops 2113929216 | bytes 4194304 | tf_op jit(solution)/shard_map/pallas_call | solution.py:279
  39.9 0.0 collective-permute-done.4.x_ref
  39.9 4.6 %shard_map.57 = (bf16[2,24,24,128]{3,2,1,0:T(8,128)(2,1)S(1)}, bf16[2,16,16,128]{3,2,1,0:T(8,128)(2,1)S(1)}) custom-call(s32[3]{0:T(128)S(1)} %pad_add_fusion.place, bf16[2,28,28,128]{3,2,1,0:T(8,128)(2,1)S(1)} %collective-permute-done.4.x_ref, f32[832,256]{1,0:T(8,128)S(1)} %get-tuple-element.22.one_ref, f32[768,256]{1,0:T(8,128)S(1)} %get-tuple-element.23.two_ref, ...), custom_call_target="tpu_custom_call" | custom-call | flops 2113929216 | bytes 4194304 | tf_op jit(solution)/shard_map/pallas_call | solution.py:305
  44.5 0.9 %collective-permute-start.9 = (bf16[2,24,24,128]{3,2,1,0:T(8,128)(2,1)S(1)}, bf16[2,24,24,128]{3,2,1,0:T(8,128)(2,1)S(1)}, u32[]{:S(2)}, u32[]{:S(2)}) collective-permute-start(bf16[2,24,24,128]{3,2,1,0:T(8,128)(2,1)S(1)} %get-tuple-element.25), channel_id=1, source_target_pairs={{128,256},{129,257},{130,258},{131,259},{132,260},{133,261},{134,2... | collective-permute-start | bytes 884744 | tf_op jit(solution)/shard_map/ppermute | solution.py:331
  45.3 0.0 collective-permute-done.9.x_ref
  45.3 3.6 %shard_map.58 = (bf16[2,20,20,128]{3,2,1,0:T(8,128)(2,1)S(1)}, bf16[2,16,16,128]{3,2,1,0:T(8,128)(2,1)S(1)}) custom-call(s32[3]{0:T(128)S(1)} %pad_add_fusion.place, bf16[2,24,24,128]{3,2,1,0:T(8,128)(2,1)S(1)} %collective-permute-done.9.x_ref, f32[832,256]{1,0:T(8,128)S(1)} %get-tuple-element.22.one_ref, f32[768,256]{1,0:T(8,128)S(1)} %get-tuple-element.23.two_ref, ...), custom_call_target="tpu_custom_call" | custom-call | flops 1811939328 | bytes 4194304 | tf_op jit(solution)/shard_map/pallas_call | solution.py:305
  48.9 1.3 %collective-permute-start.10 = (bf16[2,20,20,128]{3,2,1,0:T(8,128)(2,1)S(1)}, bf16[2,20,20,128]{3,2,1,0:T(8,128)(2,1)S(1)}, u32[]{:S(2)}, u32[]{:S(2)}) collective-permute-start(bf16[2,20,20,128]{3,2,1,0:T(8,128)(2,1)S(1)} %get-tuple-element.27), channel_id=1, source_target_pairs={{256,384},{257,385},{258,386},{259,387},{260,388},{261,389},{262,3... | collective-permute-start | bytes 614408 | tf_op jit(solution)/shard_map/ppermute | solution.py:331
  50.2 29.0 %collective-permute-done.10.x_ref = bf16[2,20,20,128]{3,2,1,0:T(8,128)(2,1)S(1)} collective-permute-done((bf16[2,20,20,128]{3,2,1,0:T(8,128)(2,1)S(1)}, bf16[2,20,20,128]{3,2,1,0:T(8,128)(2,1)S(1)}, u32[]{:S(2)}, u32[]{:S(2)}) %collective-permute-start.10) | collective-permute-done | bytes 204832 | tf_op jit(solution)/shard_map/ppermute | solution.py:331
  79.2 3.6 %shard_map.59 = bf16[2,16,16,128]{3,2,1,0:T(8,128)(2,1)} custom-call(s32[3]{0:T(128)S(1)} %pad_add_fusion.place, bf16[2,20,20,128]{3,2,1,0:T(8,128)(2,1)S(1)} %collective-permute-done.10.x_ref, f32[832,256]{1,0:T(8,128)S(1)} %get-tuple-element.22.one_ref, f32[768,256]{1,0:T(8,128)S(1)} %get-tuple-element.23.two_ref, ...), custom_call_target="tpu_custom_call" | custom-call | flops 1509949440 | bytes 4194304 | tf_op jit(solution)/shard_map/pallas_call | solution.py:305
  (6 shorter events, 0.1 us)
Async XLA Ops:
  0.0 4.5 %copy-start.1 = (bf16[2,16,16,128]{3,2,1,0:T(8,128)(2,1)S(1)}, bf16[2,16,16,128]{3,2,1,0:T(8,128)(2,1)}, u32[]{:S(2)}) copy-start(bf16[2,16,16,128]{3,2,1,0:T(8,128)(2,1)} %frames.1) | copy-start | bytes 393220
  2.0 2.6 %collective-permute-start = (bf16[6,8,16,128]{3,2,1,0:T(8,128)(2,1)S(1)}, bf16[6,8,16,128]{3,2,1,0:T(8,128)(2,1)S(1)}, u32[]{:S(2)}, u32[]{:S(2)}) collective-permute-start(bf16[6,8,16,128]{3,2,1,0:T(8,128)(2,1)S(1)} %pad_maximum_fusion.4), channel_id=1, source_target_pairs={{0,8},{1,9},{2,10},{3,11},{4,12},{5,13},{6,14},{7,15},{8,16},{9,17... | collective-permute-start | bytes 589832 | tf_op jit(solution)/shard_map/ppermute | solution.py:331
  2.6 5.8 %copy-start = (bf16[1,2,2,16,16,128]{5,4,3,2,1,0:T(8,128)(2,1)S(1)}, bf16[1,2,2,16,16,128]{5,4,3,2,1,0:T(8,128)(2,1)}, u32[]{:S(2)}) copy-start(bf16[1,2,2,16,16,128]{5,4,3,2,1,0:T(8,128)(2,1)} %param.6) | copy-start | bytes 786436
  2.7 2.6 %collective-permute-start.1 = (bf16[6,8,16,128]{3,2,1,0:T(8,128)(2,1)S(1)}, bf16[6,8,16,128]{3,2,1,0:T(8,128)(2,1)S(1)}, u32[]{:S(2)}, u32[]{:S(2)}) collective-permute-start(bf16[6,8,16,128]{3,2,1,0:T(8,128)(2,1)S(1)} %pad_maximum_fusion.5), channel_id=1, source_target_pairs={{8,0},{9,1},{10,2},{11,3},{12,4},{13,5},{14,6},{15,7},{16,8},{17,9... | collective-permute-start | bytes 589832 | tf_op jit(solution)/shard_map/ppermute | solution.py:331
  4.5 14.2 %copy-start.2 = (bf16[1,2,3,3,3,128,128]{6,5,4,3,2,1,0:T(8,128)(2,1)S(1)}, bf16[1,2,3,3,3,128,128]{6,5,4,3,2,1,0:T(8,128)(2,1)}, u32[]{:S(2)}) copy-start(bf16[1,2,3,3,3,128,128]{6,5,4,3,2,1,0:T(8,128)(2,1)} %param.7) | copy-start | bytes 5308420
  4.5 14.2 %copy-start.3 = (f32[1,2,128]{2,1,0:T(2,128)S(1)}, f32[1,2,128]{2,1,0:T(2,128)}, u32[]{:S(2)}) copy-start(f32[1,2,128]{2,1,0:T(2,128)} %param.8) | copy-start | bytes 3076
  4.5 14.2 %copy-start.4 = (f32[1,2,128]{2,1,0:T(2,128)S(1)}, f32[1,2,128]{2,1,0:T(2,128)}, u32[]{:S(2)}) copy-start(f32[1,2,128]{2,1,0:T(2,128)} %param.9) | copy-start | bytes 3076
  6.0 2.5 %collective-permute-start.2 = (bf16[6,32,8,128]{3,2,1,0:T(8,128)(2,1)S(1)}, bf16[6,32,8,128]{3,2,1,0:T(8,128)(2,1)S(1)}, u32[]{:S(2)}, u32[]{:S(2)}) collective-permute-start(bf16[6,32,8,128]{3,2,1,0:T(8,128)(2,1)S(1)} %pad_maximum_fusion), channel_id=1, source_target_pairs={{0,1},{1,2},{2,3},{3,4},{4,5},{5,6},{6,7},{8,9},{9,10},{10,11},{11... | collective-permute-start | bytes 1179656 | tf_op jit(solution)/shard_map/ppermute | solution.py:331
  7.8 11.0 %collective-permute-start.3 = (bf16[6,32,8,128]{3,2,1,0:T(8,128)(2,1)S(1)}, bf16[6,32,8,128]{3,2,1,0:T(8,128)(2,1)S(1)}, u32[]{:S(2)}, u32[]{:S(2)}) collective-permute-start(bf16[6,32,8,128]{3,2,1,0:T(8,128)(2,1)S(1)} %pad_maximum_fusion.1), channel_id=1, source_target_pairs={{1,0},{2,1},{3,2},{4,3},{5,4},{6,5},{7,6},{9,8},{10,9},{11,10},{12... | collective-permute-start | bytes 1179656 | tf_op jit(solution)/shard_map/ppermute | solution.py:331
  8.5 16.8 %collective-permute-start.6 = (bf16[4,6,16,128]{3,2,1,0:T(8,128)(2,1)S(1)}, bf16[4,6,16,128]{3,2,1,0:T(8,128)(2,1)S(1)}, u32[]{:S(2)}, u32[]{:S(2)}) collective-permute-start(bf16[4,6,16,128]{3,2,1,0:T(8,128)(2,1)S(1)} %get-tuple-element.31), channel_id=1, source_target_pairs={{136,128},{137,129},{138,130},{139,131},{140,132},{141,133},{142,1... | collective-permute-start | bytes 294920 | tf_op jit(solution)/shard_map/ppermute | solution.py:331
  16.6 11.6 %collective-permute-start.5 = (bf16[4,6,16,128]{3,2,1,0:T(8,128)(2,1)S(1)}, bf16[4,6,16,128]{3,2,1,0:T(8,128)(2,1)S(1)}, u32[]{:S(2)}, u32[]{:S(2)}) collective-permute-start(bf16[4,6,16,128]{3,2,1,0:T(8,128)(2,1)S(1)} %get-tuple-element.32), channel_id=1, source_target_pairs={{128,136},{129,137},{130,138},{131,139},{132,140},{133,141},{134,1... | collective-permute-start | bytes 294920 | tf_op jit(solution)/shard_map/ppermute | solution.py:331
  24.6 15.3 %collective-permute-start.4 = (bf16[2,28,28,128]{3,2,1,0:T(8,128)(2,1)S(1)}, bf16[2,28,28,128]{3,2,1,0:T(8,128)(2,1)S(1)}, u32[]{:S(2)}, u32[]{:S(2)}) collective-permute-start(bf16[2,28,28,128]{3,2,1,0:T(8,128)(2,1)S(1)} %get-tuple-element.19), channel_id=1, source_target_pairs={{0,128},{1,129},{2,130},{3,131},{4,132},{5,133},{6,134},{7,135},{8... | collective-permute-start | bytes 1204232 | tf_op jit(solution)/shard_map/ppermute | solution.py:331
  28.3 7.3 %collective-permute-start.7 = (bf16[4,28,6,128]{3,2,1,0:T(8,128)(2,1)S(1)}, bf16[4,28,6,128]{3,2,1,0:T(8,128)(2,1)S(1)}, u32[]{:S(2)}, u32[]{:S(2)}) collective-permute-start(bf16[4,28,6,128]{3,2,1,0:T(8,128)(2,1)S(1)} %pad_maximum_fusion.2), channel_id=1, source_target_pairs={{128,129},{129,130},{130,131},{131,132},{132,133},{133,134},{134,1... | collective-permute-start | bytes 516104 | tf_op jit(solution)/shard_map/ppermute | solution.py:331
  30.3 7.2 %collective-permute-start.8 = (bf16[4,28,6,128]{3,2,1,0:T(8,128)(2,1)S(1)}, bf16[4,28,6,128]{3,2,1,0:T(8,128)(2,1)S(1)}, u32[]{:S(2)}, u32[]{:S(2)}) collective-permute-start(bf16[4,28,6,128]{3,2,1,0:T(8,128)(2,1)S(1)} %pad_maximum_fusion.3), channel_id=1, source_target_pairs={{129,128},{130,129},{131,130},{132,131},{133,132},{134,133},{135,1... | collective-permute-start | bytes 516104 | tf_op jit(solution)/shard_map/ppermute | solution.py:331
  44.5 0.9 %collective-permute-start.9 = (bf16[2,24,24,128]{3,2,1,0:T(8,128)(2,1)S(1)}, bf16[2,24,24,128]{3,2,1,0:T(8,128)(2,1)S(1)}, u32[]{:S(2)}, u32[]{:S(2)}) collective-permute-start(bf16[2,24,24,128]{3,2,1,0:T(8,128)(2,1)S(1)} %get-tuple-element.25), channel_id=1, source_target_pairs={{128,256},{129,257},{130,258},{131,259},{132,260},{133,261},{134,2... | collective-permute-start | bytes 884744 | tf_op jit(solution)/shard_map/ppermute | solution.py:331
  48.9 30.3 %collective-permute-start.10 = (bf16[2,20,20,128]{3,2,1,0:T(8,128)(2,1)S(1)}, bf16[2,20,20,128]{3,2,1,0:T(8,128)(2,1)S(1)}, u32[]{:S(2)}, u32[]{:S(2)}) collective-permute-start(bf16[2,20,20,128]{3,2,1,0:T(8,128)(2,1)S(1)} %get-tuple-element.27), channel_id=1, source_target_pairs={{256,384},{257,385},{258,386},{259,387},{260,388},{261,389},{262,3... | collective-permute-start | bytes 614408 | tf_op jit(solution)/shard_map/ppermute | solution.py:331

commit v2 on v1

v2 whole, which is shorter than its diff:
```python
import functools

import jax
import jax.numpy as jnp
from jax import lax
from jax.experimental import pallas as pl
from jax.experimental.pallas import tpu as pltpu
from jax.sharding import PartitionSpec as P

PITCH = 32
CHUNK = 8
AXES = ("segment", "row", "col")


def norm_act(values, half_gain, mask):
    scale = lax.rsqrt(jnp.mean(values * values, axis=-1, keepdims=True) + 1e-06)
    half = values * scale * half_gain
    return (half + half * jnp.tanh(half)) * mask


def chunks(rows):
    return [(first, min(CHUNK, rows - first)) for first in range(0, rows, CHUNK)]


def column_mask(side, width, channels):
    col = lax.broadcasted_iota(jnp.int32, (PITCH, channels), 0) + side
    return jnp.where((col >= 0) & (col < width), 1.0, 0.0)


def cell_mask(columns, top, height, first, count):
    parts = []
    for row in range(first, first + count):
        here = top + row
        parts.append(columns * jnp.where((here >= 0) & (here < height), 1.0, 0.0))
    return jnp.concatenate(parts, axis=0)


def spread(source, start, patches, block, rows):
    channels = source.shape[-1]
    for tap in range(3):
        lane = (block * 3 + tap) * channels
        begin = start + tap
        patches[: rows * PITCH, lane : lane + channels] = source[
            begin : begin + rows * PITCH, :
        ].astype(jnp.bfloat16)


def weight_rows(kernel, tap, sides):
    empty = jnp.zeros(kernel.shape[2:], jnp.bfloat16)

    def column(taps):
        parts = [empty if t is None else kernel[t, tap] for t in taps]
        return parts[0] if len(parts) == 1 else jnp.concatenate(parts, axis=0)

    columns = [column(taps) for taps in sides]
    return columns[0] if len(columns) == 1 else jnp.concatenate(columns, axis=1)


HELD = ((0, 1), (None, 0))
OPENING = ((0, 1, 2), (None, 0, 1))
EARLY = ((2,), (1,))
LATE = ((2,),)


def convolve(patches, kernel, sides, total, first, rows):
    count = rows * PITCH
    for tap in range(3):
        begin = (first + tap) * PITCH
        total = total + jnp.dot(
            patches[begin : begin + count, :],
            weight_rows(kernel, tap, sides),
            preferred_element_type=jnp.float32,
        )
    return total


def bias_of(bias, count):
    return jnp.broadcast_to(
        jnp.concatenate([bias, bias], axis=1), (count, 2 * bias.shape[-1])
    )


def assemble(grid, source, mid, low, high, left, right):
    reach = low.shape[1]
    tile = mid.shape[1]
    for row in range(tile + 2 * reach):
        begin = row * PITCH
        if row < reach:
            body = low[source, row]
        elif row < reach + tile:
            body = mid[source, row - reach]
        else:
            body = high[source, row - reach - tile]
        grid[begin : begin + reach, :] = left[source, row].astype(jnp.float32)
        grid[begin + reach : begin + reach + tile, :] = body.astype(jnp.float32)
        grid[begin + reach + tile : begin + 2 * reach + tile, :] = right[
            source, row
        ].astype(jnp.float32)


def normed(place, margin, height, width, values_of, gain, flat, rows, span):
    channels = gain.shape[-1]
    tile = span - 2 * margin
    top = place[0] * tile - margin
    columns = column_mask(place[1] * tile - margin, width, channels)
    half_gain = 0.5 * gain
    for first, count in chunks(rows):
        keep = cell_mask(columns, top, height, first, count)
        flat[first * PITCH : (first + count) * PITCH, :] = norm_act(
            values_of(first, count), half_gain, keep
        )


def body(place, halo, height, width, g_ref, held, flat, patches, fill, hidden_of, branch_of, o_ref):
    span = o_ref.shape[0] + 4
    blocks = patches.shape[1] // (3 * held.shape[-1])

    def area(ref, first, count):
        return ref[first * PITCH : (first + count) * PITCH, :]

    normed(
        place, halo, height, width, lambda first, count: area(held, first, count),
        g_ref[0:1, :], flat, span, span,
    )
    fill(0)
    spread(flat, 0, patches, blocks - 1, span)
    normed(
        place, halo - 1, height, width, hidden_of, g_ref[1:2, :], flat, span - 2, span - 2
    )
    fill(1)
    spread(flat, 0, patches, blocks - 1, span - 2)
    for first, count in chunks(span - 4):
        offset = (first + 2) * PITCH + 2
        out = held[offset : offset + count * PITCH, :] + branch_of(first, count)
        for row in range(count):
            o_ref[first + row] = out[row * PITCH : row * PITCH + span - 4].astype(
                jnp.bfloat16
            )


def split_off(part):
    def apply(total, first, count):
        channels = part.shape[-1]
        part[first * PITCH : (first + count) * PITCH, :] = total[:, channels:]
        return total[:, :channels]

    return apply


def only_at(kernel, step):
    def run(place, *refs):
        @pl.when(place[2] == step)
        def _():
            kernel(place, *refs)

    return run


def keep_tile(o_ref, r_ref):
    tile = r_ref.shape[0]
    edge = (o_ref.shape[0] - tile) // 2
    r_ref[...] = o_ref[edge : edge + tile, edge : edge + tile, :]


def pass_on(place, step, p_ref, r_ref):
    @pl.when(place[2] != step)
    def _():
        r_ref[...] = p_ref[...]


def opening_kernel(
    halo, height, width, place, mid, low, high, left, right, w_ref, b_ref, g_ref,
    o_ref, r_ref, one_ref, two_ref, grid, flat, patches,
):
    for slot, source in enumerate((0, 2, 3, 4, 5)):
        assemble(grid.at[slot], source, mid, low, high, left, right)
    span = mid.shape[1] + 2 * halo

    def fill(conv):
        for frame in range(2):
            spread(
                grid.at[1 + 2 * conv + frame], conv * (PITCH + 1), patches, frame,
                span - 2 * conv,
            )

    def conv_of(conv, part):
        def run(first, count):
            bias = bias_of(b_ref[conv : conv + 1, :], count * PITCH)
            total = convolve(patches, w_ref.at[conv], OPENING, bias, first, count)
            return split_off(part)(total, first, count)

        return run

    body(
        place, halo, height, width, g_ref, grid.at[0], flat, patches, fill,
        conv_of(0, one_ref), conv_of(1, two_ref), o_ref,
    )
    keep_tile(o_ref, r_ref)


def nothing(conv):
    del conv


def late_of(patches, w_ref, conv, part):
    def run(first, count):
        known = part[first * PITCH : (first + count) * PITCH, :]
        return convolve(patches, w_ref.at[conv], LATE, known, first, count)

    return run


def opening_late_kernel(
    halo, height, width, place, mid, low, high, left, right, w_ref, g_ref,
    one_ref, two_ref, o_ref, r_ref, held, flat, patches,
):
    assemble(held, 1, mid, low, high, left, right)
    body(
        place, halo, height, width, g_ref, held, flat, patches, nothing,
        late_of(patches, w_ref, 0, one_ref), late_of(patches, w_ref, 1, two_ref), o_ref,
    )
    keep_tile(o_ref, r_ref)


def held_kernel(
    place, cached, low, high, left, right, w_ref, b_ref, one_ref, two_ref, grid, patches
):
    @pl.when(place[2] != 0)
    def _():
        add_held(
            cached, low, high, left, right, w_ref, b_ref, one_ref, two_ref, grid, patches
        )


def add_held(
    cached, low, high, left, right, w_ref, b_ref, one_ref, two_ref, grid, patches
):
    span = cached.shape[1] + 2 * low.shape[1]
    for frame in range(4):
        assemble(grid.at[frame], frame, cached, low, high, left, right)
    for conv, out in ((0, one_ref), (1, two_ref)):
        start = conv * (PITCH + 1)
        rows = span - 2 * conv
        for frame in range(2):
            spread(grid.at[2 * conv + frame], start, patches, frame, rows)
        for first, count in chunks(rows - 2):
            out[first * PITCH : (first + count) * PITCH, :] = convolve(
                patches, w_ref.at[conv], HELD,
                bias_of(b_ref[conv : conv + 1, :], count * PITCH), first, count,
            )


def load_rows(x_ref, held):
    span = x_ref.shape[0]
    for row in range(span):
        held[row * PITCH : row * PITCH + span, :] = x_ref[row].astype(jnp.float32)


def early_kernel(
    halo, drop, height, width, place, x_ref, known_one, known_two, w_ref, g_ref, p_ref,
    o_ref, r_ref, one_ref, two_ref, held, flat, patches,
):
    load_rows(x_ref, held)

    def conv_of(conv, known, part):
        def run(first, count):
            begin = drop * (PITCH + 1) + first * PITCH
            total = convolve(
                patches, w_ref.at[conv], EARLY, known[begin : begin + count * PITCH, :],
                first, count,
            )
            return split_off(part)(total, first, count)

        return run

    body(
        place, halo, height, width, g_ref, held, flat, patches, nothing,
        conv_of(0, known_one, one_ref), conv_of(1, known_two, two_ref), o_ref,
    )
    keep_tile(o_ref, r_ref)


def late_kernel(
    halo, height, width, place, x_ref, one_ref, two_ref, w_ref, g_ref, p_ref,
    o_ref, r_ref, held, flat, patches,
):
    load_rows(x_ref, held)
    body(
        place, halo, height, width, g_ref, held, flat, patches, nothing,
        late_of(patches, w_ref, 0, one_ref), late_of(patches, w_ref, 1, two_ref), o_ref,
    )
    keep_tile(o_ref, r_ref)


def last_kernel(
    halo, height, width, place, x_ref, one_ref, two_ref, w_ref, g_ref, p_ref, q_ref,
    r_ref, o_ref, held, flat, patches,
):
    late_kernel(
        halo, height, width, place, x_ref, one_ref, two_ref, w_ref, g_ref, p_ref,
        o_ref, r_ref.at[1], held, flat, patches,
    )


def own_or_passed(kernel, step, former, current, place, *refs):
    only_at(kernel, step)(place, *refs)
    pass_on(place, step, refs[former], refs[current])


def last_or_passed(kernel, step, former, current, place, *refs):
    refs[current][0] = refs[former + 1][...]
    only_at(kernel, step)(place, *refs)
    pass_on(place, step, refs[former], refs[current].at[1])


def pack_kernel(frames, cached, mid, low, high, sems):
    reach = low.shape[1]
    tile = frames.shape[1]
    copies = []
    for out, begin, rows in ((low, tile - reach, reach), (high, 0, reach), (mid, 0, tile)):
        for part, offset in ((frames, 0), (cached, 2)):
            copies.append(
                pltpu.make_async_copy(
                    part.at[:, pl.ds(begin, rows)],
                    out.at[pl.ds(offset, part.shape[0])],
                    sems.at[len(copies)],
                )
            )
    for copy in copies:
        copy.start()
    for copy in copies:
        copy.wait()


def sides_kernel(mid, low, high, left, right):
    reach = low.shape[1]
    tile = mid.shape[1]
    for out, begin in ((left, tile - reach), (right, 0)):
        cut = slice(begin, begin + reach)
        out[:, :reach] = low[:, :, cut, :]
        out[:, reach : reach + tile] = mid[:, :, cut, :]
        out[:, reach + tile :] = high[:, :, cut, :]


SCALARS = pl.BlockSpec(memory_space=pltpu.SMEM)
WHOLE = pl.BlockSpec(memory_space=pltpu.VMEM)


def shaped(*shape, dtype=jnp.bfloat16):
    return jax.ShapeDtypeStruct(shape, dtype)


def launch(kernel, arguments, outs, scratch, span, frames):
    channels = arguments[1].shape[-1]
    return pl.pallas_call(
        kernel,
        out_shape=outs,
        in_specs=[SCALARS] + [WHOLE] * (len(arguments) - 1),
        out_specs=[WHOLE] * len(outs),
        scratch_shapes=scratch,
        cost_estimate=pl.CostEstimate(
            flops=4 * 9 * frames * span * PITCH * channels * 2 * channels,
            bytes_accessed=2 << 20,
            transcendentals=0,
        ),
        compiler_params=pltpu.CompilerParams(vmem_limit_bytes=40 << 20),
    )(*arguments)


def room(span):
    return (span + 3) * PITCH


def scratches(span, frames, blocks, channels):
    grid = (room(span), channels)
    return [
        pltpu.VMEM(grid if frames == 1 else (frames,) + grid, jnp.float32),
        pltpu.VMEM(grid, jnp.float32),
        pltpu.VMEM((room(span), blocks * 3 * channels), jnp.bfloat16),
    ]


def parts_of(span, lanes):
    return [
        shaped((span - 2) * PITCH, lanes, dtype=jnp.float32),
        shaped((span - 4) * PITCH, lanes, dtype=jnp.float32),
    ]


def packed(frames, cached, halo):
    tile = (6,) + frames.shape[1:]
    shape = (6, halo) + frames.shape[2:]
    return pl.pallas_call(
        pack_kernel,
        out_shape=[shaped(*tile), shaped(*shape), shaped(*shape)],
        in_specs=[pl.BlockSpec(memory_space=pltpu.HBM)] * 2,
        out_specs=[WHOLE] * 3,
        scratch_shapes=[pltpu.SemaphoreType.DMA((6,))],
        compiler_params=pltpu.CompilerParams(vmem_limit_bytes=4 << 20),
    )(frames, cached)


def cut_sides(mid, low, high):
    halo = low.shape[1]
    tile, channels = mid.shape[1], mid.shape[-1]
    return pl.pallas_call(
        sides_kernel,
        out_shape=[shaped(6, tile + 2 * halo, halo, channels)] * 2,
        in_specs=[WHOLE] * 3,
        out_specs=[WHOLE] * 2,
        compiler_params=pltpu.CompilerParams(vmem_limit_bytes=8 << 20),
    )(mid, low, high)


def moved(value, segments, shift):
    sizes = [lax.axis_size(axis) for axis in AXES]
    pairs = []
    for segment in segments:
        for row in range(sizes[1]):
            for col in range(sizes[2]):
                target = (segment + shift[0], row + shift[1], col + shift[2])
                if all(0 <= t < n for t, n in zip(target, sizes)):
                    source = (segment * sizes[1] + row) * sizes[2] + col
                    place = (target[0] * sizes[1] + target[1]) * sizes[2] + target[2]
                    pairs.append((source, place))
    return lax.ppermute(value, AXES, pairs)


def ends(parts, cut):
    taken = [cut(part) for part in parts]
    return taken[0] if len(taken) == 1 else jnp.concatenate(taken, axis=0)


def rows_of(parts, segments, halo):
    low = moved(
        ends(parts, lambda part: part[:, part.shape[1] - halo :]), segments, (0, 1, 0)
    )
    high = moved(ends(parts, lambda part: part[:, :halo]), segments, (0, -1, 0))
    return low, high


def sides_of(parts, low, high, halo):
    def side(cut):
        return jnp.concatenate([cut(low), ends(parts, cut), cut(high)], axis=1)

    return side(lambda part: part[:, :, part.shape[2] - halo :]), side(
        lambda part: part[:, :, :halo]
    )


def columns_of(left, right, segments):
    return moved(left, segments, (0, 0, 1)), moved(right, segments, (0, 0, -1))


def on_device(height, width, frames, caches, weights, biases, gains):
    sections = lax.axis_size("segment")
    place = jnp.stack(
        [lax.axis_index("row"), lax.axis_index("col"), lax.axis_index("segment")]
    ).astype(jnp.int32)
    tile, channels = frames.shape[1], frames.shape[-1]
    kernels = weights[0].reshape((2, 3, 3, 3 * channels, channels))
    bias, gain = biases[0], gains[0]
    cached = caches[0].reshape((4,) + frames.shape[1:])
    halo = 2 * sections
    reach = halo - 2
    others = list(range(1, sections))
    mid, low, high = packed(frames, cached, halo)
    low, high = moved(low, [0], (0, 1, 0)), moved(high, [0], (0, -1, 0))
    left, right = cut_sides(mid, low, high)
    left, right = columns_of(left, right, [0])
    left, later = lax.optimization_barrier((left, cached))
    pieces = (mid, low, high, left, right)
    low, high = rows_of([later], others, reach)
    left, right = sides_of([later], low, high, reach)
    ahead = (low, high) + columns_of(left, right, others)

    span = tile + 2 * halo
    owned = shaped(tile, tile, channels)
    onward = shaped(span - 4, span - 4, channels)
    sent, result, one, two = launch(
        only_at(functools.partial(opening_kernel, halo, height, width), 0),
        (place,) + pieces + (kernels, bias, gain),
        [onward, owned] + parts_of(span, channels),
        scratches(span, 5, 3, channels), span, 3,
    )
    received = moved(sent, [0], (1, 0, 0))
    sent, result_late = launch(
        only_at(functools.partial(opening_late_kernel, halo, height, width), 0),
        (place,) + pieces + (kernels, gain, one, two),
        [onward, owned],
        scratches(span, 1, 1, channels), span, 1,
    )
    sent, cached = lax.optimization_barrier((sent, cached))
    received_late = moved(sent, [0], (1, 0, 0))
    span = tile + 2 * reach
    known = launch(
        held_kernel,
        (place, cached) + ahead + (kernels, bias),
        parts_of(span, 2 * channels),
        [
            pltpu.VMEM((4, room(span), channels), jnp.float32),
            pltpu.VMEM((room(span), 6 * channels), jnp.bfloat16),
        ],
        span, 2,
    )
    halo = reach
    for step in others:
        span = tile + 2 * halo
        onward = shaped(span - 4, span - 4, channels)
        sent, result, one, two = launch(
            functools.partial(
                own_or_passed,
                functools.partial(early_kernel, halo, reach - halo, height, width),
                step, 5, 7,
            ),
            (place, received, *known, kernels, gain, result),
            [onward, owned] + parts_of(span, channels),
            scratches(span, 1, 1, channels), span, 1,
        )
        if step + 1 < sections:
            received = moved(sent, [step], (1, 0, 0))
            sent, result_late = launch(
                functools.partial(
                    own_or_passed,
                    functools.partial(late_kernel, halo, height, width),
                    step, 5, 7,
                ),
                (place, received_late, one, two, kernels, gain, result_late),
                [onward, owned],
                scratches(span, 1, 1, channels), span, 1,
            )
            received_late = moved(sent, [step], (1, 0, 0))
        else:
            (result,) = launch(
                functools.partial(
                    last_or_passed,
                    functools.partial(last_kernel, halo, height, width),
                    step, 5, 7,
                ),
                (place, received_late, one, two, kernels, gain, result_late, result),
                [shaped(2, tile, tile, channels)],
                [pltpu.VMEM(onward.shape, jnp.bfloat16)] + scratches(span, 1, 1, channels),
                span, 1,
            )
        halo = halo - 2
    return result[None]


def solution(mesh):
    height = 16 * mesh.shape["row"]
    width = 16 * mesh.shape["col"]
    in_specs = (
        P(None, "row", "col", None),
        P("segment", None, None, "row", "col", None),
        P("segment", None, None, None, None, None, None),
        P("segment", None, None),
        P("segment", None, None),
    )
    out_specs = P("segment", None, "row", "col", None)
    return jax.shard_map(
        functools.partial(on_device, height, width),
        mesh=mesh, in_specs=in_specs, out_specs=out_specs, check_vma=False,
    )
```

time: 83.2 us -> 73.4 us (0.88)
  the two profiles are of different devices: /device:TPU:204 before, /device:TPU:194 now
where the time goes in v2:
time: 73.4 us; the launch traced here: 73 us
  waiting for transfers between devices  32.2 us (44%)
  starting transfers between devices  23.7 us (32%)
  Pallas kernels  12.7 us (17%)
  local copies, waits for them, and re-layouts  4.02 us (5%)
    ppermute x14, waiting for transfers between devices, moved(): return lax.ppermute(value, AXES, pairs)  32.2 us
    ppermute x14, starting transfers between devices, moved(): return lax.ppermute(value, AXES, pairs)  23.7 us
    pallas_call x9, Pallas kernels, launch(): pl.pallas_call(kernel, out_shape=outs, in_specs=[SCALARS] + [WHOLE] * (le...  11.4 us
    unnamed x12, local copies, waits for them, and re-layouts  2 us
  transfers between devices with their start and end apart: 14, of which 3 were waited for; matrix products, arithmetic and copies ran while one was open for 3% of the time, Pallas kernels for 12%

profile of v2, /device:TPU:194, one launch (start us, length us, event | category | flops | bytes accessed | tf_op | source)
XLA Modules:
  0.0 73.0 jit_solution(13791268954247358208)
XLA Ops:
  0.0 1.1 %copy-done.1 = bf16[1,2,2,16,16,128]{5,4,3,2,1,0:T(8,128)(2,1)S(1)} copy-done((bf16[1,2,2,16,16,128]{5,4,3,2,1,0:T(8,128)(2,1)S(1)}, bf16[1,2,2,16,16,128]{5,4,3,2,1,0:T(8,128)(2,1)}, u32[]{:S(2)}) %copy-start.1) | copy-done | bytes 262168
  1.1 0.9 %copy-done.3 = bf16[2,16,16,128]{3,2,1,0:T(8,128)(2,1)S(1)} copy-done((bf16[2,16,16,128]{3,2,1,0:T(8,128)(2,1)S(1)}, bf16[2,16,16,128]{3,2,1,0:T(8,128)(2,1)}, u32[]{:S(2)}) %copy-start.3) | copy-done | bytes 131096
  2.0 0.4 shard_map.55
  2.4 0.7 collective-permute-start
  3.1 0.7 collective-permute-start.1
  3.8 0.0 collective-permute-done.low.refs_1_
  3.8 0.0 collective-permute-done.1.high.refs_2_
  3.8 0.9 %shard_map.56 = (bf16[6,32,8,128]{3,2,1,0:T(8,128)(2,1)}, bf16[6,32,8,128]{3,2,1,0:T(8,128)(2,1)S(1)}) custom-call(bf16[6,16,16,128]{3,2,1,0:T(8,128)(2,1)S(1)} %get-tuple-element.37.mid.refs_0_, bf16[6,8,16,128]{3,2,1,0:T(8,128)(2,1)S(1)} %collective-permute-done.low.refs_1_, bf16[6,8,16,128]{3,2,1,0:T(8,128)(2,1)S(1)} %collective-permute-done.1.high.refs_2_), custom_call_target="tpu_custom_call" | custom-call | tf_op jit(solution)/shard_map/pallas_call | solution.py:406
  4.7 0.7 collective-permute-start.2
  5.4 0.1 pad_add_fusion.place
  5.4 0.7 collective-permute-start.3
  6.1 0.0 collective-permute-done.2.refs_3_
  6.1 1.0 %fusion.1 = (bf16[4,6,16,128]{3,2,1,0:T(8,128)(2,1)S(1)}, bf16[4,6,16,128]{3,2,1,0:T(8,128)(2,1)S(1)}) fusion(bf16[4,16,16,128]{3,2,1,0:T(8,128)(2,1)} %bitcast.17), kind=kLoop, calls=%fused_computation.4 | loop fusion | bytes 393216 | tf_op jit(solution)/shard_map/slice | solution.py:438
  7.1 1.3 %collective-permute-start.7 = (bf16[4,6,16,128]{3,2,1,0:T(8,128)(2,1)S(1)}, bf16[4,6,16,128]{3,2,1,0:T(8,128)(2,1)S(1)}, u32[]{:S(2)}, u32[]{:S(2)}) collective-permute-start(bf16[4,6,16,128]{3,2,1,0:T(8,128)(2,1)S(1)} %get-tuple-element.71), channel_id=1, source_target_pairs={{136,128},{137,129},{138,130},{139,131},{140,132},{141,133},{142,1... | collective-permute-start | bytes 294920 | tf_op jit(solution)/shard_map/ppermute | solution.py:426
  8.4 1.0 %fusion = (bf16[4,16,6,128]{3,2,1,0:T(8,128)(2,1)S(1)}, bf16[4,16,6,128]{3,2,1,0:T(8,128)(2,1)S(1)}) fusion(bf16[4,16,16,128]{3,2,1,0:T(8,128)(2,1)} %bitcast.18), kind=kLoop, calls=%fused_computation.3 | loop fusion | bytes 393216 | tf_op jit(solution)/shard_map/slice | solution.py:447
  9.4 8.8 %collective-permute-start.6 = (bf16[4,6,16,128]{3,2,1,0:T(8,128)(2,1)S(1)}, bf16[4,6,16,128]{3,2,1,0:T(8,128)(2,1)S(1)}, u32[]{:S(2)}, u32[]{:S(2)}) collective-permute-start(bf16[4,6,16,128]{3,2,1,0:T(8,128)(2,1)S(1)} %get-tuple-element.72), channel_id=1, source_target_pairs={{128,136},{129,137},{130,138},{131,139},{132,140},{133,141},{134,1... | collective-permute-start | bytes 294920 | tf_op jit(solution)/shard_map/ppermute | solution.py:426
  18.3 0.0 collective-permute-done.7.high
  18.3 2.4 %collective-permute-done.6.low = bf16[4,6,16,128]{3,2,1,0:T(8,128)(2,1)S(1)} collective-permute-done((bf16[4,6,16,128]{3,2,1,0:T(8,128)(2,1)S(1)}, bf16[4,6,16,128]{3,2,1,0:T(8,128)(2,1)S(1)}, u32[]{:S(2)}, u32[]{:S(2)}) %collective-permute-start.6) | collective-permute-done | bytes 98336 | tf_op jit(solution)/shard_map/ppermute | solution.py:426
  20.7 0.1 pad_maximum_fusion
  20.8 1.9 %collective-permute-start.8 = (bf16[4,28,6,128]{3,2,1,0:T(8,128)(2,1)S(1)}, bf16[4,28,6,128]{3,2,1,0:T(8,128)(2,1)S(1)}, u32[]{:S(2)}, u32[]{:S(2)}) collective-permute-start(bf16[4,28,6,128]{3,2,1,0:T(8,128)(2,1)S(1)} %pad_maximum_fusion), channel_id=1, source_target_pairs={{128,129},{129,130},{130,131},{131,132},{132,133},{133,134},{134,1... | collective-permute-start | bytes 516104 | tf_op jit(solution)/shard_map/ppermute | solution.py:426
  22.7 0.1 pad_maximum_fusion.1
  22.8 3.6 %collective-permute-start.9 = (bf16[4,28,6,128]{3,2,1,0:T(8,128)(2,1)S(1)}, bf16[4,28,6,128]{3,2,1,0:T(8,128)(2,1)S(1)}, u32[]{:S(2)}, u32[]{:S(2)}) collective-permute-start(bf16[4,28,6,128]{3,2,1,0:T(8,128)(2,1)S(1)} %pad_maximum_fusion.1), channel_id=1, source_target_pairs={{129,128},{130,129},{131,130},{132,131},{133,132},{134,133},{135,1... | collective-permute-start | bytes 516104 | tf_op jit(solution)/shard_map/ppermute | solution.py:426
  26.4 0.0 collective-permute-done.3.refs_4_
  26.5 0.6 shard_map.57
  27.0 0.7 collective-permute-start.5
  27.7 0.0 copy-start.2
  27.7 0.6 shard_map.58
  28.3 0.7 collective-permute-start.4
  29.0 0.0 collective-permute-done.8.left
  29.0 1.0 %collective-permute-done.9.right = bf16[4,28,6,128]{3,2,1,0:T(8,128)(2,1)S(1)} collective-permute-done((bf16[4,28,6,128]{3,2,1,0:T(8,128)(2,1)S(1)}, bf16[4,28,6,128]{3,2,1,0:T(8,128)(2,1)S(1)}, u32[]{:S(2)}, u32[]{:S(2)}) %collective-permute-start.9) | collective-permute-done | bytes 172064 | tf_op jit(solution)/shard_map/ppermute | solution.py:426
  30.0 0.0 copy-done.2
  30.0 2.9 %shard_map.59 = (f32[832,256]{1,0:T(8,128)S(1)}, f32[768,256]{1,0:T(8,128)S(1)}) custom-call(s32[3]{0:T(128)S(1)} %pad_add_fusion.place, bf16[4,16,16,128]{3,2,1,0:T(8,128)(2,1)S(1)} %bitcast.20, bf16[4,6,16,128]{3,2,1,0:T(8,128)(2,1)S(1)} %collective-permute-done.6.low, bf16[4,6,16,128]{3,2,1,0:T(8,128)(2,1)S(1)} %collective-permute-done.7.high, ...), custom_call_target="tpu_custom_call" | custom-call | flops 2113929216 | bytes 2097152 | tf_op jit(solution)/shard_map/pallas_call | solution.py:355
  32.9 0.0 collective-permute-done.5.refs_0_
  32.9 0.6 shard_map.60
  33.5 0.7 collective-permute-start.11
  34.2 0.0 collective-permute-done.4.refs_0_
  34.2 0.6 shard_map.61
  34.7 0.7 collective-permute-start.10
  35.4 0.0 collective-permute-done.11.refs_0_
  35.4 0.7 %shard_map.62 = (bf16[20,20,128]{2,1,0:T(8,128)(2,1)S(1)}, bf16[16,16,128]{2,1,0:T(8,128)(2,1)S(1)}, f32[704,128]{1,0:T(8,128)S(1)}, f32[640,128]{1,0:T(8,128)S(1)}) custom-call(s32[3]{0:T(128)S(1)} %pad_add_fusion.place, bf16[24,24,128]{2,1,0:T(8,128)(2,1)S(1)} %collective-permute-done.11.refs_0_, f32[832,256]{1,0:T(8,128)S(1)} %get-tuple-element.50.refs_1_, ...), custom_call_target="tpu_custom_call" | custom-call | flops 905969664 | bytes 2097152 | tf_op jit(solution)/shard_map/pallas_call | solution.py:355
  36.2 1.3 %collective-permute-start.13 = (bf16[20,20,128]{2,1,0:T(8,128)(2,1)S(1)}, bf16[20,20,128]{2,1,0:T(8,128)(2,1)S(1)}, u32[]{:S(2)}, u32[]{:S(2)}) collective-permute-start(bf16[20,20,128]{2,1,0:T(8,128)(2,1)S(1)} %get-tuple-element.63), channel_id=1, source_target_pairs={{256,384},{257,385},{258,386},{259,387},{260,388},{261,389},{262,3... | collective-permute-start | bytes 307208 | tf_op jit(solution)/shard_map/ppermute | solution.py:426
  37.5 0.0 collective-permute-done.10.refs_0_
  37.5 0.6 shard_map.63
  38.1 1.3 %collective-permute-start.12 = (bf16[20,20,128]{2,1,0:T(8,128)(2,1)S(1)}, bf16[20,20,128]{2,1,0:T(8,128)(2,1)S(1)}, u32[]{:S(2)}, u32[]{:S(2)}) collective-permute-start(bf16[20,20,128]{2,1,0:T(8,128)(2,1)S(1)} %get-tuple-element.62), channel_id=1, source_target_pairs={{256,384},{257,385},{258,386},{259,387},{260,388},{261,389},{262,3... | collective-permute-start | bytes 307208 | tf_op jit(solution)/shard_map/ppermute | solution.py:426
  39.4 28.8 %collective-permute-done.13.refs_0_ = bf16[20,20,128]{2,1,0:T(8,128)(2,1)S(1)} collective-permute-done((bf16[20,20,128]{2,1,0:T(8,128)(2,1)S(1)}, bf16[20,20,128]{2,1,0:T(8,128)(2,1)S(1)}, u32[]{:S(2)}, u32[]{:S(2)}) %collective-permute-start.13) | collective-permute-done | bytes 102432 | tf_op jit(solution)/shard_map/ppermute | solution.py:426
  68.1 2.5 %shard_map.64 = (bf16[16,16,128]{2,1,0:T(8,128)(2,1)}, bf16[16,16,128]{2,1,0:T(8,128)(2,1)S(1)}, f32[576,128]{1,0:T(8,128)S(1)}, f32[512,128]{1,0:T(8,128)S(1)}) custom-call(s32[3]{0:T(128)S(1)} %pad_add_fusion.place, bf16[20,20,128]{2,1,0:T(8,128)(2,1)S(1)} %collective-permute-done.13.refs_0_, f32[832,256]{1,0:T(8,128)S(1)} %get-tuple-element.50.refs_1_, ...), custom_call_target="tpu_custom_call" | custom-call | flops 754974720 | bytes 2097152 | tf_op jit(solution)/shard_map/pallas_call | solution.py:355
  70.7 0.0 collective-permute-done.12.refs_0_
  70.7 2.4 %shard_map.65 = bf16[2,16,16,128]{3,2,1,0:T(8,128)(2,1)} custom-call(s32[3]{0:T(128)S(1)} %pad_add_fusion.place, bf16[20,20,128]{2,1,0:T(8,128)(2,1)S(1)} %collective-permute-done.12.refs_0_, f32[576,128]{1,0:T(8,128)S(1)} %get-tuple-element.65.refs_1_, f32[512,128]{1,0:T(8,128)S(1)} %get-tuple-element.66.refs_2_, bf16[2,3,3,384,128]{4,3,2,1,0:T(8,128)(2,1)S(1)} %bitcast.16, ...), custom_call_target="tpu_custom_call" | custom-call | flops 754974720 | bytes 2097152 | tf_op jit(solution)/shard_map/pallas_call | solution.py:355
  (10 shorter events, 0.1 us)
Async XLA Ops:
  0.0 26.5 %copy-start = (bf16[1,2,3,3,3,128,128]{6,5,4,3,2,1,0:T(8,128)(2,1)S(1)}, bf16[1,2,3,3,3,128,128]{6,5,4,3,2,1,0:T(8,128)(2,1)}, u32[]{:S(2)}) copy-start(bf16[1,2,3,3,3,128,128]{6,5,4,3,2,1,0:T(8,128)(2,1)} %param.7) | copy-start | bytes 5308420
  0.0 1.1 %copy-start.1 = (bf16[1,2,2,16,16,128]{5,4,3,2,1,0:T(8,128)(2,1)S(1)}, bf16[1,2,2,16,16,128]{5,4,3,2,1,0:T(8,128)(2,1)}, u32[]{:S(2)}) copy-start(bf16[1,2,2,16,16,128]{5,4,3,2,1,0:T(8,128)(2,1)} %param.6) | copy-start | bytes 786436
  1.1 0.9 %copy-start.3 = (bf16[2,16,16,128]{3,2,1,0:T(8,128)(2,1)S(1)}, bf16[2,16,16,128]{3,2,1,0:T(8,128)(2,1)}, u32[]{:S(2)}) copy-start(bf16[2,16,16,128]{3,2,1,0:T(8,128)(2,1)} %frames.1) | copy-start | bytes 393220
  2.0 24.5 %copy-start.4 = (f32[1,2,128]{2,1,0:T(2,128)S(1)}, f32[1,2,128]{2,1,0:T(2,128)}, u32[]{:S(2)}) copy-start(f32[1,2,128]{2,1,0:T(2,128)} %param.9) | copy-start | bytes 3076
  2.0 24.5 %copy-start.5 = (f32[1,2,128]{2,1,0:T(2,128)S(1)}, f32[1,2,128]{2,1,0:T(2,128)}, u32[]{:S(2)}) copy-start(f32[1,2,128]{2,1,0:T(2,128)} %param.8) | copy-start | bytes 3076
  2.4 1.4 %collective-permute-start = (bf16[6,8,16,128]{3,2,1,0:T(8,128)(2,1)S(1)}, bf16[6,8,16,128]{3,2,1,0:T(8,128)(2,1)S(1)}, u32[]{:S(2)}, u32[]{:S(2)}) collective-permute-start(bf16[6,8,16,128]{3,2,1,0:T(8,128)(2,1)S(1)} %get-tuple-element.38), channel_id=1, source_target_pairs={{0,8},{1,9},{2,10},{3,11},{4,12},{5,13},{6,14},{7,15},{8,16},{9,17... | collective-permute-start | bytes 589832 | tf_op jit(solution)/shard_map/ppermute | solution.py:426
  3.1 0.7 collective-permute-start.1
  4.7 1.5 %collective-permute-start.2 = (bf16[6,32,8,128]{3,2,1,0:T(8,128)(2,1)}, bf16[6,32,8,128]{3,2,1,0:T(8,128)(2,1)S(1)}, u32[]{:S(2)}, u32[]{:S(2)}) collective-permute-start(bf16[6,32,8,128]{3,2,1,0:T(8,128)(2,1)} %get-tuple-element.40), channel_id=1, source_target_pairs={{0,1},{1,2},{2,3},{3,4},{4,5},{5,6},{6,7},{8,9},{9,10},{10,11},{11... | collective-permute-start | bytes 1179656 | tf_op jit(solution)/shard_map/ppermute | solution.py:426
  5.4 21.0 %collective-permute-start.3 = (bf16[6,32,8,128]{3,2,1,0:T(8,128)(2,1)S(1)}, bf16[6,32,8,128]{3,2,1,0:T(8,128)(2,1)S(1)}, u32[]{:S(2)}, u32[]{:S(2)}) collective-permute-start(bf16[6,32,8,128]{3,2,1,0:T(8,128)(2,1)S(1)} %get-tuple-element.42), channel_id=1, source_target_pairs={{1,0},{2,1},{3,2},{4,3},{5,4},{6,5},{7,6},{9,8},{10,9},{11,10},{12... | collective-permute-start | bytes 1179656 | tf_op jit(solution)/shard_map/ppermute | solution.py:426
  7.1 11.2 %collective-permute-start.7 = (bf16[4,6,16,128]{3,2,1,0:T(8,128)(2,1)S(1)}, bf16[4,6,16,128]{3,2,1,0:T(8,128)(2,1)S(1)}, u32[]{:S(2)}, u32[]{:S(2)}) collective-permute-start(bf16[4,6,16,128]{3,2,1,0:T(8,128)(2,1)S(1)} %get-tuple-element.71), channel_id=1, source_target_pairs={{136,128},{137,129},{138,130},{139,131},{140,132},{141,133},{142,1... | collective-permute-start | bytes 294920 | tf_op jit(solution)/shard_map/ppermute | solution.py:426
  9.4 11.3 %collective-permute-start.6 = (bf16[4,6,16,128]{3,2,1,0:T(8,128)(2,1)S(1)}, bf16[4,6,16,128]{3,2,1,0:T(8,128)(2,1)S(1)}, u32[]{:S(2)}, u32[]{:S(2)}) collective-permute-start(bf16[4,6,16,128]{3,2,1,0:T(8,128)(2,1)S(1)} %get-tuple-element.72), channel_id=1, source_target_pairs={{128,136},{129,137},{130,138},{131,139},{132,140},{133,141},{134,1... | collective-permute-start | bytes 294920 | tf_op jit(solution)/shard_map/ppermute | solution.py:426
  20.8 8.2 %collective-permute-start.8 = (bf16[4,28,6,128]{3,2,1,0:T(8,128)(2,1)S(1)}, bf16[4,28,6,128]{3,2,1,0:T(8,128)(2,1)S(1)}, u32[]{:S(2)}, u32[]{:S(2)}) collective-permute-start(bf16[4,28,6,128]{3,2,1,0:T(8,128)(2,1)S(1)} %pad_maximum_fusion), channel_id=1, source_target_pairs={{128,129},{129,130},{130,131},{131,132},{132,133},{133,134},{134,1... | collective-permute-start | bytes 516104 | tf_op jit(solution)/shard_map/ppermute | solution.py:426
  22.8 7.2 %collective-permute-start.9 = (bf16[4,28,6,128]{3,2,1,0:T(8,128)(2,1)S(1)}, bf16[4,28,6,128]{3,2,1,0:T(8,128)(2,1)S(1)}, u32[]{:S(2)}, u32[]{:S(2)}) collective-permute-start(bf16[4,28,6,128]{3,2,1,0:T(8,128)(2,1)S(1)} %pad_maximum_fusion.1), channel_id=1, source_target_pairs={{129,128},{130,129},{131,130},{132,131},{133,132},{134,133},{135,1... | collective-permute-start | bytes 516104 | tf_op jit(solution)/shard_map/ppermute | solution.py:426
  27.0 5.9 %collective-permute-start.5 = (bf16[28,28,128]{2,1,0:T(8,128)(2,1)S(1)}, bf16[28,28,128]{2,1,0:T(8,128)(2,1)S(1)}, u32[]{:S(2)}, u32[]{:S(2)}) collective-permute-start(bf16[28,28,128]{2,1,0:T(8,128)(2,1)S(1)} %get-tuple-element.47), channel_id=1, source_target_pairs={{0,128},{1,129},{2,130},{3,131},{4,132},{5,133},{6,134},{7,135},{8... | collective-permute-start | bytes 602120 | tf_op jit(solution)/shard_map/ppermute | solution.py:426
  27.7 2.2 %copy-start.2 = (bf16[1,2,2,16,16,128]{5,4,3,2,1,0:T(8,128)(2,1)S(1)}, bf16[1,2,2,16,16,128]{5,4,3,2,1,0:T(8,128)(2,1)}, u32[]{:S(2)}) copy-start(bf16[1,2,2,16,16,128]{5,4,3,2,1,0:T(8,128)(2,1)} %param.6) | copy-start | bytes 786436
  28.3 5.9 %collective-permute-start.4 = (bf16[28,28,128]{2,1,0:T(8,128)(2,1)S(1)}, bf16[28,28,128]{2,1,0:T(8,128)(2,1)S(1)}, u32[]{:S(2)}, u32[]{:S(2)}) collective-permute-start(bf16[28,28,128]{2,1,0:T(8,128)(2,1)S(1)} %get-tuple-element.46), channel_id=1, source_target_pairs={{0,128},{1,129},{2,130},{3,131},{4,132},{5,133},{6,134},{7,135},{8... | collective-permute-start | bytes 602120 | tf_op jit(solution)/shard_map/ppermute | solution.py:426
  33.5 1.9 %collective-permute-start.11 = (bf16[24,24,128]{2,1,0:T(8,128)(2,1)S(1)}, bf16[24,24,128]{2,1,0:T(8,128)(2,1)S(1)}, u32[]{:S(2)}, u32[]{:S(2)}) collective-permute-start(bf16[24,24,128]{2,1,0:T(8,128)(2,1)S(1)} %get-tuple-element.57), channel_id=1, source_target_pairs={{128,256},{129,257},{130,258},{131,259},{132,260},{133,261},{134,2... | collective-permute-start | bytes 442376 | tf_op jit(solution)/shard_map/ppermute | solution.py:426
  34.7 2.7 %collective-permute-start.10 = (bf16[24,24,128]{2,1,0:T(8,128)(2,1)S(1)}, bf16[24,24,128]{2,1,0:T(8,128)(2,1)S(1)}, u32[]{:S(2)}, u32[]{:S(2)}) collective-permute-start(bf16[24,24,128]{2,1,0:T(8,128)(2,1)S(1)} %get-tuple-element.56), channel_id=1, source_target_pairs={{128,256},{129,257},{130,258},{131,259},{132,260},{133,261},{134,2... | collective-permute-start | bytes 442376 | tf_op jit(solution)/shard_map/ppermute | solution.py:426
  36.2 31.9 %collective-permute-start.13 = (bf16[20,20,128]{2,1,0:T(8,128)(2,1)S(1)}, bf16[20,20,128]{2,1,0:T(8,128)(2,1)S(1)}, u32[]{:S(2)}, u32[]{:S(2)}) collective-permute-start(bf16[20,20,128]{2,1,0:T(8,128)(2,1)S(1)} %get-tuple-element.63), channel_id=1, source_target_pairs={{256,384},{257,385},{258,386},{259,387},{260,388},{261,389},{262,3... | collective-permute-start | bytes 307208 | tf_op jit(solution)/shard_map/ppermute | solution.py:426
  38.1 32.6 %collective-permute-start.12 = (bf16[20,20,128]{2,1,0:T(8,128)(2,1)S(1)}, bf16[20,20,128]{2,1,0:T(8,128)(2,1)S(1)}, u32[]{:S(2)}, u32[]{:S(2)}) collective-permute-start(bf16[20,20,128]{2,1,0:T(8,128)(2,1)S(1)} %get-tuple-element.62), channel_id=1, source_target_pairs={{256,384},{257,385},{258,386},{259,387},{260,388},{261,389},{262,3... | collective-permute-start | bytes 307208 | tf_op jit(solution)/shard_map/ppermute | solution.py:426

commit v3 on v2

--- a/solution.py
+++ b/solution.py
@@ -8,6 +8,7 @@
 from jax.sharding import PartitionSpec as P
 
 PITCH = 32
+PACK_ROOM = 58 << 20
 CHUNK = 8
 AXES = ("segment", "row", "col")
 
@@ -98,11 +99,11 @@
         ].astype(jnp.float32)
 
 
-def normed(place, margin, height, width, values_of, gain, flat, rows, span):
+def normed(margin, height, width, values_of, gain, flat, rows, span):
     channels = gain.shape[-1]
     tile = span - 2 * margin
-    top = place[0] * tile - margin
-    columns = column_mask(place[1] * tile - margin, width, channels)
+    top = lax.axis_index("row") * tile - margin
+    columns = column_mask(lax.axis_index("col") * tile - margin, width, channels)
     half_gain = 0.5 * gain
     for first, count in chunks(rows):
         keep = cell_mask(columns, top, height, first, count)
@@ -111,7 +112,7 @@
         )
 
 
-def body(place, halo, height, width, g_ref, held, flat, patches, fill, hidden_of, branch_of, o_ref):
+def body(halo, height, width, g_ref, held, flat, patches, fill, hidden_of, branch_of, o_ref):
     span = o_ref.shape[0] + 4
     blocks = patches.shape[1] // (3 * held.shape[-1])
 
@@ -119,13 +120,13 @@
         return ref[first * PITCH : (first + count) * PITCH, :]
 
     normed(
-        place, halo, height, width, lambda first, count: area(held, first, count),
+        halo, height, width, lambda first, count: area(held, first, count),
         g_ref[0:1, :], flat, span, span,
     )
     fill(0)
     spread(flat, 0, patches, blocks - 1, span)
     normed(
-        place, halo - 1, height, width, hidden_of, g_ref[1:2, :], flat, span - 2, span - 2
+        halo - 1, height, width, hidden_of, g_ref[1:2, :], flat, span - 2, span - 2
     )
     fill(1)
     spread(flat, 0, patches, blocks - 1, span - 2)
@@ -148,10 +149,10 @@
 
 
 def only_at(kernel, step):
-    def run(place, *refs):
-        @pl.when(place[2] == step)
+    def run(*refs):
+        @pl.when(lax.axis_index("segment") == step)
         def _():
-            kernel(place, *refs)
+            kernel(*refs)
 
     return run
 
@@ -162,14 +163,14 @@
     r_ref[...] = o_ref[edge : edge + tile, edge : edge + tile, :]
 
 
-def pass_on(place, step, p_ref, r_ref):
-    @pl.when(place[2] != step)
+def pass_on(step, p_ref, r_ref):
+    @pl.when(lax.axis_index("segment") != step)
     def _():
         r_ref[...] = p_ref[...]
 
 
 def opening_kernel(
-    halo, height, width, place, mid, low, high, left, right, w_ref, b_ref, g_ref,
+    halo, height, width, mid, low, high, left, right, w_ref, b_ref, g_ref,
     o_ref, r_ref, one_ref, two_ref, grid, flat, patches,
 ):
     for slot, source in enumerate((0, 2, 3, 4, 5)):
@@ -192,7 +193,7 @@
         return run
 
     body(
-        place, halo, height, width, g_ref, grid.at[0], flat, patches, fill,
+        halo, height, width, g_ref, grid.at[0], flat, patches, fill,
         conv_of(0, one_ref), conv_of(1, two_ref), o_ref,
     )
     keep_tile(o_ref, r_ref)
@@ -211,21 +212,21 @@
 
 
 def opening_late_kernel(
-    halo, height, width, place, mid, low, high, left, right, w_ref, g_ref,
+    halo, height, width, mid, low, high, left, right, w_ref, g_ref,
     one_ref, two_ref, o_ref, r_ref, held, flat, patches,
 ):
     assemble(held, 1, mid, low, high, left, right)
     body(
-        place, halo, height, width, g_ref, held, flat, patches, nothing,
+        halo, height, width, g_ref, held, flat, patches, nothing,
         late_of(patches, w_ref, 0, one_ref), late_of(patches, w_ref, 1, two_ref), o_ref,
     )
     keep_tile(o_ref, r_ref)
 
 
 def held_kernel(
-    place, cached, low, high, left, right, w_ref, b_ref, one_ref, two_ref, grid, patches
-):
-    @pl.when(place[2] != 0)
+    cached, low, high, left, right, w_ref, b_ref, one_ref, two_ref, grid, patches
+):
+    @pl.when(lax.axis_index("segment") != 0)
     def _():
         add_held(
             cached, low, high, left, right, w_ref, b_ref, one_ref, two_ref, grid, patches
@@ -257,8 +258,8 @@
 
 
 def early_kernel(
-    halo, drop, height, width, place, x_ref, known_one, known_two, w_ref, g_ref, p_ref,
-    o_ref, r_ref, one_ref, two_ref, held, flat, patches,
+    halo, drop, height, width, x_ref, known_one, known_two, w_ref, g_ref, p_ref,
+    r_ref, one_ref, two_ref, o_ref, held, flat, patches,
 ):
     load_rows(x_ref, held)
 
@@ -274,54 +275,57 @@
         return run
 
     body(
-        place, halo, height, width, g_ref, held, flat, patches, nothing,
+        halo, height, width, g_ref, held, flat, patches, nothing,
         conv_of(0, known_one, one_ref), conv_of(1, known_two, two_ref), o_ref,
     )
     keep_tile(o_ref, r_ref)
 
 
 def late_kernel(
-    halo, height, width, place, x_ref, one_ref, two_ref, w_ref, g_ref, p_ref,
+    halo, height, width, x_ref, one_ref, two_ref, w_ref, g_ref, p_ref,
     o_ref, r_ref, held, flat, patches,
 ):
     load_rows(x_ref, held)
     body(
-        place, halo, height, width, g_ref, held, flat, patches, nothing,
+        halo, height, width, g_ref, held, flat, patches, nothing,
         late_of(patches, w_ref, 0, one_ref), late_of(patches, w_ref, 1, two_ref), o_ref,
     )
     keep_tile(o_ref, r_ref)
 
 
 def last_kernel(
-    halo, height, width, place, x_ref, one_ref, two_ref, w_ref, g_ref, p_ref, q_ref,
+    halo, height, width, x_ref, one_ref, two_ref, w_ref, g_ref, p_ref, q_ref,
     r_ref, o_ref, held, flat, patches,
 ):
     late_kernel(
-        halo, height, width, place, x_ref, one_ref, two_ref, w_ref, g_ref, p_ref,
+        halo, height, width, x_ref, one_ref, two_ref, w_ref, g_ref, p_ref,
         o_ref, r_ref.at[1], held, flat, patches,
     )
 
 
-def own_or_passed(kernel, step, former, current, place, *refs):
-    only_at(kernel, step)(place, *refs)
-    pass_on(place, step, refs[former], refs[current])
-
-
-def last_or_passed(kernel, step, former, current, place, *refs):
+def own_or_passed(kernel, step, former, current, *refs):
+    only_at(kernel, step)(*refs)
+    pass_on(step, refs[former], refs[current])
+
+
+def last_or_passed(kernel, step, former, current, *refs):
     refs[current][0] = refs[former + 1][...]
-    only_at(kernel, step)(place, *refs)
-    pass_on(place, step, refs[former], refs[current].at[1])
-
-
-def pack_kernel(frames, cached, mid, low, high, sems):
+    only_at(kernel, step)(*refs)
+    pass_on(step, refs[former], refs[current].at[1])
+
+
+def pack_kernel(frames, cached, low, high, sems):
     reach = low.shape[1]
     tile = frames.shape[1]
+    upper, lower = pl.ds(0, reach), pl.ds(tile - reach, reach)
     copies = []
-    for out, begin, rows in ((low, tile - reach, reach), (high, 0, reach), (mid, 0, tile)):
+    for out, rows in (
+        (low, lower), (high, upper),
+    ):
         for part, offset in ((frames, 0), (cached, 2)):
             copies.append(
                 pltpu.make_async_copy(
-                    part.at[:, pl.ds(begin, rows)],
+                    part.at[:, rows],
                     out.at[pl.ds(offset, part.shape[0])],
                     sems.at[len(copies)],
                 )
@@ -342,7 +346,6 @@
         out[:, reach + tile :] = high[:, :, cut, :]
 
 
-SCALARS = pl.BlockSpec(memory_space=pltpu.SMEM)
 WHOLE = pl.BlockSpec(memory_space=pltpu.VMEM)
 
 
@@ -351,11 +354,11 @@
 
 
 def launch(kernel, arguments, outs, scratch, span, frames):
-    channels = arguments[1].shape[-1]
+    channels = arguments[0].shape[-1]
     return pl.pallas_call(
         kernel,
         out_shape=outs,
-        in_specs=[SCALARS] + [WHOLE] * (len(arguments) - 1),
+        in_specs=[WHOLE] * len(arguments),
         out_specs=[WHOLE] * len(outs),
         scratch_shapes=scratch,
         cost_estimate=pl.CostEstimate(
@@ -388,14 +391,29 @@
 
 
 def packed(frames, cached, halo):
-    tile = (6,) + frames.shape[1:]
     shape = (6, halo) + frames.shape[2:]
     return pl.pallas_call(
         pack_kernel,
-        out_shape=[shaped(*tile), shaped(*shape), shaped(*shape)],
+        out_shape=[shaped(*shape)] * 2,
         in_specs=[pl.BlockSpec(memory_space=pltpu.HBM)] * 2,
-        out_specs=[WHOLE] * 3,
-        scratch_shapes=[pltpu.SemaphoreType.DMA((6,))],
+        out_specs=[pl.BlockSpec(memory_space=pltpu.HBM)] * 2,
+        scratch_shapes=[pltpu.SemaphoreType.DMA((4,))],
+        compiler_params=pltpu.CompilerParams(vmem_limit_bytes=PACK_ROOM),
+    )(frames, cached)
+
+
+def join_kernel(frames, cached, mid):
+    mid[0:2] = frames[...]
+    mid[2:6] = cached[...]
+
+
+def joined(frames, cached):
+    return pl.pallas_call(
+        join_kernel,
+        out_shape=shaped(6, *frames.shape[1:]),
+        in_specs=[WHOLE] * 2,
+        out_specs=WHOLE,
+        cost_estimate=pl.CostEstimate(flops=1 << 28, bytes_accessed=1 << 20, transcendentals=0),
         compiler_params=pltpu.CompilerParams(vmem_limit_bytes=4 << 20),
     )(frames, cached)
 
@@ -454,9 +472,6 @@
 
 def on_device(height, width, frames, caches, weights, biases, gains):
     sections = lax.axis_size("segment")
-    place = jnp.stack(
-        [lax.axis_index("row"), lax.axis_index("col"), lax.axis_index("segment")]
-    ).astype(jnp.int32)
     tile, channels = frames.shape[1], frames.shape[-1]
     kernels = weights[0].reshape((2, 3, 3, 3 * channels, channels))
     bias, gain = biases[0], gains[0]
@@ -464,11 +479,13 @@
     halo = 2 * sections
     reach = halo - 2
     others = list(range(1, sections))
-    mid, low, high = packed(frames, cached, halo)
+    low, high = packed(frames, cached, halo)
+    mid = joined(frames, cached)
     low, high = moved(low, [0], (0, 1, 0)), moved(high, [0], (0, -1, 0))
     left, right = cut_sides(mid, low, high)
     left, right = columns_of(left, right, [0])
-    left, later = lax.optimization_barrier((left, cached))
+    left, later = lax.optimization_barrier((left, mid))
+    later = later[2:]
     pieces = (mid, low, high, left, right)
     low, high = rows_of([later], others, reach)
     left, right = sides_of([later], low, high, reach)
@@ -479,14 +496,14 @@
     onward = shaped(span - 4, span - 4, channels)
     sent, result, one, two = launch(
         only_at(functools.partial(opening_kernel, halo, height, width), 0),
-        (place,) + pieces + (kernels, bias, gain),
+        pieces + (kernels, bias, gain),
         [onward, owned] + parts_of(span, channels),
         scratches(span, 5, 3, channels), span, 3,
     )
     received = moved(sent, [0], (1, 0, 0))
     sent, result_late = launch(
         only_at(functools.partial(opening_late_kernel, halo, height, width), 0),
-        (place,) + pieces + (kernels, gain, one, two),
+        pieces + (kernels, gain, one, two),
         [onward, owned],
         scratches(span, 1, 1, channels), span, 1,
     )
@@ -495,7 +512,7 @@
     span = tile + 2 * reach
     known = launch(
         held_kernel,
-        (place, cached) + ahead + (kernels, bias),
+        (cached,) + ahead + (kernels, bias),
         parts_of(span, 2 * channels),
         [
             pltpu.VMEM((4, room(span), channels), jnp.float32),
@@ -507,41 +524,44 @@
     for step in others:
         span = tile + 2 * halo
         onward = shaped(span - 4, span - 4, channels)
-        sent, result, one, two = launch(
-            functools.partial(
-                own_or_passed,
-                functools.partial(early_kernel, halo, reach - halo, height, width),
-                step, 5, 7,
-            ),
-            (place, received, *known, kernels, gain, result),
-            [onward, owned] + parts_of(span, channels),
-            scratches(span, 1, 1, channels), span, 1,
+        last = step + 1 == sections
+        kernel = functools.partial(early_kernel, halo, reach - halo, height, width)
+        outs = [owned] + parts_of(span, channels)
+        scratch = scratches(span, 1, 1, channels)
+        if last:
+            scratch = [pltpu.VMEM(onward.shape, jnp.bfloat16)] + scratch
+        else:
+            outs = outs + [onward]
+        result, one, two, *sent = launch(
+            functools.partial(own_or_passed, kernel, step, 5, 6),
+            (received, *known, kernels, gain, result),
+            outs, scratch, span, 1,
         )
-        if step + 1 < sections:
-            received = moved(sent, [step], (1, 0, 0))
+        if last:
+            (result,) = launch(
+                functools.partial(
+                    last_or_passed,
+                    functools.partial(last_kernel, halo, height, width),
+                    step, 5, 7,
+                ),
+                (received_late, one, two, kernels, gain, result_late, result),
+                [shaped(2, tile, tile, channels)],
+                [pltpu.VMEM(onward.shape, jnp.bfloat16)] + scratches(span, 1, 1, channels),
+                span, 1,
+            )
+        else:
+            received = moved(sent[0], [step], (1, 0, 0))
             sent, result_late = launch(
                 functools.partial(
                     own_or_passed,
                     functools.partial(late_kernel, halo, height, width),
                     step, 5, 7,
                 ),
-                (place, received_late, one, two, kernels, gain, result_late),
+                (received_late, one, two, kernels, gain, result_late),
                 [onward, owned],
                 scratches(span, 1, 1, channels), span, 1,
             )
             received_late = moved(sent, [step], (1, 0, 0))
-        else:
-            (result,) = launch(
-                functools.partial(
-                    last_or_passed,
-                    functools.partial(last_kernel, halo, height, width),
-                    step, 5, 7,
-                ),
-                (place, received_late, one, two, kernels, gain, result_late, result),
-                [shaped(2, tile, tile, channels)],
-                [pltpu.VMEM(onward.shape, jnp.bfloat16)] + scratches(span, 1, 1, channels),
-                span, 1,
-            )
         halo = halo - 2
     return result[None]
 

time: 73.4 us -> 80.3 us (1.094)
  Pallas kernels: 12.7 us -> 19.3 us
  waiting for transfers between devices: 32.2 us -> 34.3 us
  local copies, waits for them, and re-layouts: 4.02 us -> 1.98 us
    pallas_call x10 -> x11, Pallas kernels: 11.8 us -> 19.1 us  [the longest x1 13 us: packed(): pl.pallas_call(pack_kernel, out_shape=[shaped(*shape)] * 2, in_specs=[pl....]
    ppermute x14, waiting for transfers between devices: 32.2 us -> 34.3 us  [moved(): return lax.ppermute(value, AXES, pairs)]
    slice x3, local copies, waits for them, and re-layouts: 1.05 us -> 0.1 us  [sides_of(): part[:, :, :halo]]
    slice x1, local copies, waits for them, and re-layouts: 0.96 us -> 0.02 us  [rows_of(): high = moved(ends(parts, lambda part: part[:, :halo]), segments, (0, -1, 0))]
  transfers between devices with their start and end apart: 14 -> 14, of which waited for: 3 -> 6; matrix products, arithmetic and copies ran while one was open for 3% -> 0% of each run, Pallas kernels for 12% -> 5%
where the time goes in v3:
time: 80.3 us; the launch traced here: 79.9 us
  waiting for transfers between devices  34.3 us (43%)
  starting transfers between devices  24 us (30%)
  Pallas kernels  19.3 us (24%)
  local copies, waits for them, and re-layouts  1.98 us (2%)
    ppermute x14, waiting for transfers between devices, moved(): return lax.ppermute(value, AXES, pairs)  34.3 us
    ppermute x14, starting transfers between devices, moved(): return lax.ppermute(value, AXES, pairs)  24 us
    pallas_call x1, Pallas kernels, packed(): pl.pallas_call(pack_kernel, out_shape=[shaped(*shape)] * 2, in_specs=[pl....  13 us
    pallas_call x9, Pallas kernels, launch(): pl.pallas_call(kernel, out_shape=outs, in_specs=[WHOLE] * len(arguments),...  6.07 us
    unnamed x12, local copies, waits for them, and re-layouts  1.87 us
  transfers between devices with their start and end apart: 14, of which 6 were waited for; matrix products, arithmetic and copies ran while one was open for 0% of the time, Pallas kernels for 5%

profile of v3, /device:TPU:194, one launch (start us, length us, event | category | flops | bytes accessed | tf_op | source)
XLA Modules:
  0.0 79.9 jit_solution(7926393667479066308)
XLA Ops:
  0.0 13.0 %shard_map.56 = (bf16[6,8,16,128]{3,2,1,0:T(8,128)(2,1)}, bf16[6,8,16,128]{3,2,1,0:T(8,128)(2,1)}) custom-call(bf16[2,16,16,128]{3,2,1,0:T(8,128)(2,1)} %frames.3, bf16[4,16,16,128]{3,2,1,0:T(8,128)(2,1)} %bitcast.14), custom_call_target="tpu_custom_call" | custom-call | tf_op jit(solution)/shard_map/pallas_call | solution.py:395
  13.1 0.7 collective-permute-start
  13.7 0.0 copy-start
  13.7 0.8 %collective-permute-start.1 = (bf16[6,8,16,128]{3,2,1,0:T(8,128)(2,1)}, bf16[6,8,16,128]{3,2,1,0:T(8,128)(2,1)S(1)}, u32[]{:S(2)}, u32[]{:S(2)}) collective-permute-start(bf16[6,8,16,128]{3,2,1,0:T(8,128)(2,1)} %get-tuple-element.37), channel_id=1, source_target_pairs={{8,0},{9,1},{10,2},{11,3},{12,4},{13,5},{14,6},{15,7},{16,8},{17,9... | collective-permute-start | bytes 589832 | tf_op jit(solution)/shard_map/ppermute | solution.py:444
  14.6 0.0 copy-start.1
  14.6 0.9 %copy-done.1 = bf16[1,2,2,16,16,128]{5,4,3,2,1,0:T(8,128)(2,1)S(1)} copy-done((bf16[1,2,2,16,16,128]{5,4,3,2,1,0:T(8,128)(2,1)S(1)}, bf16[1,2,2,16,16,128]{5,4,3,2,1,0:T(8,128)(2,1)}, u32[]{:S(2)}) %copy-start.1) | copy-done | bytes 262168
  15.5 0.0 copy-start.3
  15.5 0.9 %copy-done.3 = bf16[2,16,16,128]{3,2,1,0:T(8,128)(2,1)S(1)} copy-done((bf16[2,16,16,128]{3,2,1,0:T(8,128)(2,1)S(1)}, bf16[2,16,16,128]{3,2,1,0:T(8,128)(2,1)}, u32[]{:S(2)}) %copy-start.3) | copy-done | bytes 131096
  16.4 0.0 copy-start.4
  16.5 0.0 collective-permute-done.low.refs_1_
  16.5 0.0 collective-permute-done.1.high.refs_2_
  16.5 0.1 shard_map.57
  16.6 0.7 collective-permute-start.2
  17.3 0.7 collective-permute-start.3
  18.0 0.0 collective-permute-done.2.refs_3_
  18.0 1.3 %collective-permute-start.7 = (bf16[4,6,16,128]{3,2,1,0:T(8,128)(2,1)S(1)}, bf16[4,6,16,128]{3,2,1,0:T(8,128)(2,1)S(1)}, u32[]{:S(2)}, u32[]{:S(2)}) collective-permute-start(bf16[4,6,16,128]{3,2,1,0:T(8,128)(2,1)S(1)} %get-tuple-element.69), channel_id=1, source_target_pairs={{136,128},{137,129},{138,130},{139,131},{140,132},{141,133},{142,1... | collective-permute-start | bytes 294920 | tf_op jit(solution)/shard_map/ppermute | solution.py:444
  19.3 0.1 fusion
  19.4 8.8 %collective-permute-start.6 = (bf16[4,6,16,128]{3,2,1,0:T(8,128)(2,1)S(1)}, bf16[4,6,16,128]{3,2,1,0:T(8,128)(2,1)S(1)}, u32[]{:S(2)}, u32[]{:S(2)}) collective-permute-start(bf16[4,6,16,128]{3,2,1,0:T(8,128)(2,1)S(1)} %get-tuple-element.70), channel_id=1, source_target_pairs={{128,136},{129,137},{130,138},{131,139},{132,140},{133,141},{134,1... | collective-permute-start | bytes 294920 | tf_op jit(solution)/shard_map/ppermute | solution.py:444
  28.3 0.9 %collective-permute-done.7.high = bf16[4,6,16,128]{3,2,1,0:T(8,128)(2,1)S(1)} collective-permute-done((bf16[4,6,16,128]{3,2,1,0:T(8,128)(2,1)S(1)}, bf16[4,6,16,128]{3,2,1,0:T(8,128)(2,1)S(1)}, u32[]{:S(2)}, u32[]{:S(2)}) %collective-permute-start.7) | collective-permute-done | bytes 98336 | tf_op jit(solution)/shard_map/ppermute | solution.py:444
  29.2 2.5 %collective-permute-done.6.low = bf16[4,6,16,128]{3,2,1,0:T(8,128)(2,1)S(1)} collective-permute-done((bf16[4,6,16,128]{3,2,1,0:T(8,128)(2,1)S(1)}, bf16[4,6,16,128]{3,2,1,0:T(8,128)(2,1)S(1)}, u32[]{:S(2)}, u32[]{:S(2)}) %collective-permute-start.6) | collective-permute-done | bytes 98336 | tf_op jit(solution)/shard_map/ppermute | solution.py:444
  31.7 0.1 pad_maximum_fusion
  31.8 1.9 %collective-permute-start.8 = (bf16[4,28,6,128]{3,2,1,0:T(8,128)(2,1)S(1)}, bf16[4,28,6,128]{3,2,1,0:T(8,128)(2,1)S(1)}, u32[]{:S(2)}, u32[]{:S(2)}) collective-permute-start(bf16[4,28,6,128]{3,2,1,0:T(8,128)(2,1)S(1)} %pad_maximum_fusion), channel_id=1, source_target_pairs={{128,129},{129,130},{130,131},{131,132},{132,133},{133,134},{134,1... | collective-permute-start | bytes 516104 | tf_op jit(solution)/shard_map/ppermute | solution.py:444
  33.7 0.1 pad_maximum_fusion.1
  33.7 3.6 %collective-permute-start.9 = (bf16[4,28,6,128]{3,2,1,0:T(8,128)(2,1)S(1)}, bf16[4,28,6,128]{3,2,1,0:T(8,128)(2,1)S(1)}, u32[]{:S(2)}, u32[]{:S(2)}) collective-permute-start(bf16[4,28,6,128]{3,2,1,0:T(8,128)(2,1)S(1)} %pad_maximum_fusion.1), channel_id=1, source_target_pairs={{129,128},{130,129},{131,130},{132,131},{133,132},{134,133},{135,1... | collective-permute-start | bytes 516104 | tf_op jit(solution)/shard_map/ppermute | solution.py:444
  37.4 0.0 collective-permute-done.3.refs_4_
  37.4 0.0 copy-done
  37.4 0.0 copy-done.4
  37.4 0.0 copy-done.5
  37.5 0.7 collective-permute-start.5
  38.1 0.0 copy-start.2
  38.2 0.8 %collective-permute-start.4 = (bf16[28,28,128]{2,1,0:T(8,128)(2,1)S(1)}, bf16[28,28,128]{2,1,0:T(8,128)(2,1)S(1)}, u32[]{:S(2)}, u32[]{:S(2)}) collective-permute-start(bf16[28,28,128]{2,1,0:T(8,128)(2,1)S(1)} %get-tuple-element.44), channel_id=1, source_target_pairs={{0,128},{1,129},{2,130},{3,131},{4,132},{5,133},{6,134},{7,135},{8... | collective-permute-start | bytes 602120 | tf_op jit(solution)/shard_map/ppermute | solution.py:444
  39.0 0.1 collective-permute-done.8.left
  39.1 1.8 %collective-permute-done.9.right = bf16[4,28,6,128]{3,2,1,0:T(8,128)(2,1)S(1)} collective-permute-done((bf16[4,28,6,128]{3,2,1,0:T(8,128)(2,1)S(1)}, bf16[4,28,6,128]{3,2,1,0:T(8,128)(2,1)S(1)}, u32[]{:S(2)}, u32[]{:S(2)}) %collective-permute-start.9) | collective-permute-done | bytes 172064 | tf_op jit(solution)/shard_map/ppermute | solution.py:444
  40.9 0.0 copy-done.2
  40.9 2.5 %shard_map.60 = (f32[832,256]{1,0:T(8,128)S(1)}, f32[768,256]{1,0:T(8,128)S(1)}) custom-call(bf16[4,16,16,128]{3,2,1,0:T(8,128)(2,1)S(1)} %bitcast.16, bf16[4,6,16,128]{3,2,1,0:T(8,128)(2,1)S(1)} %collective-permute-done.6.low, bf16[4,6,16,128]{3,2,1,0:T(8,128)(2,1)S(1)} %collective-permute-done.7.high, ...), custom_call_target="tpu_custom_call" | custom-call | flops 2113929216 | bytes 2097152 | tf_op jit(solution)/shard_map/pallas_call | solution.py:358
  43.4 0.0 collective-permute-done.5.refs_0_
  43.4 0.7 collective-permute-start.11
  44.1 0.0 collective-permute-done.4.refs_0_
  44.2 0.7 collective-permute-start.10
  44.8 0.0 collective-permute-done.11.refs_0_
  44.9 0.2 shard_map.63
  45.1 1.3 %collective-permute-start.13 = (bf16[20,20,128]{2,1,0:T(8,128)(2,1)S(1)}, bf16[20,20,128]{2,1,0:T(8,128)(2,1)S(1)}, u32[]{:S(2)}, u32[]{:S(2)}) collective-permute-start(bf16[20,20,128]{2,1,0:T(8,128)(2,1)S(1)} %get-tuple-element.61), channel_id=1, source_target_pairs={{256,384},{257,385},{258,386},{259,387},{260,388},{261,389},{262,3... | collective-permute-start | bytes 307208 | tf_op jit(solution)/shard_map/ppermute | solution.py:444
  46.4 0.0 collective-permute-done.10.refs_0_
  46.4 1.3 %collective-permute-start.12 = (bf16[20,20,128]{2,1,0:T(8,128)(2,1)S(1)}, bf16[20,20,128]{2,1,0:T(8,128)(2,1)S(1)}, u32[]{:S(2)}, u32[]{:S(2)}) collective-permute-start(bf16[20,20,128]{2,1,0:T(8,128)(2,1)S(1)} %get-tuple-element.60), channel_id=1, source_target_pairs={{256,384},{257,385},{258,386},{259,387},{260,388},{261,389},{262,3... | collective-permute-start | bytes 307208 | tf_op jit(solution)/shard_map/ppermute | solution.py:444
  47.7 26.2 %collective-permute-done.13.refs_0_ = bf16[20,20,128]{2,1,0:T(8,128)(2,1)S(1)} collective-permute-done((bf16[20,20,128]{2,1,0:T(8,128)(2,1)S(1)}, bf16[20,20,128]{2,1,0:T(8,128)(2,1)S(1)}, u32[]{:S(2)}, u32[]{:S(2)}) %collective-permute-start.13) | collective-permute-done | bytes 102432 | tf_op jit(solution)/shard_map/ppermute | solution.py:444
  73.9 1.4 %shard_map.65 = (bf16[16,16,128]{2,1,0:T(8,128)(2,1)S(1)}, f32[576,128]{1,0:T(8,128)S(1)}, f32[512,128]{1,0:T(8,128)S(1)}) custom-call(bf16[20,20,128]{2,1,0:T(8,128)(2,1)S(1)} %collective-permute-done.13.refs_0_, f32[832,256]{1,0:T(8,128)S(1)} %get-tuple-element.48.refs_1_, f32[768,256]{1,0:T(8,128)S(1)} %get-tuple-element.49.refs_2_, ...), custom_call_target="tpu_custom_call" | custom-call | flops 754974720 | bytes 2097152 | tf_op jit(solution)/shard_map/pallas_call | solution.py:358
  75.3 2.7 %collective-permute-done.12.refs_0_ = bf16[20,20,128]{2,1,0:T(8,128)(2,1)S(1)} collective-permute-done((bf16[20,20,128]{2,1,0:T(8,128)(2,1)S(1)}, bf16[20,20,128]{2,1,0:T(8,128)(2,1)S(1)}, u32[]{:S(2)}, u32[]{:S(2)}) %collective-permute-start.12) | collective-permute-done | bytes 102432 | tf_op jit(solution)/shard_map/ppermute | solution.py:444
  78.1 1.9 %shard_map.66 = bf16[2,16,16,128]{3,2,1,0:T(8,128)(2,1)} custom-call(bf16[20,20,128]{2,1,0:T(8,128)(2,1)S(1)} %collective-permute-done.12.refs_0_, f32[576,128]{1,0:T(8,128)S(1)} %get-tuple-element.63.refs_1_, f32[512,128]{1,0:T(8,128)S(1)} %get-tuple-element.64.refs_2_, bf16[2,3,3,384,128]{4,3,2,1,0:T(8,128)(2,1)S(1)} %bitcast.13, f32[2,128]{1,0:T(2,128)S(1)} %bitcast.24, ...), custom_call_target="tpu_custom_call" | custom-call | flops 754974720 | bytes 2097152 | tf_op jit(solution)/shard_map/pallas_call | solution.py:358
  (10 shorter events, 0.2 us)
Async XLA Ops:
  13.1 3.4 %collective-permute-start = (bf16[6,8,16,128]{3,2,1,0:T(8,128)(2,1)}, bf16[6,8,16,128]{3,2,1,0:T(8,128)(2,1)S(1)}, u32[]{:S(2)}, u32[]{:S(2)}) collective-permute-start(bf16[6,8,16,128]{3,2,1,0:T(8,128)(2,1)} %get-tuple-element.36), channel_id=1, source_target_pairs={{0,8},{1,9},{2,10},{3,11},{4,12},{5,13},{6,14},{7,15},{8,16},{9,17... | collective-permute-start | bytes 589832 | tf_op jit(solution)/shard_map/ppermute | solution.py:444
  13.7 23.7 %copy-start = (bf16[1,2,3,3,3,128,128]{6,5,4,3,2,1,0:T(8,128)(2,1)S(1)}, bf16[1,2,3,3,3,128,128]{6,5,4,3,2,1,0:T(8,128)(2,1)}, u32[]{:S(2)}) copy-start(bf16[1,2,3,3,3,128,128]{6,5,4,3,2,1,0:T(8,128)(2,1)} %param.7) | copy-start | bytes 5308420
  13.7 2.7 %collective-permute-start.1 = (bf16[6,8,16,128]{3,2,1,0:T(8,128)(2,1)}, bf16[6,8,16,128]{3,2,1,0:T(8,128)(2,1)S(1)}, u32[]{:S(2)}, u32[]{:S(2)}) collective-permute-start(bf16[6,8,16,128]{3,2,1,0:T(8,128)(2,1)} %get-tuple-element.37), channel_id=1, source_target_pairs={{8,0},{9,1},{10,2},{11,3},{12,4},{13,5},{14,6},{15,7},{16,8},{17,9... | collective-permute-start | bytes 589832 | tf_op jit(solution)/shard_map/ppermute | solution.py:444
  14.6 1.0 %copy-start.1 = (bf16[1,2,2,16,16,128]{5,4,3,2,1,0:T(8,128)(2,1)S(1)}, bf16[1,2,2,16,16,128]{5,4,3,2,1,0:T(8,128)(2,1)}, u32[]{:S(2)}) copy-start(bf16[1,2,2,16,16,128]{5,4,3,2,1,0:T(8,128)(2,1)} %param.6) | copy-start | bytes 786436
  15.5 0.9 %copy-start.3 = (bf16[2,16,16,128]{3,2,1,0:T(8,128)(2,1)S(1)}, bf16[2,16,16,128]{3,2,1,0:T(8,128)(2,1)}, u32[]{:S(2)}) copy-start(bf16[2,16,16,128]{3,2,1,0:T(8,128)(2,1)} %frames.3) | copy-start | bytes 393220
  16.4 21.0 %copy-start.4 = (f32[1,2,128]{2,1,0:T(2,128)S(1)}, f32[1,2,128]{2,1,0:T(2,128)}, u32[]{:S(2)}) copy-start(f32[1,2,128]{2,1,0:T(2,128)} %param.9) | copy-start | bytes 3076
  16.4 21.0 %copy-start.5 = (f32[1,2,128]{2,1,0:T(2,128)S(1)}, f32[1,2,128]{2,1,0:T(2,128)}, u32[]{:S(2)}) copy-start(f32[1,2,128]{2,1,0:T(2,128)} %param.8) | copy-start | bytes 3076
  16.6 1.4 %collective-permute-start.2 = (bf16[6,32,8,128]{3,2,1,0:T(8,128)(2,1)S(1)}, bf16[6,32,8,128]{3,2,1,0:T(8,128)(2,1)S(1)}, u32[]{:S(2)}, u32[]{:S(2)}) collective-permute-start(bf16[6,32,8,128]{3,2,1,0:T(8,128)(2,1)S(1)} %get-tuple-element.38), channel_id=1, source_target_pairs={{0,1},{1,2},{2,3},{3,4},{4,5},{5,6},{6,7},{8,9},{9,10},{10,11},{11... | collective-permute-start | bytes 1179656 | tf_op jit(solution)/shard_map/ppermute | solution.py:444
  17.3 20.1 %collective-permute-start.3 = (bf16[6,32,8,128]{3,2,1,0:T(8,128)(2,1)S(1)}, bf16[6,32,8,128]{3,2,1,0:T(8,128)(2,1)S(1)}, u32[]{:S(2)}, u32[]{:S(2)}) collective-permute-start(bf16[6,32,8,128]{3,2,1,0:T(8,128)(2,1)S(1)} %get-tuple-element.40), channel_id=1, source_target_pairs={{1,0},{2,1},{3,2},{4,3},{5,4},{6,5},{7,6},{9,8},{10,9},{11,10},{12... | collective-permute-start | bytes 1179656 | tf_op jit(solution)/shard_map/ppermute | solution.py:444
  18.0 11.1 %collective-permute-start.7 = (bf16[4,6,16,128]{3,2,1,0:T(8,128)(2,1)S(1)}, bf16[4,6,16,128]{3,2,1,0:T(8,128)(2,1)S(1)}, u32[]{:S(2)}, u32[]{:S(2)}) collective-permute-start(bf16[4,6,16,128]{3,2,1,0:T(8,128)(2,1)S(1)} %get-tuple-element.69), channel_id=1, source_target_pairs={{136,128},{137,129},{138,130},{139,131},{140,132},{141,133},{142,1... | collective-permute-start | bytes 294920 | tf_op jit(solution)/shard_map/ppermute | solution.py:444
  19.4 12.3 %collective-permute-start.6 = (bf16[4,6,16,128]{3,2,1,0:T(8,128)(2,1)S(1)}, bf16[4,6,16,128]{3,2,1,0:T(8,128)(2,1)S(1)}, u32[]{:S(2)}, u32[]{:S(2)}) collective-permute-start(bf16[4,6,16,128]{3,2,1,0:T(8,128)(2,1)S(1)} %get-tuple-element.70), channel_id=1, source_target_pairs={{128,136},{129,137},{130,138},{131,139},{132,140},{133,141},{134,1... | collective-permute-start | bytes 294920 | tf_op jit(solution)/shard_map/ppermute | solution.py:444
  31.8 7.3 %collective-permute-start.8 = (bf16[4,28,6,128]{3,2,1,0:T(8,128)(2,1)S(1)}, bf16[4,28,6,128]{3,2,1,0:T(8,128)(2,1)S(1)}, u32[]{:S(2)}, u32[]{:S(2)}) collective-permute-start(bf16[4,28,6,128]{3,2,1,0:T(8,128)(2,1)S(1)} %pad_maximum_fusion), channel_id=1, source_target_pairs={{128,129},{129,130},{130,131},{131,132},{132,133},{133,134},{134,1... | collective-permute-start | bytes 516104 | tf_op jit(solution)/shard_map/ppermute | solution.py:444
  33.7 7.2 %collective-permute-start.9 = (bf16[4,28,6,128]{3,2,1,0:T(8,128)(2,1)S(1)}, bf16[4,28,6,128]{3,2,1,0:T(8,128)(2,1)S(1)}, u32[]{:S(2)}, u32[]{:S(2)}) collective-permute-start(bf16[4,28,6,128]{3,2,1,0:T(8,128)(2,1)S(1)} %pad_maximum_fusion.1), channel_id=1, source_target_pairs={{129,128},{130,129},{131,130},{132,131},{133,132},{134,133},{135,1... | collective-permute-start | bytes 516104 | tf_op jit(solution)/shard_map/ppermute | solution.py:444
  37.5 5.9 %collective-permute-start.5 = (bf16[28,28,128]{2,1,0:T(8,128)(2,1)S(1)}, bf16[28,28,128]{2,1,0:T(8,128)(2,1)S(1)}, u32[]{:S(2)}, u32[]{:S(2)}) collective-permute-start(bf16[28,28,128]{2,1,0:T(8,128)(2,1)S(1)} %get-tuple-element.45), channel_id=1, source_target_pairs={{0,128},{1,129},{2,130},{3,131},{4,132},{5,133},{6,134},{7,135},{8... | collective-permute-start | bytes 602120 | tf_op jit(solution)/shard_map/ppermute | solution.py:444
  38.1 2.8 %copy-start.2 = (bf16[1,2,2,16,16,128]{5,4,3,2,1,0:T(8,128)(2,1)S(1)}, bf16[1,2,2,16,16,128]{5,4,3,2,1,0:T(8,128)(2,1)}, u32[]{:S(2)}) copy-start(bf16[1,2,2,16,16,128]{5,4,3,2,1,0:T(8,128)(2,1)} %param.6) | copy-start | bytes 786436
  38.2 5.9 %collective-permute-start.4 = (bf16[28,28,128]{2,1,0:T(8,128)(2,1)S(1)}, bf16[28,28,128]{2,1,0:T(8,128)(2,1)S(1)}, u32[]{:S(2)}, u32[]{:S(2)}) collective-permute-start(bf16[28,28,128]{2,1,0:T(8,128)(2,1)S(1)} %get-tuple-element.44), channel_id=1, source_target_pairs={{0,128},{1,129},{2,130},{3,131},{4,132},{5,133},{6,134},{7,135},{8... | collective-permute-start | bytes 602120 | tf_op jit(solution)/shard_map/ppermute | solution.py:444
  43.4 1.4 %collective-permute-start.11 = (bf16[24,24,128]{2,1,0:T(8,128)(2,1)S(1)}, bf16[24,24,128]{2,1,0:T(8,128)(2,1)S(1)}, u32[]{:S(2)}, u32[]{:S(2)}) collective-permute-start(bf16[24,24,128]{2,1,0:T(8,128)(2,1)S(1)} %get-tuple-element.55), channel_id=1, source_target_pairs={{128,256},{129,257},{130,258},{131,259},{132,260},{133,261},{134,2... | collective-permute-start | bytes 442376 | tf_op jit(solution)/shard_map/ppermute | solution.py:444
  44.2 2.2 %collective-permute-start.10 = (bf16[24,24,128]{2,1,0:T(8,128)(2,1)S(1)}, bf16[24,24,128]{2,1,0:T(8,128)(2,1)S(1)}, u32[]{:S(2)}, u32[]{:S(2)}) collective-permute-start(bf16[24,24,128]{2,1,0:T(8,128)(2,1)S(1)} %get-tuple-element.54), channel_id=1, source_target_pairs={{128,256},{129,257},{130,258},{131,259},{132,260},{133,261},{134,2... | collective-permute-start | bytes 442376 | tf_op jit(solution)/shard_map/ppermute | solution.py:444
  45.1 28.8 %collective-permute-start.13 = (bf16[20,20,128]{2,1,0:T(8,128)(2,1)S(1)}, bf16[20,20,128]{2,1,0:T(8,128)(2,1)S(1)}, u32[]{:S(2)}, u32[]{:S(2)}) collective-permute-start(bf16[20,20,128]{2,1,0:T(8,128)(2,1)S(1)} %get-tuple-element.61), channel_id=1, source_target_pairs={{256,384},{257,385},{258,386},{259,387},{260,388},{261,389},{262,3... | collective-permute-start | bytes 307208 | tf_op jit(solution)/shard_map/ppermute | solution.py:444
  46.4 31.7 %collective-permute-start.12 = (bf16[20,20,128]{2,1,0:T(8,128)(2,1)S(1)}, bf16[20,20,128]{2,1,0:T(8,128)(2,1)S(1)}, u32[]{:S(2)}, u32[]{:S(2)}) collective-permute-start(bf16[20,20,128]{2,1,0:T(8,128)(2,1)S(1)} %get-tuple-element.60), channel_id=1, source_target_pairs={{256,384},{257,385},{258,386},{259,387},{260,388},{261,389},{262,3... | collective-permute-start | bytes 307208 | tf_op jit(solution)/shard_map/ppermute | solution.py:444

commit v4 on v3

--- a/solution.py
+++ b/solution.py
@@ -8,7 +8,7 @@
 from jax.sharding import PartitionSpec as P
 
 PITCH = 32
-PACK_ROOM = 58 << 20
+PACK_ROOM = 4 << 20
 CHUNK = 8
 AXES = ("segment", "row", "col")
 
@@ -314,13 +314,13 @@
     pass_on(step, refs[former], refs[current].at[1])
 
 
-def pack_kernel(frames, cached, low, high, sems):
+def pack_kernel(frames, cached, mid, low, high, sems):
     reach = low.shape[1]
     tile = frames.shape[1]
-    upper, lower = pl.ds(0, reach), pl.ds(tile - reach, reach)
+    upper, lower, every = pl.ds(0, reach), pl.ds(tile - reach, reach), pl.ds(0, tile)
     copies = []
     for out, rows in (
-        (low, lower), (high, upper),
+        (low, lower), (high, upper), (mid, every),
     ):
         for part, offset in ((frames, 0), (cached, 2)):
             copies.append(
@@ -391,30 +391,15 @@
 
 
 def packed(frames, cached, halo):
+    tile = (6,) + frames.shape[1:]
     shape = (6, halo) + frames.shape[2:]
     return pl.pallas_call(
         pack_kernel,
-        out_shape=[shaped(*shape)] * 2,
+        out_shape=[shaped(*tile), shaped(*shape), shaped(*shape)],
         in_specs=[pl.BlockSpec(memory_space=pltpu.HBM)] * 2,
-        out_specs=[pl.BlockSpec(memory_space=pltpu.HBM)] * 2,
-        scratch_shapes=[pltpu.SemaphoreType.DMA((4,))],
+        out_specs=[WHOLE] * 3,
+        scratch_shapes=[pltpu.SemaphoreType.DMA((6,))],
         compiler_params=pltpu.CompilerParams(vmem_limit_bytes=PACK_ROOM),
-    )(frames, cached)
-
-
-def join_kernel(frames, cached, mid):
-    mid[0:2] = frames[...]
-    mid[2:6] = cached[...]
-
-
-def joined(frames, cached):
-    return pl.pallas_call(
-        join_kernel,
-        out_shape=shaped(6, *frames.shape[1:]),
-        in_specs=[WHOLE] * 2,
-        out_specs=WHOLE,
-        cost_estimate=pl.CostEstimate(flops=1 << 28, bytes_accessed=1 << 20, transcendentals=0),
-        compiler_params=pltpu.CompilerParams(vmem_limit_bytes=4 << 20),
     )(frames, cached)
 
 
@@ -479,8 +464,7 @@
     halo = 2 * sections
     reach = halo - 2
     others = list(range(1, sections))
-    low, high = packed(frames, cached, halo)
-    mid = joined(frames, cached)
+    mid, low, high = packed(frames, cached, halo)
     low, high = moved(low, [0], (0, 1, 0)), moved(high, [0], (0, -1, 0))
     left, right = cut_sides(mid, low, high)
     left, right = columns_of(left, right, [0])

time: 80.3 us -> 71.2 us (0.89)
  the two profiles are of different devices: /device:TPU:194 before, /device:TPU:210 now
where the time goes in v4:
time: 71.2 us; the launch traced here: 70.9 us
  waiting for transfers between devices  37.9 us (53%)
  starting transfers between devices  23.8 us (33%)
  Pallas kernels  6.61 us (9%)
  local copies, waits for them, and re-layouts  2.12 us (3%)
    ppermute x14, waiting for transfers between devices, moved(): return lax.ppermute(value, AXES, pairs)  37.9 us
    ppermute x14, starting transfers between devices, moved(): return lax.ppermute(value, AXES, pairs)  23.8 us
    pallas_call x9, Pallas kernels, launch(): pl.pallas_call(kernel, out_shape=outs, in_specs=[WHOLE] * len(arguments),...  6.07 us
    unnamed x12, local copies, waits for them, and re-layouts  2 us
  transfers between devices with their start and end apart: 14, of which 6 were waited for; matrix products, arithmetic and copies ran while one was open for 0% of the time, Pallas kernels for 6%

profile of v4, /device:TPU:210, one launch (start us, length us, event | category | flops | bytes accessed | tf_op | source)
XLA Modules:
  0.0 70.9 jit_solution(716955287963924690)
XLA Ops:
  0.0 0.0 copy-start
  0.0 0.0 copy-start.1
  0.0 1.1 %copy-done.1 = bf16[1,2,2,16,16,128]{5,4,3,2,1,0:T(8,128)(2,1)S(1)} copy-done((bf16[1,2,2,16,16,128]{5,4,3,2,1,0:T(8,128)(2,1)S(1)}, bf16[1,2,2,16,16,128]{5,4,3,2,1,0:T(8,128)(2,1)}, u32[]{:S(2)}) %copy-start.1) | copy-done | bytes 262168
  1.1 0.0 copy-start.3
  1.1 0.9 %copy-done.3 = bf16[2,16,16,128]{3,2,1,0:T(8,128)(2,1)S(1)} copy-done((bf16[2,16,16,128]{3,2,1,0:T(8,128)(2,1)S(1)}, bf16[2,16,16,128]{3,2,1,0:T(8,128)(2,1)}, u32[]{:S(2)}) %copy-start.3) | copy-done | bytes 131096
  2.0 0.0 copy-start.4
  2.0 0.4 shard_map.55
  2.4 0.7 collective-permute-start
  3.1 0.7 collective-permute-start.1
  3.8 0.0 collective-permute-done.low.refs_1_
  3.8 0.0 collective-permute-done.1.high.refs_2_
  3.8 0.1 shard_map.56
  3.9 0.7 collective-permute-start.2
  4.6 0.7 collective-permute-start.3
  5.3 0.0 collective-permute-done.2.refs_3_
  5.4 8.1 %collective-permute-start.7 = (bf16[4,6,16,128]{3,2,1,0:T(8,128)(2,1)S(1)}, bf16[4,6,16,128]{3,2,1,0:T(8,128)(2,1)S(1)}, u32[]{:S(2)}, u32[]{:S(2)}) collective-permute-start(bf16[4,6,16,128]{3,2,1,0:T(8,128)(2,1)S(1)} %get-tuple-element.71), channel_id=1, source_target_pairs={{136,128},{137,129},{138,130},{139,131},{140,132},{141,133},{142,1... | collective-permute-start | bytes 294920 | tf_op jit(solution)/shard_map/ppermute | solution.py:429
  13.5 0.1 fusion
  13.5 2.0 %collective-permute-start.6 = (bf16[4,6,16,128]{3,2,1,0:T(8,128)(2,1)S(1)}, bf16[4,6,16,128]{3,2,1,0:T(8,128)(2,1)S(1)}, u32[]{:S(2)}, u32[]{:S(2)}) collective-permute-start(bf16[4,6,16,128]{3,2,1,0:T(8,128)(2,1)S(1)} %get-tuple-element.72), channel_id=1, source_target_pairs={{128,136},{129,137},{130,138},{131,139},{132,140},{133,141},{134,1... | collective-permute-start | bytes 294920 | tf_op jit(solution)/shard_map/ppermute | solution.py:429
  15.6 0.9 %collective-permute-done.7.high = bf16[4,6,16,128]{3,2,1,0:T(8,128)(2,1)S(1)} collective-permute-done((bf16[4,6,16,128]{3,2,1,0:T(8,128)(2,1)S(1)}, bf16[4,6,16,128]{3,2,1,0:T(8,128)(2,1)S(1)}, u32[]{:S(2)}, u32[]{:S(2)}) %collective-permute-start.7) | collective-permute-done | bytes 98336 | tf_op jit(solution)/shard_map/ppermute | solution.py:429
  16.5 8.6 %collective-permute-done.6.low = bf16[4,6,16,128]{3,2,1,0:T(8,128)(2,1)S(1)} collective-permute-done((bf16[4,6,16,128]{3,2,1,0:T(8,128)(2,1)S(1)}, bf16[4,6,16,128]{3,2,1,0:T(8,128)(2,1)S(1)}, u32[]{:S(2)}, u32[]{:S(2)}) %collective-permute-start.6) | collective-permute-done | bytes 98336 | tf_op jit(solution)/shard_map/ppermute | solution.py:429
  25.2 0.1 pad_maximum_fusion
  25.2 1.9 %collective-permute-start.8 = (bf16[4,28,6,128]{3,2,1,0:T(8,128)(2,1)S(1)}, bf16[4,28,6,128]{3,2,1,0:T(8,128)(2,1)S(1)}, u32[]{:S(2)}, u32[]{:S(2)}) collective-permute-start(bf16[4,28,6,128]{3,2,1,0:T(8,128)(2,1)S(1)} %pad_maximum_fusion), channel_id=1, source_target_pairs={{128,129},{129,130},{130,131},{131,132},{132,133},{133,134},{134,1... | collective-permute-start | bytes 516104 | tf_op jit(solution)/shard_map/ppermute | solution.py:429
  27.2 0.1 pad_maximum_fusion.1
  27.2 3.6 %collective-permute-start.9 = (bf16[4,28,6,128]{3,2,1,0:T(8,128)(2,1)S(1)}, bf16[4,28,6,128]{3,2,1,0:T(8,128)(2,1)S(1)}, u32[]{:S(2)}, u32[]{:S(2)}) collective-permute-start(bf16[4,28,6,128]{3,2,1,0:T(8,128)(2,1)S(1)} %pad_maximum_fusion.1), channel_id=1, source_target_pairs={{129,128},{130,129},{131,130},{132,131},{133,132},{134,133},{135,1... | collective-permute-start | bytes 516104 | tf_op jit(solution)/shard_map/ppermute | solution.py:429
  30.9 0.0 collective-permute-done.3.refs_4_
  30.9 0.0 copy-done
  30.9 0.0 copy-done.4
  30.9 0.0 copy-done.5
  30.9 0.7 collective-permute-start.5
  31.6 0.0 copy-start.2
  31.7 0.8 %collective-permute-start.4 = (bf16[28,28,128]{2,1,0:T(8,128)(2,1)S(1)}, bf16[28,28,128]{2,1,0:T(8,128)(2,1)S(1)}, u32[]{:S(2)}, u32[]{:S(2)}) collective-permute-start(bf16[28,28,128]{2,1,0:T(8,128)(2,1)S(1)} %get-tuple-element.46), channel_id=1, source_target_pairs={{0,128},{1,129},{2,130},{3,131},{4,132},{5,133},{6,134},{7,135},{8... | collective-permute-start | bytes 602120 | tf_op jit(solution)/shard_map/ppermute | solution.py:429
  32.5 0.1 collective-permute-done.8.left
  32.6 1.8 %collective-permute-done.9.right = bf16[4,28,6,128]{3,2,1,0:T(8,128)(2,1)S(1)} collective-permute-done((bf16[4,28,6,128]{3,2,1,0:T(8,128)(2,1)S(1)}, bf16[4,28,6,128]{3,2,1,0:T(8,128)(2,1)S(1)}, u32[]{:S(2)}, u32[]{:S(2)}) %collective-permute-start.9) | collective-permute-done | bytes 172064 | tf_op jit(solution)/shard_map/ppermute | solution.py:429
  34.4 0.0 copy-done.2
  34.4 2.5 %shard_map.59 = (f32[832,256]{1,0:T(8,128)S(1)}, f32[768,256]{1,0:T(8,128)S(1)}) custom-call(bf16[4,16,16,128]{3,2,1,0:T(8,128)(2,1)S(1)} %bitcast.15, bf16[4,6,16,128]{3,2,1,0:T(8,128)(2,1)S(1)} %collective-permute-done.6.low, bf16[4,6,16,128]{3,2,1,0:T(8,128)(2,1)S(1)} %collective-permute-done.7.high, ...), custom_call_target="tpu_custom_call" | custom-call | flops 2113929216 | bytes 2097152 | tf_op jit(solution)/shard_map/pallas_call | solution.py:358
  36.9 0.0 collective-permute-done.5.refs_0_
  36.9 0.7 collective-permute-start.11
  37.6 0.0 collective-permute-done.4.refs_0_
  37.6 0.7 collective-permute-start.10
  38.3 0.0 collective-permute-done.11.refs_0_
  38.3 0.2 shard_map.62
  38.5 1.3 %collective-permute-start.13 = (bf16[20,20,128]{2,1,0:T(8,128)(2,1)S(1)}, bf16[20,20,128]{2,1,0:T(8,128)(2,1)S(1)}, u32[]{:S(2)}, u32[]{:S(2)}) collective-permute-start(bf16[20,20,128]{2,1,0:T(8,128)(2,1)S(1)} %get-tuple-element.63), channel_id=1, source_target_pairs={{256,384},{257,385},{258,386},{259,387},{260,388},{261,389},{262,3... | collective-permute-start | bytes 307208 | tf_op jit(solution)/shard_map/ppermute | solution.py:429
  39.8 0.0 collective-permute-done.10.refs_0_
  39.9 1.3 %collective-permute-start.12 = (bf16[20,20,128]{2,1,0:T(8,128)(2,1)S(1)}, bf16[20,20,128]{2,1,0:T(8,128)(2,1)S(1)}, u32[]{:S(2)}, u32[]{:S(2)}) collective-permute-start(bf16[20,20,128]{2,1,0:T(8,128)(2,1)S(1)} %get-tuple-element.62), channel_id=1, source_target_pairs={{256,384},{257,385},{258,386},{259,387},{260,388},{261,389},{262,3... | collective-permute-start | bytes 307208 | tf_op jit(solution)/shard_map/ppermute | solution.py:429
  41.2 23.7 %collective-permute-done.13.refs_0_ = bf16[20,20,128]{2,1,0:T(8,128)(2,1)S(1)} collective-permute-done((bf16[20,20,128]{2,1,0:T(8,128)(2,1)S(1)}, bf16[20,20,128]{2,1,0:T(8,128)(2,1)S(1)}, u32[]{:S(2)}, u32[]{:S(2)}) %collective-permute-start.13) | collective-permute-done | bytes 102432 | tf_op jit(solution)/shard_map/ppermute | solution.py:429
  64.8 1.4 %shard_map.64 = (bf16[16,16,128]{2,1,0:T(8,128)(2,1)S(1)}, f32[576,128]{1,0:T(8,128)S(1)}, f32[512,128]{1,0:T(8,128)S(1)}) custom-call(bf16[20,20,128]{2,1,0:T(8,128)(2,1)S(1)} %collective-permute-done.13.refs_0_, f32[832,256]{1,0:T(8,128)S(1)} %get-tuple-element.50.refs_1_, f32[768,256]{1,0:T(8,128)S(1)} %get-tuple-element.51.refs_2_, ...), custom_call_target="tpu_custom_call" | custom-call | flops 754974720 | bytes 2097152 | tf_op jit(solution)/shard_map/pallas_call | solution.py:358
  66.2 2.8 %collective-permute-done.12.refs_0_ = bf16[20,20,128]{2,1,0:T(8,128)(2,1)S(1)} collective-permute-done((bf16[20,20,128]{2,1,0:T(8,128)(2,1)S(1)}, bf16[20,20,128]{2,1,0:T(8,128)(2,1)S(1)}, u32[]{:S(2)}, u32[]{:S(2)}) %collective-permute-start.12) | collective-permute-done | bytes 102432 | tf_op jit(solution)/shard_map/ppermute | solution.py:429
  69.0 1.9 %shard_map.65 = bf16[2,16,16,128]{3,2,1,0:T(8,128)(2,1)} custom-call(bf16[20,20,128]{2,1,0:T(8,128)(2,1)S(1)} %collective-permute-done.12.refs_0_, f32[576,128]{1,0:T(8,128)S(1)} %get-tuple-element.65.refs_1_, f32[512,128]{1,0:T(8,128)S(1)} %get-tuple-element.66.refs_2_, bf16[2,3,3,384,128]{4,3,2,1,0:T(8,128)(2,1)S(1)} %bitcast.13, f32[2,128]{1,0:T(2,128)S(1)} %bitcast.23, ...), custom_call_target="tpu_custom_call" | custom-call | flops 754974720 | bytes 2097152 | tf_op jit(solution)/shard_map/pallas_call | solution.py:358
  (9 shorter events, 0.2 us)
Async XLA Ops:
  0.0 30.9 %copy-start = (bf16[1,2,3,3,3,128,128]{6,5,4,3,2,1,0:T(8,128)(2,1)S(1)}, bf16[1,2,3,3,3,128,128]{6,5,4,3,2,1,0:T(8,128)(2,1)}, u32[]{:S(2)}) copy-start(bf16[1,2,3,3,3,128,128]{6,5,4,3,2,1,0:T(8,128)(2,1)} %param.7) | copy-start | bytes 5308420
  0.0 1.1 %copy-start.1 = (bf16[1,2,2,16,16,128]{5,4,3,2,1,0:T(8,128)(2,1)S(1)}, bf16[1,2,2,16,16,128]{5,4,3,2,1,0:T(8,128)(2,1)}, u32[]{:S(2)}) copy-start(bf16[1,2,2,16,16,128]{5,4,3,2,1,0:T(8,128)(2,1)} %param.6) | copy-start | bytes 786436
  1.1 0.9 %copy-start.3 = (bf16[2,16,16,128]{3,2,1,0:T(8,128)(2,1)S(1)}, bf16[2,16,16,128]{3,2,1,0:T(8,128)(2,1)}, u32[]{:S(2)}) copy-start(bf16[2,16,16,128]{3,2,1,0:T(8,128)(2,1)} %frames.1) | copy-start | bytes 393220
  2.0 28.9 %copy-start.4 = (f32[1,2,128]{2,1,0:T(2,128)S(1)}, f32[1,2,128]{2,1,0:T(2,128)}, u32[]{:S(2)}) copy-start(f32[1,2,128]{2,1,0:T(2,128)} %param.9) | copy-start | bytes 3076
  2.0 28.9 %copy-start.5 = (f32[1,2,128]{2,1,0:T(2,128)S(1)}, f32[1,2,128]{2,1,0:T(2,128)}, u32[]{:S(2)}) copy-start(f32[1,2,128]{2,1,0:T(2,128)} %param.8) | copy-start | bytes 3076
  2.4 1.4 %collective-permute-start = (bf16[6,8,16,128]{3,2,1,0:T(8,128)(2,1)S(1)}, bf16[6,8,16,128]{3,2,1,0:T(8,128)(2,1)S(1)}, u32[]{:S(2)}, u32[]{:S(2)}) collective-permute-start(bf16[6,8,16,128]{3,2,1,0:T(8,128)(2,1)S(1)} %get-tuple-element.38), channel_id=1, source_target_pairs={{0,8},{1,9},{2,10},{3,11},{4,12},{5,13},{6,14},{7,15},{8,16},{9,17... | collective-permute-start | bytes 589832 | tf_op jit(solution)/shard_map/ppermute | solution.py:429
  3.1 0.7 collective-permute-start.1
  3.9 1.4 %collective-permute-start.2 = (bf16[6,32,8,128]{3,2,1,0:T(8,128)(2,1)S(1)}, bf16[6,32,8,128]{3,2,1,0:T(8,128)(2,1)S(1)}, u32[]{:S(2)}, u32[]{:S(2)}) collective-permute-start(bf16[6,32,8,128]{3,2,1,0:T(8,128)(2,1)S(1)} %get-tuple-element.40), channel_id=1, source_target_pairs={{0,1},{1,2},{2,3},{3,4},{4,5},{5,6},{6,7},{8,9},{9,10},{10,11},{11... | collective-permute-start | bytes 1179656 | tf_op jit(solution)/shard_map/ppermute | solution.py:429
  4.6 26.2 %collective-permute-start.3 = (bf16[6,32,8,128]{3,2,1,0:T(8,128)(2,1)S(1)}, bf16[6,32,8,128]{3,2,1,0:T(8,128)(2,1)S(1)}, u32[]{:S(2)}, u32[]{:S(2)}) collective-permute-start(bf16[6,32,8,128]{3,2,1,0:T(8,128)(2,1)S(1)} %get-tuple-element.42), channel_id=1, source_target_pairs={{1,0},{2,1},{3,2},{4,3},{5,4},{6,5},{7,6},{9,8},{10,9},{11,10},{12... | collective-permute-start | bytes 1179656 | tf_op jit(solution)/shard_map/ppermute | solution.py:429
  5.4 11.1 %collective-permute-start.7 = (bf16[4,6,16,128]{3,2,1,0:T(8,128)(2,1)S(1)}, bf16[4,6,16,128]{3,2,1,0:T(8,128)(2,1)S(1)}, u32[]{:S(2)}, u32[]{:S(2)}) collective-permute-start(bf16[4,6,16,128]{3,2,1,0:T(8,128)(2,1)S(1)} %get-tuple-element.71), channel_id=1, source_target_pairs={{136,128},{137,129},{138,130},{139,131},{140,132},{141,133},{142,1... | collective-permute-start | bytes 294920 | tf_op jit(solution)/shard_map/ppermute | solution.py:429
  13.5 11.6 %collective-permute-start.6 = (bf16[4,6,16,128]{3,2,1,0:T(8,128)(2,1)S(1)}, bf16[4,6,16,128]{3,2,1,0:T(8,128)(2,1)S(1)}, u32[]{:S(2)}, u32[]{:S(2)}) collective-permute-start(bf16[4,6,16,128]{3,2,1,0:T(8,128)(2,1)S(1)} %get-tuple-element.72), channel_id=1, source_target_pairs={{128,136},{129,137},{130,138},{131,139},{132,140},{133,141},{134,1... | collective-permute-start | bytes 294920 | tf_op jit(solution)/shard_map/ppermute | solution.py:429
  25.2 7.3 %collective-permute-start.8 = (bf16[4,28,6,128]{3,2,1,0:T(8,128)(2,1)S(1)}, bf16[4,28,6,128]{3,2,1,0:T(8,128)(2,1)S(1)}, u32[]{:S(2)}, u32[]{:S(2)}) collective-permute-start(bf16[4,28,6,128]{3,2,1,0:T(8,128)(2,1)S(1)} %pad_maximum_fusion), channel_id=1, source_target_pairs={{128,129},{129,130},{130,131},{131,132},{132,133},{133,134},{134,1... | collective-permute-start | bytes 516104 | tf_op jit(solution)/shard_map/ppermute | solution.py:429
  27.2 7.2 %collective-permute-start.9 = (bf16[4,28,6,128]{3,2,1,0:T(8,128)(2,1)S(1)}, bf16[4,28,6,128]{3,2,1,0:T(8,128)(2,1)S(1)}, u32[]{:S(2)}, u32[]{:S(2)}) collective-permute-start(bf16[4,28,6,128]{3,2,1,0:T(8,128)(2,1)S(1)} %pad_maximum_fusion.1), channel_id=1, source_target_pairs={{129,128},{130,129},{131,130},{132,131},{133,132},{134,133},{135,1... | collective-permute-start | bytes 516104 | tf_op jit(solution)/shard_map/ppermute | solution.py:429
  30.9 5.9 %collective-permute-start.5 = (bf16[28,28,128]{2,1,0:T(8,128)(2,1)S(1)}, bf16[28,28,128]{2,1,0:T(8,128)(2,1)S(1)}, u32[]{:S(2)}, u32[]{:S(2)}) collective-permute-start(bf16[28,28,128]{2,1,0:T(8,128)(2,1)S(1)} %get-tuple-element.47), channel_id=1, source_target_pairs={{0,128},{1,129},{2,130},{3,131},{4,132},{5,133},{6,134},{7,135},{8... | collective-permute-start | bytes 602120 | tf_op jit(solution)/shard_map/ppermute | solution.py:429
  31.6 2.8 %copy-start.2 = (bf16[1,2,2,16,16,128]{5,4,3,2,1,0:T(8,128)(2,1)S(1)}, bf16[1,2,2,16,16,128]{5,4,3,2,1,0:T(8,128)(2,1)}, u32[]{:S(2)}) copy-start(bf16[1,2,2,16,16,128]{5,4,3,2,1,0:T(8,128)(2,1)} %param.6) | copy-start | bytes 786436
  31.7 5.9 %collective-permute-start.4 = (bf16[28,28,128]{2,1,0:T(8,128)(2,1)S(1)}, bf16[28,28,128]{2,1,0:T(8,128)(2,1)S(1)}, u32[]{:S(2)}, u32[]{:S(2)}) collective-permute-start(bf16[28,28,128]{2,1,0:T(8,128)(2,1)S(1)} %get-tuple-element.46), channel_id=1, source_target_pairs={{0,128},{1,129},{2,130},{3,131},{4,132},{5,133},{6,134},{7,135},{8... | collective-permute-start | bytes 602120 | tf_op jit(solution)/shard_map/ppermute | solution.py:429
  36.9 1.4 %collective-permute-start.11 = (bf16[24,24,128]{2,1,0:T(8,128)(2,1)S(1)}, bf16[24,24,128]{2,1,0:T(8,128)(2,1)S(1)}, u32[]{:S(2)}, u32[]{:S(2)}) collective-permute-start(bf16[24,24,128]{2,1,0:T(8,128)(2,1)S(1)} %get-tuple-element.57), channel_id=1, source_target_pairs={{128,256},{129,257},{130,258},{131,259},{132,260},{133,261},{134,2... | collective-permute-start | bytes 442376 | tf_op jit(solution)/shard_map/ppermute | solution.py:429
  37.6 2.2 %collective-permute-start.10 = (bf16[24,24,128]{2,1,0:T(8,128)(2,1)S(1)}, bf16[24,24,128]{2,1,0:T(8,128)(2,1)S(1)}, u32[]{:S(2)}, u32[]{:S(2)}) collective-permute-start(bf16[24,24,128]{2,1,0:T(8,128)(2,1)S(1)} %get-tuple-element.56), channel_id=1, source_target_pairs={{128,256},{129,257},{130,258},{131,259},{132,260},{133,261},{134,2... | collective-permute-start | bytes 442376 | tf_op jit(solution)/shard_map/ppermute | solution.py:429
  38.5 26.3 %collective-permute-start.13 = (bf16[20,20,128]{2,1,0:T(8,128)(2,1)S(1)}, bf16[20,20,128]{2,1,0:T(8,128)(2,1)S(1)}, u32[]{:S(2)}, u32[]{:S(2)}) collective-permute-start(bf16[20,20,128]{2,1,0:T(8,128)(2,1)S(1)} %get-tuple-element.63), channel_id=1, source_target_pairs={{256,384},{257,385},{258,386},{259,387},{260,388},{261,389},{262,3... | collective-permute-start | bytes 307208 | tf_op jit(solution)/shard_map/ppermute | solution.py:429
  39.9 29.1 %collective-permute-start.12 = (bf16[20,20,128]{2,1,0:T(8,128)(2,1)S(1)}, bf16[20,20,128]{2,1,0:T(8,128)(2,1)S(1)}, u32[]{:S(2)}, u32[]{:S(2)}) collective-permute-start(bf16[20,20,128]{2,1,0:T(8,128)(2,1)S(1)} %get-tuple-element.62), channel_id=1, source_target_pairs={{256,384},{257,385},{258,386},{259,387},{260,388},{261,389},{262,3... | collective-permute-start | bytes 307208 | tf_op jit(solution)/shard_map/ppermute | solution.py:429

commit v5 on v4

--- a/solution.py
+++ b/solution.py
@@ -19,8 +19,8 @@
     return (half + half * jnp.tanh(half)) * mask
 
 
-def chunks(rows):
-    return [(first, min(CHUNK, rows - first)) for first in range(0, rows, CHUNK)]
+def chunks(rows, size=CHUNK):
+    return [(first, min(size, rows - first)) for first in range(0, rows, size)]
 
 
 def column_mask(side, width, channels):
@@ -65,14 +65,10 @@
 
 def convolve(patches, kernel, sides, total, first, rows):
     count = rows * PITCH
-    for tap in range(3):
-        begin = (first + tap) * PITCH
-        total = total + jnp.dot(
-            patches[begin : begin + count, :],
-            weight_rows(kernel, tap, sides),
-            preferred_element_type=jnp.float32,
-        )
-    return total
+    starts = [(first + tap) * PITCH for tap in range(3)]
+    cells = jnp.concatenate([patches[begin : begin + count, :] for begin in starts], axis=1)
+    weight = jnp.concatenate([weight_rows(kernel, tap, sides) for tap in range(3)], axis=0)
+    return total + jnp.dot(cells, weight, preferred_element_type=jnp.float32)
 
 
 def bias_of(bias, count):
@@ -99,20 +95,20 @@
         ].astype(jnp.float32)
 
 
-def normed(margin, height, width, values_of, gain, flat, rows, span):
+def normed(margin, height, width, values_of, gain, flat, rows, span, size):
     channels = gain.shape[-1]
     tile = span - 2 * margin
     top = lax.axis_index("row") * tile - margin
     columns = column_mask(lax.axis_index("col") * tile - margin, width, channels)
     half_gain = 0.5 * gain
-    for first, count in chunks(rows):
+    for first, count in chunks(rows, size):
         keep = cell_mask(columns, top, height, first, count)
         flat[first * PITCH : (first + count) * PITCH, :] = norm_act(
             values_of(first, count), half_gain, keep
         )
 
 
-def body(halo, height, width, g_ref, held, flat, patches, fill, hidden_of, branch_of, o_ref):
+def body(halo, height, width, g_ref, held, flat, patches, fill, hidden_of, branch_of, o_ref, size):
     span = o_ref.shape[0] + 4
     blocks = patches.shape[1] // (3 * held.shape[-1])
 
@@ -121,16 +117,16 @@
 
     normed(
         halo, height, width, lambda first, count: area(held, first, count),
-        g_ref[0:1, :], flat, span, span,
+        g_ref[0:1, :], flat, span, span, size,
     )
     fill(0)
     spread(flat, 0, patches, blocks - 1, span)
     normed(
-        halo - 1, height, width, hidden_of, g_ref[1:2, :], flat, span - 2, span - 2
+        halo - 1, height, width, hidden_of, g_ref[1:2, :], flat, span - 2, span - 2, size
     )
     fill(1)
     spread(flat, 0, patches, blocks - 1, span - 2)
-    for first, count in chunks(span - 4):
+    for first, count in chunks(span - 4, size):
         offset = (first + 2) * PITCH + 2
         out = held[offset : offset + count * PITCH, :] + branch_of(first, count)
         for row in range(count):
@@ -194,7 +190,7 @@
 
     body(
         halo, height, width, g_ref, grid.at[0], flat, patches, fill,
-        conv_of(0, one_ref), conv_of(1, two_ref), o_ref,
+        conv_of(0, one_ref), conv_of(1, two_ref), o_ref, 10,
     )
     keep_tile(o_ref, r_ref)
 
@@ -218,7 +214,7 @@
     assemble(held, 1, mid, low, high, left, right)
     body(
         halo, height, width, g_ref, held, flat, patches, nothing,
-        late_of(patches, w_ref, 0, one_ref), late_of(patches, w_ref, 1, two_ref), o_ref,
+        late_of(patches, w_ref, 0, one_ref), late_of(patches, w_ref, 1, two_ref), o_ref, 4,
     )
     keep_tile(o_ref, r_ref)
 
@@ -276,7 +272,7 @@
 
     body(
         halo, height, width, g_ref, held, flat, patches, nothing,
-        conv_of(0, known_one, one_ref), conv_of(1, known_two, two_ref), o_ref,
+        conv_of(0, known_one, one_ref), conv_of(1, known_two, two_ref), o_ref, CHUNK,
     )
     keep_tile(o_ref, r_ref)
 
@@ -288,7 +284,7 @@
     load_rows(x_ref, held)
     body(
         halo, height, width, g_ref, held, flat, patches, nothing,
-        late_of(patches, w_ref, 0, one_ref), late_of(patches, w_ref, 1, two_ref), o_ref,
+        late_of(patches, w_ref, 0, one_ref), late_of(patches, w_ref, 1, two_ref), o_ref, 4,
     )
     keep_tile(o_ref, r_ref)
 
@@ -400,7 +396,7 @@
         out_specs=[WHOLE] * 3,
         scratch_shapes=[pltpu.SemaphoreType.DMA((6,))],
         compiler_params=pltpu.CompilerParams(vmem_limit_bytes=PACK_ROOM),
-    )(frames, cached)
+    )(*(pltpu.with_memory_space_constraint(part, pltpu.HBM) for part in (frames, cached)))
 
 
 def cut_sides(mid, low, high):

time: 71.2 us -> 69.8 us (0.980)
  local copies, waits for them, and re-layouts: 2.12 us -> 0.13 us
  Pallas kernels: 6.61 us -> 7.44 us
    unnamed x12 -> x8, local copies, waits for them, and re-layouts: 2 us -> 0.02 us
    pallas_call x1, Pallas kernels: 0.41 us -> 1.38 us  [packed(): pl.pallas_call(pack_kernel, out_shape=[shaped(*tile), shaped(*shape), sha...]
where the time goes in v5:
time: 69.8 us; the launch traced here: 69.4 us
  waiting for transfers between devices  37.6 us (54%)
  starting transfers between devices  23.8 us (34%)
  Pallas kernels  7.44 us (11%)
    ppermute x14, waiting for transfers between devices, moved(): return lax.ppermute(value, AXES, pairs)  37.6 us
    ppermute x14, starting transfers between devices, moved(): return lax.ppermute(value, AXES, pairs)  23.8 us
    pallas_call x9, Pallas kernels, launch(): pl.pallas_call(kernel, out_shape=outs, in_specs=[WHOLE] * len(arguments),...  5.92 us
  transfers between devices with their start and end apart: 14, of which 6 were waited for; matrix products, arithmetic and copies ran while one was open for 0% of the time, Pallas kernels for 6%

profile of v5, /device:TPU:210, one launch (start us, length us, event | category | flops | bytes accessed | tf_op | source)
XLA Modules:
  0.0 69.4 jit_solution(6581335237969664285)
XLA Ops:
  0.0 0.0 copy-start
  0.0 0.0 copy-start.2
  0.0 0.0 copy-start.3
  0.0 1.4 %shard_map.55 = (bf16[6,16,16,128]{3,2,1,0:T(8,128)(2,1)S(1)}, bf16[6,8,16,128]{3,2,1,0:T(8,128)(2,1)S(1)}, bf16[6,8,16,128]{3,2,1,0:T(8,128)(2,1)S(1)}) custom-call(bf16[2,16,16,128]{3,2,1,0:T(8,128)(2,1)} %frames.1, bf16[4,16,16,128]{3,2,1,0:T(8,128)(2,1)} %bitcast.14), custom_call_target="tpu_custom_call" | custom-call | tf_op jit(solution)/shard_map/pallas_call | solution.py:392
  1.4 0.7 collective-permute-start
  2.1 0.7 collective-permute-start.1
  2.8 0.0 collective-permute-done.low.refs_1_
  2.8 0.0 collective-permute-done.1.high.refs_2_
  2.8 0.1 shard_map.56
  2.9 0.7 collective-permute-start.2
  3.6 0.7 collective-permute-start.3
  4.3 0.0 collective-permute-done.2.refs_3_
  4.4 8.1 %collective-permute-start.7 = (bf16[4,6,16,128]{3,2,1,0:T(8,128)(2,1)S(1)}, bf16[4,6,16,128]{3,2,1,0:T(8,128)(2,1)S(1)}, u32[]{:S(2)}, u32[]{:S(2)}) collective-permute-start(bf16[4,6,16,128]{3,2,1,0:T(8,128)(2,1)S(1)} %get-tuple-element.71), channel_id=1, source_target_pairs={{136,128},{137,129},{138,130},{139,131},{140,132},{141,133},{142,1... | collective-permute-start | bytes 294920 | tf_op jit(solution)/shard_map/ppermute | solution.py:425
  12.5 0.1 fusion
  12.5 2.0 %collective-permute-start.6 = (bf16[4,6,16,128]{3,2,1,0:T(8,128)(2,1)S(1)}, bf16[4,6,16,128]{3,2,1,0:T(8,128)(2,1)S(1)}, u32[]{:S(2)}, u32[]{:S(2)}) collective-permute-start(bf16[4,6,16,128]{3,2,1,0:T(8,128)(2,1)S(1)} %get-tuple-element.72), channel_id=1, source_target_pairs={{128,136},{129,137},{130,138},{131,139},{132,140},{133,141},{134,1... | collective-permute-start | bytes 294920 | tf_op jit(solution)/shard_map/ppermute | solution.py:425
  14.6 0.9 %collective-permute-done.7.high = bf16[4,6,16,128]{3,2,1,0:T(8,128)(2,1)S(1)} collective-permute-done((bf16[4,6,16,128]{3,2,1,0:T(8,128)(2,1)S(1)}, bf16[4,6,16,128]{3,2,1,0:T(8,128)(2,1)S(1)}, u32[]{:S(2)}, u32[]{:S(2)}) %collective-permute-start.7) | collective-permute-done | bytes 98336 | tf_op jit(solution)/shard_map/ppermute | solution.py:425
  15.5 8.6 %collective-permute-done.6.low = bf16[4,6,16,128]{3,2,1,0:T(8,128)(2,1)S(1)} collective-permute-done((bf16[4,6,16,128]{3,2,1,0:T(8,128)(2,1)S(1)}, bf16[4,6,16,128]{3,2,1,0:T(8,128)(2,1)S(1)}, u32[]{:S(2)}, u32[]{:S(2)}) %collective-permute-start.6) | collective-permute-done | bytes 98336 | tf_op jit(solution)/shard_map/ppermute | solution.py:425
  24.2 0.1 pad_maximum_fusion
  24.2 1.9 %collective-permute-start.8 = (bf16[4,28,6,128]{3,2,1,0:T(8,128)(2,1)S(1)}, bf16[4,28,6,128]{3,2,1,0:T(8,128)(2,1)S(1)}, u32[]{:S(2)}, u32[]{:S(2)}) collective-permute-start(bf16[4,28,6,128]{3,2,1,0:T(8,128)(2,1)S(1)} %pad_maximum_fusion), channel_id=1, source_target_pairs={{128,129},{129,130},{130,131},{131,132},{132,133},{133,134},{134,1... | collective-permute-start | bytes 516104 | tf_op jit(solution)/shard_map/ppermute | solution.py:425
  26.2 0.1 pad_maximum_fusion.1
  26.2 3.6 %collective-permute-start.9 = (bf16[4,28,6,128]{3,2,1,0:T(8,128)(2,1)S(1)}, bf16[4,28,6,128]{3,2,1,0:T(8,128)(2,1)S(1)}, u32[]{:S(2)}, u32[]{:S(2)}) collective-permute-start(bf16[4,28,6,128]{3,2,1,0:T(8,128)(2,1)S(1)} %pad_maximum_fusion.1), channel_id=1, source_target_pairs={{129,128},{130,129},{131,130},{132,131},{133,132},{134,133},{135,1... | collective-permute-start | bytes 516104 | tf_op jit(solution)/shard_map/ppermute | solution.py:425
  29.9 0.0 collective-permute-done.3.refs_4_
  29.9 0.0 copy-done
  29.9 0.0 copy-done.2
  29.9 0.0 copy-done.3
  29.9 0.7 collective-permute-start.5
  30.6 0.0 copy-start.1
  30.7 0.8 %collective-permute-start.4 = (bf16[28,28,128]{2,1,0:T(8,128)(2,1)S(1)}, bf16[28,28,128]{2,1,0:T(8,128)(2,1)S(1)}, u32[]{:S(2)}, u32[]{:S(2)}) collective-permute-start(bf16[28,28,128]{2,1,0:T(8,128)(2,1)S(1)} %get-tuple-element.46), channel_id=1, source_target_pairs={{0,128},{1,129},{2,130},{3,131},{4,132},{5,133},{6,134},{7,135},{8... | collective-permute-start | bytes 602120 | tf_op jit(solution)/shard_map/ppermute | solution.py:425
  31.5 0.1 collective-permute-done.8.left
  31.6 1.8 %collective-permute-done.9.right = bf16[4,28,6,128]{3,2,1,0:T(8,128)(2,1)S(1)} collective-permute-done((bf16[4,28,6,128]{3,2,1,0:T(8,128)(2,1)S(1)}, bf16[4,28,6,128]{3,2,1,0:T(8,128)(2,1)S(1)}, u32[]{:S(2)}, u32[]{:S(2)}) %collective-permute-start.9) | collective-permute-done | bytes 172064 | tf_op jit(solution)/shard_map/ppermute | solution.py:425
  33.4 0.0 copy-done.1
  33.4 2.6 %shard_map.59 = (f32[832,256]{1,0:T(8,128)S(1)}, f32[768,256]{1,0:T(8,128)S(1)}) custom-call(bf16[4,16,16,128]{3,2,1,0:T(8,128)(2,1)S(1)} %bitcast.15, bf16[4,6,16,128]{3,2,1,0:T(8,128)(2,1)S(1)} %collective-permute-done.6.low, bf16[4,6,16,128]{3,2,1,0:T(8,128)(2,1)S(1)} %collective-permute-done.7.high, ...), custom_call_target="tpu_custom_call" | custom-call | flops 2113929216 | bytes 2097152 | tf_op jit(solution)/shard_map/pallas_call | solution.py:354
  36.0 0.0 collective-permute-done.5.refs_0_
  36.0 0.7 collective-permute-start.11
  36.7 0.0 collective-permute-done.4.refs_0_
  36.7 0.7 collective-permute-start.10
  37.4 0.0 collective-permute-done.11.refs_0_
  37.4 0.2 shard_map.62
  37.6 1.3 %collective-permute-start.13 = (bf16[20,20,128]{2,1,0:T(8,128)(2,1)S(1)}, bf16[20,20,128]{2,1,0:T(8,128)(2,1)S(1)}, u32[]{:S(2)}, u32[]{:S(2)}) collective-permute-start(bf16[20,20,128]{2,1,0:T(8,128)(2,1)S(1)} %get-tuple-element.63), channel_id=1, source_target_pairs={{256,384},{257,385},{258,386},{259,387},{260,388},{261,389},{262,3... | collective-permute-start | bytes 307208 | tf_op jit(solution)/shard_map/ppermute | solution.py:425
  38.9 0.0 collective-permute-done.10.refs_0_
  39.0 1.3 %collective-permute-start.12 = (bf16[20,20,128]{2,1,0:T(8,128)(2,1)S(1)}, bf16[20,20,128]{2,1,0:T(8,128)(2,1)S(1)}, u32[]{:S(2)}, u32[]{:S(2)}) collective-permute-start(bf16[20,20,128]{2,1,0:T(8,128)(2,1)S(1)} %get-tuple-element.62), channel_id=1, source_target_pairs={{256,384},{257,385},{258,386},{259,387},{260,388},{261,389},{262,3... | collective-permute-start | bytes 307208 | tf_op jit(solution)/shard_map/ppermute | solution.py:425
  40.3 23.1 %collective-permute-done.13.refs_0_ = bf16[20,20,128]{2,1,0:T(8,128)(2,1)S(1)} collective-permute-done((bf16[20,20,128]{2,1,0:T(8,128)(2,1)S(1)}, bf16[20,20,128]{2,1,0:T(8,128)(2,1)S(1)}, u32[]{:S(2)}, u32[]{:S(2)}) %collective-permute-start.13) | collective-permute-done | bytes 102432 | tf_op jit(solution)/shard_map/ppermute | solution.py:425
  63.4 1.3 %shard_map.64 = (bf16[16,16,128]{2,1,0:T(8,128)(2,1)S(1)}, f32[576,128]{1,0:T(8,128)S(1)}, f32[512,128]{1,0:T(8,128)S(1)}) custom-call(bf16[20,20,128]{2,1,0:T(8,128)(2,1)S(1)} %collective-permute-done.13.refs_0_, f32[832,256]{1,0:T(8,128)S(1)} %get-tuple-element.50.refs_1_, f32[768,256]{1,0:T(8,128)S(1)} %get-tuple-element.51.refs_2_, ...), custom_call_target="tpu_custom_call" | custom-call | flops 754974720 | bytes 2097152 | tf_op jit(solution)/shard_map/pallas_call | solution.py:354
  64.7 3.0 %collective-permute-done.12.refs_0_ = bf16[20,20,128]{2,1,0:T(8,128)(2,1)S(1)} collective-permute-done((bf16[20,20,128]{2,1,0:T(8,128)(2,1)S(1)}, bf16[20,20,128]{2,1,0:T(8,128)(2,1)S(1)}, u32[]{:S(2)}, u32[]{:S(2)}) %collective-permute-start.12) | collective-permute-done | bytes 102432 | tf_op jit(solution)/shard_map/ppermute | solution.py:425
  67.7 1.7 %shard_map.65 = bf16[2,16,16,128]{3,2,1,0:T(8,128)(2,1)} custom-call(bf16[20,20,128]{2,1,0:T(8,128)(2,1)S(1)} %collective-permute-done.12.refs_0_, f32[576,128]{1,0:T(8,128)S(1)} %get-tuple-element.65.refs_1_, f32[512,128]{1,0:T(8,128)S(1)} %get-tuple-element.66.refs_2_, bf16[2,3,3,384,128]{4,3,2,1,0:T(8,128)(2,1)S(1)} %bitcast.13, f32[2,128]{1,0:T(2,128)S(1)} %bitcast.23, ...), custom_call_target="tpu_custom_call" | custom-call | flops 754974720 | bytes 2097152 | tf_op jit(solution)/shard_map/pallas_call | solution.py:354
  (8 shorter events, 0.2 us)
Async XLA Ops:
  0.0 29.9 %copy-start = (bf16[1,2,3,3,3,128,128]{6,5,4,3,2,1,0:T(8,128)(2,1)S(1)}, bf16[1,2,3,3,3,128,128]{6,5,4,3,2,1,0:T(8,128)(2,1)}, u32[]{:S(2)}) copy-start(bf16[1,2,3,3,3,128,128]{6,5,4,3,2,1,0:T(8,128)(2,1)} %param.7) | copy-start | bytes 5308420
  0.0 29.9 %copy-start.2 = (f32[1,2,128]{2,1,0:T(2,128)S(1)}, f32[1,2,128]{2,1,0:T(2,128)}, u32[]{:S(2)}) copy-start(f32[1,2,128]{2,1,0:T(2,128)} %param.9) | copy-start | bytes 3076
  0.0 29.9 %copy-start.3 = (f32[1,2,128]{2,1,0:T(2,128)S(1)}, f32[1,2,128]{2,1,0:T(2,128)}, u32[]{:S(2)}) copy-start(f32[1,2,128]{2,1,0:T(2,128)} %param.8) | copy-start | bytes 3076
  1.4 1.4 %collective-permute-start = (bf16[6,8,16,128]{3,2,1,0:T(8,128)(2,1)S(1)}, bf16[6,8,16,128]{3,2,1,0:T(8,128)(2,1)S(1)}, u32[]{:S(2)}, u32[]{:S(2)}) collective-permute-start(bf16[6,8,16,128]{3,2,1,0:T(8,128)(2,1)S(1)} %get-tuple-element.38), channel_id=1, source_target_pairs={{0,8},{1,9},{2,10},{3,11},{4,12},{5,13},{6,14},{7,15},{8,16},{9,17... | collective-permute-start | bytes 589832 | tf_op jit(solution)/shard_map/ppermute | solution.py:425
  2.1 0.7 collective-permute-start.1
  2.9 1.4 %collective-permute-start.2 = (bf16[6,32,8,128]{3,2,1,0:T(8,128)(2,1)S(1)}, bf16[6,32,8,128]{3,2,1,0:T(8,128)(2,1)S(1)}, u32[]{:S(2)}, u32[]{:S(2)}) collective-permute-start(bf16[6,32,8,128]{3,2,1,0:T(8,128)(2,1)S(1)} %get-tuple-element.40), channel_id=1, source_target_pairs={{0,1},{1,2},{2,3},{3,4},{4,5},{5,6},{6,7},{8,9},{9,10},{10,11},{11... | collective-permute-start | bytes 1179656 | tf_op jit(solution)/shard_map/ppermute | solution.py:425
  3.6 26.2 %collective-permute-start.3 = (bf16[6,32,8,128]{3,2,1,0:T(8,128)(2,1)S(1)}, bf16[6,32,8,128]{3,2,1,0:T(8,128)(2,1)S(1)}, u32[]{:S(2)}, u32[]{:S(2)}) collective-permute-start(bf16[6,32,8,128]{3,2,1,0:T(8,128)(2,1)S(1)} %get-tuple-element.42), channel_id=1, source_target_pairs={{1,0},{2,1},{3,2},{4,3},{5,4},{6,5},{7,6},{9,8},{10,9},{11,10},{12... | collective-permute-start | bytes 1179656 | tf_op jit(solution)/shard_map/ppermute | solution.py:425
  4.4 11.1 %collective-permute-start.7 = (bf16[4,6,16,128]{3,2,1,0:T(8,128)(2,1)S(1)}, bf16[4,6,16,128]{3,2,1,0:T(8,128)(2,1)S(1)}, u32[]{:S(2)}, u32[]{:S(2)}) collective-permute-start(bf16[4,6,16,128]{3,2,1,0:T(8,128)(2,1)S(1)} %get-tuple-element.71), channel_id=1, source_target_pairs={{136,128},{137,129},{138,130},{139,131},{140,132},{141,133},{142,1... | collective-permute-start | bytes 294920 | tf_op jit(solution)/shard_map/ppermute | solution.py:425
  12.5 11.6 %collective-permute-start.6 = (bf16[4,6,16,128]{3,2,1,0:T(8,128)(2,1)S(1)}, bf16[4,6,16,128]{3,2,1,0:T(8,128)(2,1)S(1)}, u32[]{:S(2)}, u32[]{:S(2)}) collective-permute-start(bf16[4,6,16,128]{3,2,1,0:T(8,128)(2,1)S(1)} %get-tuple-element.72), channel_id=1, source_target_pairs={{128,136},{129,137},{130,138},{131,139},{132,140},{133,141},{134,1... | collective-permute-start | bytes 294920 | tf_op jit(solution)/shard_map/ppermute | solution.py:425
  24.2 7.3 %collective-permute-start.8 = (bf16[4,28,6,128]{3,2,1,0:T(8,128)(2,1)S(1)}, bf16[4,28,6,128]{3,2,1,0:T(8,128)(2,1)S(1)}, u32[]{:S(2)}, u32[]{:S(2)}) collective-permute-start(bf16[4,28,6,128]{3,2,1,0:T(8,128)(2,1)S(1)} %pad_maximum_fusion), channel_id=1, source_target_pairs={{128,129},{129,130},{130,131},{131,132},{132,133},{133,134},{134,1... | collective-permute-start | bytes 516104 | tf_op jit(solution)/shard_map/ppermute | solution.py:425
  26.2 7.2 %collective-permute-start.9 = (bf16[4,28,6,128]{3,2,1,0:T(8,128)(2,1)S(1)}, bf16[4,28,6,128]{3,2,1,0:T(8,128)(2,1)S(1)}, u32[]{:S(2)}, u32[]{:S(2)}) collective-permute-start(bf16[4,28,6,128]{3,2,1,0:T(8,128)(2,1)S(1)} %pad_maximum_fusion.1), channel_id=1, source_target_pairs={{129,128},{130,129},{131,130},{132,131},{133,132},{134,133},{135,1... | collective-permute-start | bytes 516104 | tf_op jit(solution)/shard_map/ppermute | solution.py:425
  29.9 6.0 %collective-permute-start.5 = (bf16[28,28,128]{2,1,0:T(8,128)(2,1)S(1)}, bf16[28,28,128]{2,1,0:T(8,128)(2,1)S(1)}, u32[]{:S(2)}, u32[]{:S(2)}) collective-permute-start(bf16[28,28,128]{2,1,0:T(8,128)(2,1)S(1)} %get-tuple-element.47), channel_id=1, source_target_pairs={{0,128},{1,129},{2,130},{3,131},{4,132},{5,133},{6,134},{7,135},{8... | collective-permute-start | bytes 602120 | tf_op jit(solution)/shard_map/ppermute | solution.py:425
  30.6 2.8 %copy-start.1 = (bf16[1,2,2,16,16,128]{5,4,3,2,1,0:T(8,128)(2,1)S(1)}, bf16[1,2,2,16,16,128]{5,4,3,2,1,0:T(8,128)(2,1)}, u32[]{:S(2)}) copy-start(bf16[1,2,2,16,16,128]{5,4,3,2,1,0:T(8,128)(2,1)} %param.6) | copy-start | bytes 786436
  30.7 6.0 %collective-permute-start.4 = (bf16[28,28,128]{2,1,0:T(8,128)(2,1)S(1)}, bf16[28,28,128]{2,1,0:T(8,128)(2,1)S(1)}, u32[]{:S(2)}, u32[]{:S(2)}) collective-permute-start(bf16[28,28,128]{2,1,0:T(8,128)(2,1)S(1)} %get-tuple-element.46), channel_id=1, source_target_pairs={{0,128},{1,129},{2,130},{3,131},{4,132},{5,133},{6,134},{7,135},{8... | collective-permute-start | bytes 602120 | tf_op jit(solution)/shard_map/ppermute | solution.py:425
  36.0 1.4 %collective-permute-start.11 = (bf16[24,24,128]{2,1,0:T(8,128)(2,1)S(1)}, bf16[24,24,128]{2,1,0:T(8,128)(2,1)S(1)}, u32[]{:S(2)}, u32[]{:S(2)}) collective-permute-start(bf16[24,24,128]{2,1,0:T(8,128)(2,1)S(1)} %get-tuple-element.57), channel_id=1, source_target_pairs={{128,256},{129,257},{130,258},{131,259},{132,260},{133,261},{134,2... | collective-permute-start | bytes 442376 | tf_op jit(solution)/shard_map/ppermute | solution.py:425
  36.7 2.2 %collective-permute-start.10 = (bf16[24,24,128]{2,1,0:T(8,128)(2,1)S(1)}, bf16[24,24,128]{2,1,0:T(8,128)(2,1)S(1)}, u32[]{:S(2)}, u32[]{:S(2)}) collective-permute-start(bf16[24,24,128]{2,1,0:T(8,128)(2,1)S(1)} %get-tuple-element.56), channel_id=1, source_target_pairs={{128,256},{129,257},{130,258},{131,259},{132,260},{133,261},{134,2... | collective-permute-start | bytes 442376 | tf_op jit(solution)/shard_map/ppermute | solution.py:425
  37.6 25.8 %collective-permute-start.13 = (bf16[20,20,128]{2,1,0:T(8,128)(2,1)S(1)}, bf16[20,20,128]{2,1,0:T(8,128)(2,1)S(1)}, u32[]{:S(2)}, u32[]{:S(2)}) collective-permute-start(bf16[20,20,128]{2,1,0:T(8,128)(2,1)S(1)} %get-tuple-element.63), channel_id=1, source_target_pairs={{256,384},{257,385},{258,386},{259,387},{260,388},{261,389},{262,3... | collective-permute-start | bytes 307208 | tf_op jit(solution)/shard_map/ppermute | solution.py:425
  39.0 28.8 %collective-permute-start.12 = (bf16[20,20,128]{2,1,0:T(8,128)(2,1)S(1)}, bf16[20,20,128]{2,1,0:T(8,128)(2,1)S(1)}, u32[]{:S(2)}, u32[]{:S(2)}) collective-permute-start(bf16[20,20,128]{2,1,0:T(8,128)(2,1)S(1)} %get-tuple-element.62), channel_id=1, source_target_pairs={{256,384},{257,385},{258,386},{259,387},{260,388},{261,389},{262,3... | collective-permute-start | bytes 307208 | tf_op jit(solution)/shard_map/ppermute | solution.py:425

commit v6 on v5

--- a/solution.py
+++ b/solution.py
@@ -8,6 +8,12 @@
 from jax.sharding import PartitionSpec as P
 
 PITCH = 32
+
+
+def pitch_of(span):
+    return -(-span // 8) * 8
+
+
 PACK_ROOM = 4 << 20
 CHUNK = 8
 AXES = ("segment", "row", "col")
@@ -23,8 +29,8 @@
     return [(first, min(size, rows - first)) for first in range(0, rows, size)]
 
 
-def column_mask(side, width, channels):
-    col = lax.broadcasted_iota(jnp.int32, (PITCH, channels), 0) + side
+def column_mask(side, width, channels, pitch):
+    col = lax.broadcasted_iota(jnp.int32, (pitch, channels), 0) + side
     return jnp.where((col >= 0) & (col < width), 1.0, 0.0)
 
 
@@ -36,13 +42,13 @@
     return jnp.concatenate(parts, axis=0)
 
 
-def spread(source, start, patches, block, rows):
+def spread(source, start, patches, block, rows, pitch):
     channels = source.shape[-1]
     for tap in range(3):
         lane = (block * 3 + tap) * channels
         begin = start + tap
-        patches[: rows * PITCH, lane : lane + channels] = source[
-            begin : begin + rows * PITCH, :
+        patches[: rows * pitch, lane : lane + channels] = source[
+            begin : begin + rows * pitch, :
         ].astype(jnp.bfloat16)
 
 
@@ -63,9 +69,9 @@
 LATE = ((2,),)
 
 
-def convolve(patches, kernel, sides, total, first, rows):
-    count = rows * PITCH
-    starts = [(first + tap) * PITCH for tap in range(3)]
+def convolve(patches, kernel, sides, total, first, rows, pitch):
+    count = rows * pitch
+    starts = [(first + tap) * pitch for tap in range(3)]
     cells = jnp.concatenate([patches[begin : begin + count, :] for begin in starts], axis=1)
     weight = jnp.concatenate([weight_rows(kernel, tap, sides) for tap in range(3)], axis=0)
     return total + jnp.dot(cells, weight, preferred_element_type=jnp.float32)
@@ -95,50 +101,51 @@
         ].astype(jnp.float32)
 
 
-def normed(margin, height, width, values_of, gain, flat, rows, span, size):
+def normed(margin, height, width, values_of, gain, flat, rows, span, size, pitch):
     channels = gain.shape[-1]
     tile = span - 2 * margin
     top = lax.axis_index("row") * tile - margin
-    columns = column_mask(lax.axis_index("col") * tile - margin, width, channels)
+    columns = column_mask(lax.axis_index("col") * tile - margin, width, channels, pitch)
     half_gain = 0.5 * gain
     for first, count in chunks(rows, size):
         keep = cell_mask(columns, top, height, first, count)
-        flat[first * PITCH : (first + count) * PITCH, :] = norm_act(
+        flat[first * pitch : (first + count) * pitch, :] = norm_act(
             values_of(first, count), half_gain, keep
         )
 
 
 def body(halo, height, width, g_ref, held, flat, patches, fill, hidden_of, branch_of, o_ref, size):
     span = o_ref.shape[0] + 4
+    pitch = pitch_of(span)
     blocks = patches.shape[1] // (3 * held.shape[-1])
 
     def area(ref, first, count):
-        return ref[first * PITCH : (first + count) * PITCH, :]
+        return ref[first * pitch : (first + count) * pitch, :]
 
     normed(
         halo, height, width, lambda first, count: area(held, first, count),
-        g_ref[0:1, :], flat, span, span, size,
+        g_ref[0:1, :], flat, span, span, size, pitch,
     )
     fill(0)
-    spread(flat, 0, patches, blocks - 1, span)
+    spread(flat, 0, patches, blocks - 1, span, pitch)
     normed(
-        halo - 1, height, width, hidden_of, g_ref[1:2, :], flat, span - 2, span - 2, size
+        halo - 1, height, width, hidden_of, g_ref[1:2, :], flat, span - 2, span - 2, size, pitch,
     )
     fill(1)
-    spread(flat, 0, patches, blocks - 1, span - 2)
+    spread(flat, 0, patches, blocks - 1, span - 2, pitch)
     for first, count in chunks(span - 4, size):
-        offset = (first + 2) * PITCH + 2
-        out = held[offset : offset + count * PITCH, :] + branch_of(first, count)
+        offset = (first + 2) * pitch + 2
+        out = held[offset : offset + count * pitch, :] + branch_of(first, count)
         for row in range(count):
-            o_ref[first + row] = out[row * PITCH : row * PITCH + span - 4].astype(
+            o_ref[first + row] = out[row * pitch : row * pitch + span - 4].astype(
                 jnp.bfloat16
             )
 
 
-def split_off(part):
+def split_off(part, pitch):
     def apply(total, first, count):
         channels = part.shape[-1]
-        part[first * PITCH : (first + count) * PITCH, :] = total[:, channels:]
+        part[first * pitch : (first + count) * pitch, :] = total[:, channels:]
         return total[:, :channels]
 
     return apply
@@ -177,14 +184,14 @@
         for frame in range(2):
             spread(
                 grid.at[1 + 2 * conv + frame], conv * (PITCH + 1), patches, frame,
-                span - 2 * conv,
+                span - 2 * conv, PITCH,
             )
 
     def conv_of(conv, part):
         def run(first, count):
             bias = bias_of(b_ref[conv : conv + 1, :], count * PITCH)
-            total = convolve(patches, w_ref.at[conv], OPENING, bias, first, count)
-            return split_off(part)(total, first, count)
+            total = convolve(patches, w_ref.at[conv], OPENING, bias, first, count, PITCH)
+            return split_off(part, PITCH)(total, first, count)
 
         return run
 
@@ -199,10 +206,12 @@
     del conv
 
 
-def late_of(patches, w_ref, conv, part):
+def late_of(patches, w_ref, conv, part, span):
+    pitch = pitch_of(span)
+
     def run(first, count):
-        known = part[first * PITCH : (first + count) * PITCH, :]
-        return convolve(patches, w_ref.at[conv], LATE, known, first, count)
+        known = part[first * pitch : (first + count) * pitch, :]
+        return convolve(patches, w_ref.at[conv], LATE, known, first, count, pitch)
 
     return run
 
@@ -214,7 +223,8 @@
     assemble(held, 1, mid, low, high, left, right)
     body(
         halo, height, width, g_ref, held, flat, patches, nothing,
-        late_of(patches, w_ref, 0, one_ref), late_of(patches, w_ref, 1, two_ref), o_ref, 4,
+        late_of(patches, w_ref, 0, one_ref, o_ref.shape[0] + 4),
+        late_of(patches, w_ref, 1, two_ref, o_ref.shape[0] + 4), o_ref, 4,
     )
     keep_tile(o_ref, r_ref)
 
@@ -239,18 +249,19 @@
         start = conv * (PITCH + 1)
         rows = span - 2 * conv
         for frame in range(2):
-            spread(grid.at[2 * conv + frame], start, patches, frame, rows)
+            spread(grid.at[2 * conv + frame], start, patches, frame, rows, PITCH)
         for first, count in chunks(rows - 2):
             out[first * PITCH : (first + count) * PITCH, :] = convolve(
                 patches, w_ref.at[conv], HELD,
-                bias_of(b_ref[conv : conv + 1, :], count * PITCH), first, count,
+                bias_of(b_ref[conv : conv + 1, :], count * PITCH), first, count, PITCH,
             )
 
 
 def load_rows(x_ref, held):
     span = x_ref.shape[0]
+    pitch = pitch_of(span)
     for row in range(span):
-        held[row * PITCH : row * PITCH + span, :] = x_ref[row].astype(jnp.float32)
+        held[row * pitch : row * pitch + span, :] = x_ref[row].astype(jnp.float32)
 
 
 def early_kernel(
@@ -258,15 +269,16 @@
     r_ref, one_ref, two_ref, o_ref, held, flat, patches,
 ):
     load_rows(x_ref, held)
+    pitch = pitch_of(x_ref.shape[0])
 
     def conv_of(conv, known, part):
         def run(first, count):
-            begin = drop * (PITCH + 1) + first * PITCH
-            total = convolve(
-                patches, w_ref.at[conv], EARLY, known[begin : begin + count * PITCH, :],
-                first, count,
-            )
-            return split_off(part)(total, first, count)
+            begins = [(drop + row) * PITCH + drop for row in range(first, first + count)]
+            total = jnp.concatenate(
+                [known[begin : begin + pitch, :] for begin in begins], axis=0
+            )
+            total = convolve(patches, w_ref.at[conv], EARLY, total, first, count, pitch)
+            return split_off(part, pitch)(total, first, count)
 
         return run
 
@@ -284,7 +296,8 @@
     load_rows(x_ref, held)
     body(
         halo, height, width, g_ref, held, flat, patches, nothing,
-        late_of(patches, w_ref, 0, one_ref), late_of(patches, w_ref, 1, two_ref), o_ref, 4,
+        late_of(patches, w_ref, 0, one_ref, o_ref.shape[0] + 4),
+        late_of(patches, w_ref, 1, two_ref, o_ref.shape[0] + 4), o_ref, 4,
     )
     keep_tile(o_ref, r_ref)
 
@@ -381,8 +394,8 @@
 
 def parts_of(span, lanes):
     return [
-        shaped((span - 2) * PITCH, lanes, dtype=jnp.float32),
-        shaped((span - 4) * PITCH, lanes, dtype=jnp.float32),
+        shaped((span - 2) * pitch_of(span), lanes, dtype=jnp.float32),
+        shaped((span - 4) * pitch_of(span), lanes, dtype=jnp.float32),
     ]
 
 

time: 69.8 us -> 69.5 us (level)
  no operation moved by 1% of the time
where the time goes in v6:
time: 69.5 us; the launch traced here: 69.1 us
  waiting for transfers between devices  37.6 us (54%)
  starting transfers between devices  23.8 us (34%)
  Pallas kernels  7.15 us (10%)
    ppermute x14, waiting for transfers between devices, moved(): return lax.ppermute(value, AXES, pairs)  37.6 us
    ppermute x14, starting transfers between devices, moved(): return lax.ppermute(value, AXES, pairs)  23.8 us
    pallas_call x9, Pallas kernels, launch(): pl.pallas_call(kernel, out_shape=outs, in_specs=[WHOLE] * len(arguments),...  5.62 us
  transfers between devices with their start and end apart: 14, of which 6 were waited for; matrix products, arithmetic and copies ran while one was open for 0% of the time, Pallas kernels for 6%

profile of v6, /device:TPU:210, one launch (start us, length us, event | category | flops | bytes accessed | tf_op | source)
XLA Modules:
  0.0 69.1 jit_solution(7549928674455580673)
XLA Ops:
  0.0 0.0 copy-start
  0.0 0.0 copy-start.2
  0.0 0.0 copy-start.3
  0.0 1.4 %shard_map.55 = (bf16[6,16,16,128]{3,2,1,0:T(8,128)(2,1)S(1)}, bf16[6,8,16,128]{3,2,1,0:T(8,128)(2,1)S(1)}, bf16[6,8,16,128]{3,2,1,0:T(8,128)(2,1)S(1)}) custom-call(bf16[2,16,16,128]{3,2,1,0:T(8,128)(2,1)} %frames.1, bf16[4,16,16,128]{3,2,1,0:T(8,128)(2,1)} %bitcast.14), custom_call_target="tpu_custom_call" | custom-call | tf_op jit(solution)/shard_map/pallas_call | solution.py:405
  1.4 0.7 collective-permute-start
  2.1 0.7 collective-permute-start.1
  2.8 0.0 collective-permute-done.low.refs_1_
  2.8 0.0 collective-permute-done.1.high.refs_2_
  2.8 0.1 shard_map.56
  2.9 0.7 collective-permute-start.2
  3.6 0.7 collective-permute-start.3
  4.3 0.0 collective-permute-done.2.refs_3_
  4.4 8.1 %collective-permute-start.7 = (bf16[4,6,16,128]{3,2,1,0:T(8,128)(2,1)S(1)}, bf16[4,6,16,128]{3,2,1,0:T(8,128)(2,1)S(1)}, u32[]{:S(2)}, u32[]{:S(2)}) collective-permute-start(bf16[4,6,16,128]{3,2,1,0:T(8,128)(2,1)S(1)} %get-tuple-element.71), channel_id=1, source_target_pairs={{136,128},{137,129},{138,130},{139,131},{140,132},{141,133},{142,1... | collective-permute-start | bytes 294920 | tf_op jit(solution)/shard_map/ppermute | solution.py:438
  12.5 0.1 fusion
  12.5 2.0 %collective-permute-start.6 = (bf16[4,6,16,128]{3,2,1,0:T(8,128)(2,1)S(1)}, bf16[4,6,16,128]{3,2,1,0:T(8,128)(2,1)S(1)}, u32[]{:S(2)}, u32[]{:S(2)}) collective-permute-start(bf16[4,6,16,128]{3,2,1,0:T(8,128)(2,1)S(1)} %get-tuple-element.72), channel_id=1, source_target_pairs={{128,136},{129,137},{130,138},{131,139},{132,140},{133,141},{134,1... | collective-permute-start | bytes 294920 | tf_op jit(solution)/shard_map/ppermute | solution.py:438
  14.6 0.9 %collective-permute-done.7.high = bf16[4,6,16,128]{3,2,1,0:T(8,128)(2,1)S(1)} collective-permute-done((bf16[4,6,16,128]{3,2,1,0:T(8,128)(2,1)S(1)}, bf16[4,6,16,128]{3,2,1,0:T(8,128)(2,1)S(1)}, u32[]{:S(2)}, u32[]{:S(2)}) %collective-permute-start.7) | collective-permute-done | bytes 98336 | tf_op jit(solution)/shard_map/ppermute | solution.py:438
  15.5 8.6 %collective-permute-done.6.low = bf16[4,6,16,128]{3,2,1,0:T(8,128)(2,1)S(1)} collective-permute-done((bf16[4,6,16,128]{3,2,1,0:T(8,128)(2,1)S(1)}, bf16[4,6,16,128]{3,2,1,0:T(8,128)(2,1)S(1)}, u32[]{:S(2)}, u32[]{:S(2)}) %collective-permute-start.6) | collective-permute-done | bytes 98336 | tf_op jit(solution)/shard_map/ppermute | solution.py:438
  24.2 0.1 pad_maximum_fusion
  24.2 1.9 %collective-permute-start.8 = (bf16[4,28,6,128]{3,2,1,0:T(8,128)(2,1)S(1)}, bf16[4,28,6,128]{3,2,1,0:T(8,128)(2,1)S(1)}, u32[]{:S(2)}, u32[]{:S(2)}) collective-permute-start(bf16[4,28,6,128]{3,2,1,0:T(8,128)(2,1)S(1)} %pad_maximum_fusion), channel_id=1, source_target_pairs={{128,129},{129,130},{130,131},{131,132},{132,133},{133,134},{134,1... | collective-permute-start | bytes 516104 | tf_op jit(solution)/shard_map/ppermute | solution.py:438
  26.2 0.1 pad_maximum_fusion.1
  26.2 3.6 %collective-permute-start.9 = (bf16[4,28,6,128]{3,2,1,0:T(8,128)(2,1)S(1)}, bf16[4,28,6,128]{3,2,1,0:T(8,128)(2,1)S(1)}, u32[]{:S(2)}, u32[]{:S(2)}) collective-permute-start(bf16[4,28,6,128]{3,2,1,0:T(8,128)(2,1)S(1)} %pad_maximum_fusion.1), channel_id=1, source_target_pairs={{129,128},{130,129},{131,130},{132,131},{133,132},{134,133},{135,1... | collective-permute-start | bytes 516104 | tf_op jit(solution)/shard_map/ppermute | solution.py:438
  29.9 0.0 collective-permute-done.3.refs_4_
  29.9 0.0 copy-done
  29.9 0.0 copy-done.2
  29.9 0.0 copy-done.3
  29.9 0.7 collective-permute-start.5
  30.6 0.0 copy-start.1
  30.7 0.8 %collective-permute-start.4 = (bf16[28,28,128]{2,1,0:T(8,128)(2,1)S(1)}, bf16[28,28,128]{2,1,0:T(8,128)(2,1)S(1)}, u32[]{:S(2)}, u32[]{:S(2)}) collective-permute-start(bf16[28,28,128]{2,1,0:T(8,128)(2,1)S(1)} %get-tuple-element.46), channel_id=1, source_target_pairs={{0,128},{1,129},{2,130},{3,131},{4,132},{5,133},{6,134},{7,135},{8... | collective-permute-start | bytes 602120 | tf_op jit(solution)/shard_map/ppermute | solution.py:438
  31.5 0.1 collective-permute-done.8.left
  31.6 1.8 %collective-permute-done.9.right = bf16[4,28,6,128]{3,2,1,0:T(8,128)(2,1)S(1)} collective-permute-done((bf16[4,28,6,128]{3,2,1,0:T(8,128)(2,1)S(1)}, bf16[4,28,6,128]{3,2,1,0:T(8,128)(2,1)S(1)}, u32[]{:S(2)}, u32[]{:S(2)}) %collective-permute-start.9) | collective-permute-done | bytes 172064 | tf_op jit(solution)/shard_map/ppermute | solution.py:438
  33.4 0.0 copy-done.1
  33.4 2.6 %shard_map.59 = (f32[832,256]{1,0:T(8,128)S(1)}, f32[768,256]{1,0:T(8,128)S(1)}) custom-call(bf16[4,16,16,128]{3,2,1,0:T(8,128)(2,1)S(1)} %bitcast.15, bf16[4,6,16,128]{3,2,1,0:T(8,128)(2,1)S(1)} %collective-permute-done.6.low, bf16[4,6,16,128]{3,2,1,0:T(8,128)(2,1)S(1)} %collective-permute-done.7.high, ...), custom_call_target="tpu_custom_call" | custom-call | flops 2113929216 | bytes 2097152 | tf_op jit(solution)/shard_map/pallas_call | solution.py:367
  36.0 0.0 collective-permute-done.5.refs_0_
  36.0 0.7 collective-permute-start.11
  36.7 0.0 collective-permute-done.4.refs_0_
  36.7 0.7 collective-permute-start.10
  37.4 0.0 collective-permute-done.11.refs_0_
  37.4 0.2 shard_map.62
  37.6 1.3 %collective-permute-start.13 = (bf16[20,20,128]{2,1,0:T(8,128)(2,1)S(1)}, bf16[20,20,128]{2,1,0:T(8,128)(2,1)S(1)}, u32[]{:S(2)}, u32[]{:S(2)}) collective-permute-start(bf16[20,20,128]{2,1,0:T(8,128)(2,1)S(1)} %get-tuple-element.63), channel_id=1, source_target_pairs={{256,384},{257,385},{258,386},{259,387},{260,388},{261,389},{262,3... | collective-permute-start | bytes 307208 | tf_op jit(solution)/shard_map/ppermute | solution.py:438
  38.9 0.0 collective-permute-done.10.refs_0_
  39.0 1.3 %collective-permute-start.12 = (bf16[20,20,128]{2,1,0:T(8,128)(2,1)S(1)}, bf16[20,20,128]{2,1,0:T(8,128)(2,1)S(1)}, u32[]{:S(2)}, u32[]{:S(2)}) collective-permute-start(bf16[20,20,128]{2,1,0:T(8,128)(2,1)S(1)} %get-tuple-element.62), channel_id=1, source_target_pairs={{256,384},{257,385},{258,386},{259,387},{260,388},{261,389},{262,3... | collective-permute-start | bytes 307208 | tf_op jit(solution)/shard_map/ppermute | solution.py:438
  40.3 23.0 %collective-permute-done.13.refs_0_ = bf16[20,20,128]{2,1,0:T(8,128)(2,1)S(1)} collective-permute-done((bf16[20,20,128]{2,1,0:T(8,128)(2,1)S(1)}, bf16[20,20,128]{2,1,0:T(8,128)(2,1)S(1)}, u32[]{:S(2)}, u32[]{:S(2)}) %collective-permute-start.13) | collective-permute-done | bytes 102432 | tf_op jit(solution)/shard_map/ppermute | solution.py:438
  63.2 1.1 %shard_map.64 = (bf16[16,16,128]{2,1,0:T(8,128)(2,1)S(1)}, f32[432,128]{1,0:T(8,128)S(1)}, f32[384,128]{1,0:T(8,128)S(1)}) custom-call(bf16[20,20,128]{2,1,0:T(8,128)(2,1)S(1)} %collective-permute-done.13.refs_0_, f32[832,256]{1,0:T(8,128)S(1)} %get-tuple-element.50.refs_1_, f32[768,256]{1,0:T(8,128)S(1)} %get-tuple-element.51.refs_2_, ...), custom_call_target="tpu_custom_call" | custom-call | flops 754974720 | bytes 2097152 | tf_op jit(solution)/shard_map/pallas_call | solution.py:367
  64.4 3.1 %collective-permute-done.12.refs_0_ = bf16[20,20,128]{2,1,0:T(8,128)(2,1)S(1)} collective-permute-done((bf16[20,20,128]{2,1,0:T(8,128)(2,1)S(1)}, bf16[20,20,128]{2,1,0:T(8,128)(2,1)S(1)}, u32[]{:S(2)}, u32[]{:S(2)}) %collective-permute-start.12) | collective-permute-done | bytes 102432 | tf_op jit(solution)/shard_map/ppermute | solution.py:438
  67.5 1.6 %shard_map.65 = bf16[2,16,16,128]{3,2,1,0:T(8,128)(2,1)} custom-call(bf16[20,20,128]{2,1,0:T(8,128)(2,1)S(1)} %collective-permute-done.12.refs_0_, f32[432,128]{1,0:T(8,128)S(1)} %get-tuple-element.65.refs_1_, f32[384,128]{1,0:T(8,128)S(1)} %get-tuple-element.66.refs_2_, bf16[2,3,3,384,128]{4,3,2,1,0:T(8,128)(2,1)S(1)} %bitcast.13, f32[2,128]{1,0:T(2,128)S(1)} %bitcast.23, ...), custom_call_target="tpu_custom_call" | custom-call | flops 754974720 | bytes 2097152 | tf_op jit(solution)/shard_map/pallas_call | solution.py:367
  (8 shorter events, 0.2 us)
Async XLA Ops:
  0.0 29.9 %copy-start = (bf16[1,2,3,3,3,128,128]{6,5,4,3,2,1,0:T(8,128)(2,1)S(1)}, bf16[1,2,3,3,3,128,128]{6,5,4,3,2,1,0:T(8,128)(2,1)}, u32[]{:S(2)}) copy-start(bf16[1,2,3,3,3,128,128]{6,5,4,3,2,1,0:T(8,128)(2,1)} %param.7) | copy-start | bytes 5308420
  0.0 29.9 %copy-start.2 = (f32[1,2,128]{2,1,0:T(2,128)S(1)}, f32[1,2,128]{2,1,0:T(2,128)}, u32[]{:S(2)}) copy-start(f32[1,2,128]{2,1,0:T(2,128)} %param.9) | copy-start | bytes 3076
  0.0 29.9 %copy-start.3 = (f32[1,2,128]{2,1,0:T(2,128)S(1)}, f32[1,2,128]{2,1,0:T(2,128)}, u32[]{:S(2)}) copy-start(f32[1,2,128]{2,1,0:T(2,128)} %param.8) | copy-start | bytes 3076
  1.4 1.4 %collective-permute-start = (bf16[6,8,16,128]{3,2,1,0:T(8,128)(2,1)S(1)}, bf16[6,8,16,128]{3,2,1,0:T(8,128)(2,1)S(1)}, u32[]{:S(2)}, u32[]{:S(2)}) collective-permute-start(bf16[6,8,16,128]{3,2,1,0:T(8,128)(2,1)S(1)} %get-tuple-element.38), channel_id=1, source_target_pairs={{0,8},{1,9},{2,10},{3,11},{4,12},{5,13},{6,14},{7,15},{8,16},{9,17... | collective-permute-start | bytes 589832 | tf_op jit(solution)/shard_map/ppermute | solution.py:438
  2.1 0.7 %collective-permute-start.1 = (bf16[6,8,16,128]{3,2,1,0:T(8,128)(2,1)S(1)}, bf16[6,8,16,128]{3,2,1,0:T(8,128)(2,1)S(1)}, u32[]{:S(2)}, u32[]{:S(2)}) collective-permute-start(bf16[6,8,16,128]{3,2,1,0:T(8,128)(2,1)S(1)} %get-tuple-element.39), channel_id=1, source_target_pairs={{8,0},{9,1},{10,2},{11,3},{12,4},{13,5},{14,6},{15,7},{16,8},{17,9... | collective-permute-start | bytes 589832 | tf_op jit(solution)/shard_map/ppermute | solution.py:438
  2.9 1.4 %collective-permute-start.2 = (bf16[6,32,8,128]{3,2,1,0:T(8,128)(2,1)S(1)}, bf16[6,32,8,128]{3,2,1,0:T(8,128)(2,1)S(1)}, u32[]{:S(2)}, u32[]{:S(2)}) collective-permute-start(bf16[6,32,8,128]{3,2,1,0:T(8,128)(2,1)S(1)} %get-tuple-element.40), channel_id=1, source_target_pairs={{0,1},{1,2},{2,3},{3,4},{4,5},{5,6},{6,7},{8,9},{9,10},{10,11},{11... | collective-permute-start | bytes 1179656 | tf_op jit(solution)/shard_map/ppermute | solution.py:438
  3.6 26.2 %collective-permute-start.3 = (bf16[6,32,8,128]{3,2,1,0:T(8,128)(2,1)S(1)}, bf16[6,32,8,128]{3,2,1,0:T(8,128)(2,1)S(1)}, u32[]{:S(2)}, u32[]{:S(2)}) collective-permute-start(bf16[6,32,8,128]{3,2,1,0:T(8,128)(2,1)S(1)} %get-tuple-element.42), channel_id=1, source_target_pairs={{1,0},{2,1},{3,2},{4,3},{5,4},{6,5},{7,6},{9,8},{10,9},{11,10},{12... | collective-permute-start | bytes 1179656 | tf_op jit(solution)/shard_map/ppermute | solution.py:438
  4.4 11.1 %collective-permute-start.7 = (bf16[4,6,16,128]{3,2,1,0:T(8,128)(2,1)S(1)}, bf16[4,6,16,128]{3,2,1,0:T(8,128)(2,1)S(1)}, u32[]{:S(2)}, u32[]{:S(2)}) collective-permute-start(bf16[4,6,16,128]{3,2,1,0:T(8,128)(2,1)S(1)} %get-tuple-element.71), channel_id=1, source_target_pairs={{136,128},{137,129},{138,130},{139,131},{140,132},{141,133},{142,1... | collective-permute-start | bytes 294920 | tf_op jit(solution)/shard_map/ppermute | solution.py:438
  12.5 11.6 %collective-permute-start.6 = (bf16[4,6,16,128]{3,2,1,0:T(8,128)(2,1)S(1)}, bf16[4,6,16,128]{3,2,1,0:T(8,128)(2,1)S(1)}, u32[]{:S(2)}, u32[]{:S(2)}) collective-permute-start(bf16[4,6,16,128]{3,2,1,0:T(8,128)(2,1)S(1)} %get-tuple-element.72), channel_id=1, source_target_pairs={{128,136},{129,137},{130,138},{131,139},{132,140},{133,141},{134,1... | collective-permute-start | bytes 294920 | tf_op jit(solution)/shard_map/ppermute | solution.py:438
  24.2 7.3 %collective-permute-start.8 = (bf16[4,28,6,128]{3,2,1,0:T(8,128)(2,1)S(1)}, bf16[4,28,6,128]{3,2,1,0:T(8,128)(2,1)S(1)}, u32[]{:S(2)}, u32[]{:S(2)}) collective-permute-start(bf16[4,28,6,128]{3,2,1,0:T(8,128)(2,1)S(1)} %pad_maximum_fusion), channel_id=1, source_target_pairs={{128,129},{129,130},{130,131},{131,132},{132,133},{133,134},{134,1... | collective-permute-start | bytes 516104 | tf_op jit(solution)/shard_map/ppermute | solution.py:438
  26.2 7.2 %collective-permute-start.9 = (bf16[4,28,6,128]{3,2,1,0:T(8,128)(2,1)S(1)}, bf16[4,28,6,128]{3,2,1,0:T(8,128)(2,1)S(1)}, u32[]{:S(2)}, u32[]{:S(2)}) collective-permute-start(bf16[4,28,6,128]{3,2,1,0:T(8,128)(2,1)S(1)} %pad_maximum_fusion.1), channel_id=1, source_target_pairs={{129,128},{130,129},{131,130},{132,131},{133,132},{134,133},{135,1... | collective-permute-start | bytes 516104 | tf_op jit(solution)/shard_map/ppermute | solution.py:438
  29.9 6.0 %collective-permute-start.5 = (bf16[28,28,128]{2,1,0:T(8,128)(2,1)S(1)}, bf16[28,28,128]{2,1,0:T(8,128)(2,1)S(1)}, u32[]{:S(2)}, u32[]{:S(2)}) collective-permute-start(bf16[28,28,128]{2,1,0:T(8,128)(2,1)S(1)} %get-tuple-element.47), channel_id=1, source_target_pairs={{0,128},{1,129},{2,130},{3,131},{4,132},{5,133},{6,134},{7,135},{8... | collective-permute-start | bytes 602120 | tf_op jit(solution)/shard_map/ppermute | solution.py:438
  30.6 2.8 %copy-start.1 = (bf16[1,2,2,16,16,128]{5,4,3,2,1,0:T(8,128)(2,1)S(1)}, bf16[1,2,2,16,16,128]{5,4,3,2,1,0:T(8,128)(2,1)}, u32[]{:S(2)}) copy-start(bf16[1,2,2,16,16,128]{5,4,3,2,1,0:T(8,128)(2,1)} %param.6) | copy-start | bytes 786436
  30.7 6.0 %collective-permute-start.4 = (bf16[28,28,128]{2,1,0:T(8,128)(2,1)S(1)}, bf16[28,28,128]{2,1,0:T(8,128)(2,1)S(1)}, u32[]{:S(2)}, u32[]{:S(2)}) collective-permute-start(bf16[28,28,128]{2,1,0:T(8,128)(2,1)S(1)} %get-tuple-element.46), channel_id=1, source_target_pairs={{0,128},{1,129},{2,130},{3,131},{4,132},{5,133},{6,134},{7,135},{8... | collective-permute-start | bytes 602120 | tf_op jit(solution)/shard_map/ppermute | solution.py:438
  36.0 1.4 %collective-permute-start.11 = (bf16[24,24,128]{2,1,0:T(8,128)(2,1)S(1)}, bf16[24,24,128]{2,1,0:T(8,128)(2,1)S(1)}, u32[]{:S(2)}, u32[]{:S(2)}) collective-permute-start(bf16[24,24,128]{2,1,0:T(8,128)(2,1)S(1)} %get-tuple-element.57), channel_id=1, source_target_pairs={{128,256},{129,257},{130,258},{131,259},{132,260},{133,261},{134,2... | collective-permute-start | bytes 442376 | tf_op jit(solution)/shard_map/ppermute | solution.py:438
  36.7 2.2 %collective-permute-start.10 = (bf16[24,24,128]{2,1,0:T(8,128)(2,1)S(1)}, bf16[24,24,128]{2,1,0:T(8,128)(2,1)S(1)}, u32[]{:S(2)}, u32[]{:S(2)}) collective-permute-start(bf16[24,24,128]{2,1,0:T(8,128)(2,1)S(1)} %get-tuple-element.56), channel_id=1, source_target_pairs={{128,256},{129,257},{130,258},{131,259},{132,260},{133,261},{134,2... | collective-permute-start | bytes 442376 | tf_op jit(solution)/shard_map/ppermute | solution.py:438
  37.6 25.6 %collective-permute-start.13 = (bf16[20,20,128]{2,1,0:T(8,128)(2,1)S(1)}, bf16[20,20,128]{2,1,0:T(8,128)(2,1)S(1)}, u32[]{:S(2)}, u32[]{:S(2)}) collective-permute-start(bf16[20,20,128]{2,1,0:T(8,128)(2,1)S(1)} %get-tuple-element.63), channel_id=1, source_target_pairs={{256,384},{257,385},{258,386},{259,387},{260,388},{261,389},{262,3... | collective-permute-start | bytes 307208 | tf_op jit(solution)/shard_map/ppermute | solution.py:438
  39.0 28.6 %collective-permute-start.12 = (bf16[20,20,128]{2,1,0:T(8,128)(2,1)S(1)}, bf16[20,20,128]{2,1,0:T(8,128)(2,1)S(1)}, u32[]{:S(2)}, u32[]{:S(2)}) collective-permute-start(bf16[20,20,128]{2,1,0:T(8,128)(2,1)S(1)} %get-tuple-element.62), channel_id=1, source_target_pairs={{256,384},{257,385},{258,386},{259,387},{260,388},{261,389},{262,3... | collective-permute-start | bytes 307208 | tf_op jit(solution)/shard_map/ppermute | solution.py:438

commit v7 on v6

--- a/solution.py
+++ b/solution.py
@@ -197,7 +197,7 @@
 
     body(
         halo, height, width, g_ref, grid.at[0], flat, patches, fill,
-        conv_of(0, one_ref), conv_of(1, two_ref), o_ref, 10,
+        conv_of(0, one_ref), conv_of(1, two_ref), o_ref, 15,
     )
     keep_tile(o_ref, r_ref)
 

time: 69.5 us -> 69.5 us (level)
  no operation moved by 1% of the time
where the time goes in v7:
time: 69.5 us; the launch traced here: 69.2 us
  waiting for transfers between devices  37.6 us (54%)
  starting transfers between devices  23.8 us (34%)
  Pallas kernels  7.15 us (10%)
    ppermute x14, waiting for transfers between devices, moved(): return lax.ppermute(value, AXES, pairs)  37.6 us
    ppermute x14, starting transfers between devices, moved(): return lax.ppermute(value, AXES, pairs)  23.8 us
    pallas_call x9, Pallas kernels, launch(): pl.pallas_call(kernel, out_shape=outs, in_specs=[WHOLE] * len(arguments),...  5.62 us
  transfers between devices with their start and end apart: 14, of which 6 were waited for; matrix products, arithmetic and copies ran while one was open for 0% of the time, Pallas kernels for 6%

profile of v7, /device:TPU:210, one launch (start us, length us, event | category | flops | bytes accessed | tf_op | source)
XLA Modules:
  0.0 69.2 jit_solution(18182020890217385227)
XLA Ops:
  0.0 0.0 copy-start
  0.0 0.0 copy-start.2
  0.0 0.0 copy-start.3
  0.0 1.4 %shard_map.55 = (bf16[6,16,16,128]{3,2,1,0:T(8,128)(2,1)S(1)}, bf16[6,8,16,128]{3,2,1,0:T(8,128)(2,1)S(1)}, bf16[6,8,16,128]{3,2,1,0:T(8,128)(2,1)S(1)}) custom-call(bf16[2,16,16,128]{3,2,1,0:T(8,128)(2,1)} %frames.1, bf16[4,16,16,128]{3,2,1,0:T(8,128)(2,1)} %bitcast.14), custom_call_target="tpu_custom_call" | custom-call | tf_op jit(solution)/shard_map/pallas_call | solution.py:405
  1.4 0.7 collective-permute-start
  2.1 0.7 collective-permute-start.1
  2.8 0.0 collective-permute-done.low.refs_1_
  2.8 0.0 collective-permute-done.1.high.refs_2_
  2.8 0.1 shard_map.56
  2.9 0.7 collective-permute-start.2
  3.6 0.7 collective-permute-start.3
  4.3 0.0 collective-permute-done.2.refs_3_
  4.4 8.1 %collective-permute-start.7 = (bf16[4,6,16,128]{3,2,1,0:T(8,128)(2,1)S(1)}, bf16[4,6,16,128]{3,2,1,0:T(8,128)(2,1)S(1)}, u32[]{:S(2)}, u32[]{:S(2)}) collective-permute-start(bf16[4,6,16,128]{3,2,1,0:T(8,128)(2,1)S(1)} %get-tuple-element.71), channel_id=1, source_target_pairs={{136,128},{137,129},{138,130},{139,131},{140,132},{141,133},{142,1... | collective-permute-start | bytes 294920 | tf_op jit(solution)/shard_map/ppermute | solution.py:438
  12.5 0.1 fusion
  12.5 2.0 %collective-permute-start.6 = (bf16[4,6,16,128]{3,2,1,0:T(8,128)(2,1)S(1)}, bf16[4,6,16,128]{3,2,1,0:T(8,128)(2,1)S(1)}, u32[]{:S(2)}, u32[]{:S(2)}) collective-permute-start(bf16[4,6,16,128]{3,2,1,0:T(8,128)(2,1)S(1)} %get-tuple-element.72), channel_id=1, source_target_pairs={{128,136},{129,137},{130,138},{131,139},{132,140},{133,141},{134,1... | collective-permute-start | bytes 294920 | tf_op jit(solution)/shard_map/ppermute | solution.py:438
  14.6 0.9 %collective-permute-done.7.high = bf16[4,6,16,128]{3,2,1,0:T(8,128)(2,1)S(1)} collective-permute-done((bf16[4,6,16,128]{3,2,1,0:T(8,128)(2,1)S(1)}, bf16[4,6,16,128]{3,2,1,0:T(8,128)(2,1)S(1)}, u32[]{:S(2)}, u32[]{:S(2)}) %collective-permute-start.7) | collective-permute-done | bytes 98336 | tf_op jit(solution)/shard_map/ppermute | solution.py:438
  15.5 8.6 %collective-permute-done.6.low = bf16[4,6,16,128]{3,2,1,0:T(8,128)(2,1)S(1)} collective-permute-done((bf16[4,6,16,128]{3,2,1,0:T(8,128)(2,1)S(1)}, bf16[4,6,16,128]{3,2,1,0:T(8,128)(2,1)S(1)}, u32[]{:S(2)}, u32[]{:S(2)}) %collective-permute-start.6) | collective-permute-done | bytes 98336 | tf_op jit(solution)/shard_map/ppermute | solution.py:438
  24.2 0.1 pad_maximum_fusion
  24.2 1.9 %collective-permute-start.8 = (bf16[4,28,6,128]{3,2,1,0:T(8,128)(2,1)S(1)}, bf16[4,28,6,128]{3,2,1,0:T(8,128)(2,1)S(1)}, u32[]{:S(2)}, u32[]{:S(2)}) collective-permute-start(bf16[4,28,6,128]{3,2,1,0:T(8,128)(2,1)S(1)} %pad_maximum_fusion), channel_id=1, source_target_pairs={{128,129},{129,130},{130,131},{131,132},{132,133},{133,134},{134,1... | collective-permute-start | bytes 516104 | tf_op jit(solution)/shard_map/ppermute | solution.py:438
  26.2 0.1 pad_maximum_fusion.1
  26.2 3.6 %collective-permute-start.9 = (bf16[4,28,6,128]{3,2,1,0:T(8,128)(2,1)S(1)}, bf16[4,28,6,128]{3,2,1,0:T(8,128)(2,1)S(1)}, u32[]{:S(2)}, u32[]{:S(2)}) collective-permute-start(bf16[4,28,6,128]{3,2,1,0:T(8,128)(2,1)S(1)} %pad_maximum_fusion.1), channel_id=1, source_target_pairs={{129,128},{130,129},{131,130},{132,131},{133,132},{134,133},{135,1... | collective-permute-start | bytes 516104 | tf_op jit(solution)/shard_map/ppermute | solution.py:438
  29.9 0.0 collective-permute-done.3.refs_4_
  29.9 0.0 copy-done
  29.9 0.0 copy-done.2
  29.9 0.0 copy-done.3
  29.9 0.7 collective-permute-start.5
  30.6 0.0 copy-start.1
  30.7 0.8 %collective-permute-start.4 = (bf16[28,28,128]{2,1,0:T(8,128)(2,1)S(1)}, bf16[28,28,128]{2,1,0:T(8,128)(2,1)S(1)}, u32[]{:S(2)}, u32[]{:S(2)}) collective-permute-start(bf16[28,28,128]{2,1,0:T(8,128)(2,1)S(1)} %get-tuple-element.46), channel_id=1, source_target_pairs={{0,128},{1,129},{2,130},{3,131},{4,132},{5,133},{6,134},{7,135},{8... | collective-permute-start | bytes 602120 | tf_op jit(solution)/shard_map/ppermute | solution.py:438
  31.5 0.1 collective-permute-done.8.left
  31.6 1.8 %collective-permute-done.9.right = bf16[4,28,6,128]{3,2,1,0:T(8,128)(2,1)S(1)} collective-permute-done((bf16[4,28,6,128]{3,2,1,0:T(8,128)(2,1)S(1)}, bf16[4,28,6,128]{3,2,1,0:T(8,128)(2,1)S(1)}, u32[]{:S(2)}, u32[]{:S(2)}) %collective-permute-start.9) | collective-permute-done | bytes 172064 | tf_op jit(solution)/shard_map/ppermute | solution.py:438
  33.4 0.0 copy-done.1
  33.4 2.6 %shard_map.59 = (f32[832,256]{1,0:T(8,128)S(1)}, f32[768,256]{1,0:T(8,128)S(1)}) custom-call(bf16[4,16,16,128]{3,2,1,0:T(8,128)(2,1)S(1)} %bitcast.15, bf16[4,6,16,128]{3,2,1,0:T(8,128)(2,1)S(1)} %collective-permute-done.6.low, bf16[4,6,16,128]{3,2,1,0:T(8,128)(2,1)S(1)} %collective-permute-done.7.high, ...), custom_call_target="tpu_custom_call" | custom-call | flops 2113929216 | bytes 2097152 | tf_op jit(solution)/shard_map/pallas_call | solution.py:367
  36.0 0.0 collective-permute-done.5.refs_0_
  36.0 0.7 collective-permute-start.11
  36.7 0.0 collective-permute-done.4.refs_0_
  36.7 0.7 collective-permute-start.10
  37.4 0.0 collective-permute-done.11.refs_0_
  37.4 0.2 shard_map.62
  37.6 1.3 %collective-permute-start.13 = (bf16[20,20,128]{2,1,0:T(8,128)(2,1)S(1)}, bf16[20,20,128]{2,1,0:T(8,128)(2,1)S(1)}, u32[]{:S(2)}, u32[]{:S(2)}) collective-permute-start(bf16[20,20,128]{2,1,0:T(8,128)(2,1)S(1)} %get-tuple-element.63), channel_id=1, source_target_pairs={{256,384},{257,385},{258,386},{259,387},{260,388},{261,389},{262,3... | collective-permute-start | bytes 307208 | tf_op jit(solution)/shard_map/ppermute | solution.py:438
  38.9 0.0 collective-permute-done.10.refs_0_
  39.0 1.3 %collective-permute-start.12 = (bf16[20,20,128]{2,1,0:T(8,128)(2,1)S(1)}, bf16[20,20,128]{2,1,0:T(8,128)(2,1)S(1)}, u32[]{:S(2)}, u32[]{:S(2)}) collective-permute-start(bf16[20,20,128]{2,1,0:T(8,128)(2,1)S(1)} %get-tuple-element.62), channel_id=1, source_target_pairs={{256,384},{257,385},{258,386},{259,387},{260,388},{261,389},{262,3... | collective-permute-start | bytes 307208 | tf_op jit(solution)/shard_map/ppermute | solution.py:438
  40.3 23.0 %collective-permute-done.13.refs_0_ = bf16[20,20,128]{2,1,0:T(8,128)(2,1)S(1)} collective-permute-done((bf16[20,20,128]{2,1,0:T(8,128)(2,1)S(1)}, bf16[20,20,128]{2,1,0:T(8,128)(2,1)S(1)}, u32[]{:S(2)}, u32[]{:S(2)}) %collective-permute-start.13) | collective-permute-done | bytes 102432 | tf_op jit(solution)/shard_map/ppermute | solution.py:438
  63.3 1.1 %shard_map.64 = (bf16[16,16,128]{2,1,0:T(8,128)(2,1)S(1)}, f32[432,128]{1,0:T(8,128)S(1)}, f32[384,128]{1,0:T(8,128)S(1)}) custom-call(bf16[20,20,128]{2,1,0:T(8,128)(2,1)S(1)} %collective-permute-done.13.refs_0_, f32[832,256]{1,0:T(8,128)S(1)} %get-tuple-element.50.refs_1_, f32[768,256]{1,0:T(8,128)S(1)} %get-tuple-element.51.refs_2_, ...), custom_call_target="tpu_custom_call" | custom-call | flops 754974720 | bytes 2097152 | tf_op jit(solution)/shard_map/pallas_call | solution.py:367
  64.4 3.1 %collective-permute-done.12.refs_0_ = bf16[20,20,128]{2,1,0:T(8,128)(2,1)S(1)} collective-permute-done((bf16[20,20,128]{2,1,0:T(8,128)(2,1)S(1)}, bf16[20,20,128]{2,1,0:T(8,128)(2,1)S(1)}, u32[]{:S(2)}, u32[]{:S(2)}) %collective-permute-start.12) | collective-permute-done | bytes 102432 | tf_op jit(solution)/shard_map/ppermute | solution.py:438
  67.6 1.6 %shard_map.65 = bf16[2,16,16,128]{3,2,1,0:T(8,128)(2,1)} custom-call(bf16[20,20,128]{2,1,0:T(8,128)(2,1)S(1)} %collective-permute-done.12.refs_0_, f32[432,128]{1,0:T(8,128)S(1)} %get-tuple-element.65.refs_1_, f32[384,128]{1,0:T(8,128)S(1)} %get-tuple-element.66.refs_2_, bf16[2,3,3,384,128]{4,3,2,1,0:T(8,128)(2,1)S(1)} %bitcast.13, f32[2,128]{1,0:T(2,128)S(1)} %bitcast.23, ...), custom_call_target="tpu_custom_call" | custom-call | flops 754974720 | bytes 2097152 | tf_op jit(solution)/shard_map/pallas_call | solution.py:367
  (8 shorter events, 0.2 us)
Async XLA Ops:
  0.0 29.9 %copy-start = (bf16[1,2,3,3,3,128,128]{6,5,4,3,2,1,0:T(8,128)(2,1)S(1)}, bf16[1,2,3,3,3,128,128]{6,5,4,3,2,1,0:T(8,128)(2,1)}, u32[]{:S(2)}) copy-start(bf16[1,2,3,3,3,128,128]{6,5,4,3,2,1,0:T(8,128)(2,1)} %param.7) | copy-start | bytes 5308420
  0.0 29.9 %copy-start.2 = (f32[1,2,128]{2,1,0:T(2,128)S(1)}, f32[1,2,128]{2,1,0:T(2,128)}, u32[]{:S(2)}) copy-start(f32[1,2,128]{2,1,0:T(2,128)} %param.9) | copy-start | bytes 3076
  0.0 29.9 %copy-start.3 = (f32[1,2,128]{2,1,0:T(2,128)S(1)}, f32[1,2,128]{2,1,0:T(2,128)}, u32[]{:S(2)}) copy-start(f32[1,2,128]{2,1,0:T(2,128)} %param.8) | copy-start | bytes 3076
  1.4 1.4 %collective-permute-start = (bf16[6,8,16,128]{3,2,1,0:T(8,128)(2,1)S(1)}, bf16[6,8,16,128]{3,2,1,0:T(8,128)(2,1)S(1)}, u32[]{:S(2)}, u32[]{:S(2)}) collective-permute-start(bf16[6,8,16,128]{3,2,1,0:T(8,128)(2,1)S(1)} %get-tuple-element.38), channel_id=1, source_target_pairs={{0,8},{1,9},{2,10},{3,11},{4,12},{5,13},{6,14},{7,15},{8,16},{9,17... | collective-permute-start | bytes 589832 | tf_op jit(solution)/shard_map/ppermute | solution.py:438
  2.1 0.7 %collective-permute-start.1 = (bf16[6,8,16,128]{3,2,1,0:T(8,128)(2,1)S(1)}, bf16[6,8,16,128]{3,2,1,0:T(8,128)(2,1)S(1)}, u32[]{:S(2)}, u32[]{:S(2)}) collective-permute-start(bf16[6,8,16,128]{3,2,1,0:T(8,128)(2,1)S(1)} %get-tuple-element.39), channel_id=1, source_target_pairs={{8,0},{9,1},{10,2},{11,3},{12,4},{13,5},{14,6},{15,7},{16,8},{17,9... | collective-permute-start | bytes 589832 | tf_op jit(solution)/shard_map/ppermute | solution.py:438
  2.9 1.4 %collective-permute-start.2 = (bf16[6,32,8,128]{3,2,1,0:T(8,128)(2,1)S(1)}, bf16[6,32,8,128]{3,2,1,0:T(8,128)(2,1)S(1)}, u32[]{:S(2)}, u32[]{:S(2)}) collective-permute-start(bf16[6,32,8,128]{3,2,1,0:T(8,128)(2,1)S(1)} %get-tuple-element.40), channel_id=1, source_target_pairs={{0,1},{1,2},{2,3},{3,4},{4,5},{5,6},{6,7},{8,9},{9,10},{10,11},{11... | collective-permute-start | bytes 1179656 | tf_op jit(solution)/shard_map/ppermute | solution.py:438
  3.6 26.2 %collective-permute-start.3 = (bf16[6,32,8,128]{3,2,1,0:T(8,128)(2,1)S(1)}, bf16[6,32,8,128]{3,2,1,0:T(8,128)(2,1)S(1)}, u32[]{:S(2)}, u32[]{:S(2)}) collective-permute-start(bf16[6,32,8,128]{3,2,1,0:T(8,128)(2,1)S(1)} %get-tuple-element.42), channel_id=1, source_target_pairs={{1,0},{2,1},{3,2},{4,3},{5,4},{6,5},{7,6},{9,8},{10,9},{11,10},{12... | collective-permute-start | bytes 1179656 | tf_op jit(solution)/shard_map/ppermute | solution.py:438
  4.4 11.1 %collective-permute-start.7 = (bf16[4,6,16,128]{3,2,1,0:T(8,128)(2,1)S(1)}, bf16[4,6,16,128]{3,2,1,0:T(8,128)(2,1)S(1)}, u32[]{:S(2)}, u32[]{:S(2)}) collective-permute-start(bf16[4,6,16,128]{3,2,1,0:T(8,128)(2,1)S(1)} %get-tuple-element.71), channel_id=1, source_target_pairs={{136,128},{137,129},{138,130},{139,131},{140,132},{141,133},{142,1... | collective-permute-start | bytes 294920 | tf_op jit(solution)/shard_map/ppermute | solution.py:438
  12.5 11.6 %collective-permute-start.6 = (bf16[4,6,16,128]{3,2,1,0:T(8,128)(2,1)S(1)}, bf16[4,6,16,128]{3,2,1,0:T(8,128)(2,1)S(1)}, u32[]{:S(2)}, u32[]{:S(2)}) collective-permute-start(bf16[4,6,16,128]{3,2,1,0:T(8,128)(2,1)S(1)} %get-tuple-element.72), channel_id=1, source_target_pairs={{128,136},{129,137},{130,138},{131,139},{132,140},{133,141},{134,1... | collective-permute-start | bytes 294920 | tf_op jit(solution)/shard_map/ppermute | solution.py:438
  24.2 7.3 %collective-permute-start.8 = (bf16[4,28,6,128]{3,2,1,0:T(8,128)(2,1)S(1)}, bf16[4,28,6,128]{3,2,1,0:T(8,128)(2,1)S(1)}, u32[]{:S(2)}, u32[]{:S(2)}) collective-permute-start(bf16[4,28,6,128]{3,2,1,0:T(8,128)(2,1)S(1)} %pad_maximum_fusion), channel_id=1, source_target_pairs={{128,129},{129,130},{130,131},{131,132},{132,133},{133,134},{134,1... | collective-permute-start | bytes 516104 | tf_op jit(solution)/shard_map/ppermute | solution.py:438
  26.2 7.2 %collective-permute-start.9 = (bf16[4,28,6,128]{3,2,1,0:T(8,128)(2,1)S(1)}, bf16[4,28,6,128]{3,2,1,0:T(8,128)(2,1)S(1)}, u32[]{:S(2)}, u32[]{:S(2)}) collective-permute-start(bf16[4,28,6,128]{3,2,1,0:T(8,128)(2,1)S(1)} %pad_maximum_fusion.1), channel_id=1, source_target_pairs={{129,128},{130,129},{131,130},{132,131},{133,132},{134,133},{135,1... | collective-permute-start | bytes 516104 | tf_op jit(solution)/shard_map/ppermute | solution.py:438
  29.9 6.0 %collective-permute-start.5 = (bf16[28,28,128]{2,1,0:T(8,128)(2,1)S(1)}, bf16[28,28,128]{2,1,0:T(8,128)(2,1)S(1)}, u32[]{:S(2)}, u32[]{:S(2)}) collective-permute-start(bf16[28,28,128]{2,1,0:T(8,128)(2,1)S(1)} %get-tuple-element.47), channel_id=1, source_target_pairs={{0,128},{1,129},{2,130},{3,131},{4,132},{5,133},{6,134},{7,135},{8... | collective-permute-start | bytes 602120 | tf_op jit(solution)/shard_map/ppermute | solution.py:438
  30.6 2.8 %copy-start.1 = (bf16[1,2,2,16,16,128]{5,4,3,2,1,0:T(8,128)(2,1)S(1)}, bf16[1,2,2,16,16,128]{5,4,3,2,1,0:T(8,128)(2,1)}, u32[]{:S(2)}) copy-start(bf16[1,2,2,16,16,128]{5,4,3,2,1,0:T(8,128)(2,1)} %param.6) | copy-start | bytes 786436
  30.7 6.0 %collective-permute-start.4 = (bf16[28,28,128]{2,1,0:T(8,128)(2,1)S(1)}, bf16[28,28,128]{2,1,0:T(8,128)(2,1)S(1)}, u32[]{:S(2)}, u32[]{:S(2)}) collective-permute-start(bf16[28,28,128]{2,1,0:T(8,128)(2,1)S(1)} %get-tuple-element.46), channel_id=1, source_target_pairs={{0,128},{1,129},{2,130},{3,131},{4,132},{5,133},{6,134},{7,135},{8... | collective-permute-start | bytes 602120 | tf_op jit(solution)/shard_map/ppermute | solution.py:438
  36.0 1.4 %collective-permute-start.11 = (bf16[24,24,128]{2,1,0:T(8,128)(2,1)S(1)}, bf16[24,24,128]{2,1,0:T(8,128)(2,1)S(1)}, u32[]{:S(2)}, u32[]{:S(2)}) collective-permute-start(bf16[24,24,128]{2,1,0:T(8,128)(2,1)S(1)} %get-tuple-element.57), channel_id=1, source_target_pairs={{128,256},{129,257},{130,258},{131,259},{132,260},{133,261},{134,2... | collective-permute-start | bytes 442376 | tf_op jit(solution)/shard_map/ppermute | solution.py:438
  36.7 2.2 %collective-permute-start.10 = (bf16[24,24,128]{2,1,0:T(8,128)(2,1)S(1)}, bf16[24,24,128]{2,1,0:T(8,128)(2,1)S(1)}, u32[]{:S(2)}, u32[]{:S(2)}) collective-permute-start(bf16[24,24,128]{2,1,0:T(8,128)(2,1)S(1)} %get-tuple-element.56), channel_id=1, source_target_pairs={{128,256},{129,257},{130,258},{131,259},{132,260},{133,261},{134,2... | collective-permute-start | bytes 442376 | tf_op jit(solution)/shard_map/ppermute | solution.py:438
  37.6 25.7 %collective-permute-start.13 = (bf16[20,20,128]{2,1,0:T(8,128)(2,1)S(1)}, bf16[20,20,128]{2,1,0:T(8,128)(2,1)S(1)}, u32[]{:S(2)}, u32[]{:S(2)}) collective-permute-start(bf16[20,20,128]{2,1,0:T(8,128)(2,1)S(1)} %get-tuple-element.63), channel_id=1, source_target_pairs={{256,384},{257,385},{258,386},{259,387},{260,388},{261,389},{262,3... | collective-permute-start | bytes 307208 | tf_op jit(solution)/shard_map/ppermute | solution.py:438
  39.0 28.6 %collective-permute-start.12 = (bf16[20,20,128]{2,1,0:T(8,128)(2,1)S(1)}, bf16[20,20,128]{2,1,0:T(8,128)(2,1)S(1)}, u32[]{:S(2)}, u32[]{:S(2)}) collective-permute-start(bf16[20,20,128]{2,1,0:T(8,128)(2,1)S(1)} %get-tuple-element.62), channel_id=1, source_target_pairs={{256,384},{257,385},{258,386},{259,387},{260,388},{261,389},{262,3... | collective-permute-start | bytes 307208 | tf_op jit(solution)/shard_map/ppermute | solution.py:438
